TPU v7x, 32 devices: a whole 2x2x4 slice. The times are simulated.
32 devices in a mesh: section: 2 (over core), cin: 4 (over y, x), cout: 4 (over z).
Axes of the slice: x: 2, y: 2, z: 4, core: 2. Of those that a mesh axis runs over, the one named last changes fastest.
Arguments:
- inner_features: bfloat16 [2, 784, 2560], P('section', None, ('cin', 'cout')), may hold values from 0 to 2
- block_input: bfloat16 [2, 784, 5120], P('section', None, ('cin', 'cout')), may hold values from -6 to 6
- first_kernel: bfloat16 [9, 2560, 2560], P(None, 'cin', 'cout'), may hold values from -0.0546875 to 0.0546875
- expand_weight: bfloat16 [2560, 5120], P('cout', 'cin'), may hold values from -0.15625 to 0.15625
- reduce_weight: bfloat16 [5120, 5120], P(('cin', 'section'), 'cout'), may hold values from -0.125 to 0.125
- stride_kernel: bfloat16 [9, 5120, 5120], P(None, 'cout', ('section', 'cin')), may hold values from -0.0390625 to 0.0390625
- output_grad: bfloat16 [2, 196, 5120], P(None, None, ('section', 'cin', 'cout')), may hold values from -6 to 6
Outputs:
- inner_gradient: float32 [2, 784, 2560], P('section', None, ('cin', 'cout'))
- input_gradient: bfloat16 [2, 784, 5120], P('section', None, ('cin', 'cout'))
- first_gradient: float32 [9, 2560, 2560], P(None, 'cin', 'cout')
- expand_gradient: float32 [2560, 5120], P('cout', 'cin')
- reduce_gradient: float32 [5120, 5120], P(('cin', 'section'), 'cout')
- stride_gradient: float32 [9, 5120, 5120], P(None, 'cout', ('section', 'cin'))
All inputs are finite; a program needn't handle non-finite values.
Results may differ from a plain program's by a relative error of at most 0.013.
Values may be sent and summed in bfloat16 or wider, within the bound.
No kernel may reach another device: no remote copies, remote signals or barrier semaphores. Data moves between devices by JAX's collectives and lax.ppermute only.
A program may use at most 256 MiB of HBM per device.

v0:
```python
import jax
import jax.numpy as jnp
from jax import lax
from jax.sharding import PartitionSpec as P

SIDE = 28


def smooth_gate(values):
    return values * jax.nn.sigmoid(values)


def gate_slope(values):
    logistic = jax.nn.sigmoid(values)
    return logistic * (1.0 + values * (1.0 - logistic))


def flatten_rows(images):
    return images.reshape(images.shape[0] * images.shape[1], images.shape[2])


def project(images, matrix):
    product = jnp.dot(flatten_rows(images), matrix, preferred_element_type=jnp.float32)
    return product.reshape(images.shape[0], images.shape[1], matrix.shape[1])


def project_back(grads, matrix):
    product = lax.dot_general(
        flatten_rows(grads), matrix, (((1,), (1,)), ((), ())), preferred_element_type=jnp.float32
    )
    return product.reshape(grads.shape[0], grads.shape[1], matrix.shape[0])


def outer_rows(left, right):
    return lax.dot_general(
        flatten_rows(left),
        flatten_rows(right),
        (((0,), (0,)), ((), ())),
        preferred_element_type=jnp.float32,
    )


def padded_grid(images, side):
    grid = images.reshape(images.shape[0], side, side, images.shape[2])
    return jnp.pad(grid, ((0, 0), (1, 1), (1, 1), (0, 0)))


def conv_same(images, kernel, side):
    padded = padded_grid(images, side)
    total = jnp.zeros((images.shape[0] * side * side, kernel.shape[2]), jnp.float32)
    for row in range(3):
        for column in range(3):
            window = padded[:, row : row + side, column : column + side, :].reshape(
                -1, images.shape[2]
            )
            total = total + jnp.dot(
                window, kernel[3 * row + column], preferred_element_type=jnp.float32
            )
    return total.reshape(images.shape[0], side * side, kernel.shape[2])


def conv_same_back(grads, kernel, side):
    padded = padded_grid(grads, side)
    total = jnp.zeros((grads.shape[0] * side * side, kernel.shape[1]), jnp.float32)
    for row in range(3):
        for column in range(3):
            window = padded[:, 2 - row : 2 - row + side, 2 - column : 2 - column + side, :].reshape(
                -1, grads.shape[2]
            )
            total = total + lax.dot_general(
                window,
                kernel[3 * row + column],
                (((1,), (1,)), ((), ())),
                preferred_element_type=jnp.float32,
            )
    return total.reshape(grads.shape[0], side * side, kernel.shape[1])


def conv_same_weight(images, grads, side):
    padded = padded_grid(images, side)
    flat = flatten_rows(grads)
    terms = []
    for row in range(3):
        for column in range(3):
            window = padded[:, row : row + side, column : column + side, :].reshape(
                -1, images.shape[2]
            )
            terms.append(
                lax.dot_general(
                    window, flat, (((0,), (0,)), ((), ())), preferred_element_type=jnp.float32
                )
            )
    return jnp.stack(terms)


def conv_half_back(grads, kernel, side):
    half = side // 2
    count = grads.shape[0]
    flat = flatten_rows(grads)
    canvas = None
    for row in range(3):
        for column in range(3):
            term = lax.dot_general(
                flat,
                kernel[3 * row + column],
                (((1,), (1,)), ((), ())),
                preferred_element_type=jnp.float32,
            )
            term = term.reshape(count, half, half, kernel.shape[1])
            placed = lax.pad(
                term,
                jnp.zeros((), term.dtype),
                ((0, 0, 0), (row, 3 - row, 1), (column, 3 - column, 1), (0, 0, 0)),
            )
            canvas = placed if canvas is None else canvas + placed
    return canvas[:, 1 : side + 1, 1 : side + 1, :].reshape(count, side * side, kernel.shape[1])


def conv_half_weight(images, grads, side):
    padded = padded_grid(images, side)
    flat = flatten_rows(grads)
    terms = []
    for row in range(3):
        for column in range(3):
            window = padded[:, row : row + side : 2, column : column + side : 2, :].reshape(
                -1, images.shape[2]
            )
            terms.append(
                lax.dot_general(
                    window, flat, (((0,), (0,)), ((), ())), preferred_element_type=jnp.float32
                )
            )
    return jnp.stack(terms)


def gather_outer(shard):
    return lax.all_gather(shard, "cout", axis=2, tiled=True)


def gather_inner(shard):
    return lax.all_gather(shard, "cin", axis=2, tiled=True)


def sum_inner(partial_value):
    return lax.psum_scatter(partial_value, "cin", scatter_dimension=2, tiled=True)


def sum_outer(partial_value):
    return lax.psum_scatter(partial_value, "cout", scatter_dimension=2, tiled=True)


def shards(
    inner_features,
    block_input,
    first_kernel,
    expand_weight,
    reduce_weight,
    stride_kernel,
    output_grad,
):
    feature_block = gather_outer(inner_features)
    first_hidden = sum_inner(conv_same(feature_block, first_kernel, SIDE))
    first_act = smooth_gate(first_hidden).astype(jnp.bfloat16)
    first_block = gather_inner(first_act)
    expanded = sum_outer(project(first_block, expand_weight))
    joined_pre = block_input.astype(jnp.float32) + expanded
    joined = smooth_gate(joined_pre).astype(jnp.bfloat16)
    joined_wide = gather_outer(joined)
    joined_pair = lax.all_to_all(joined_wide, "section", split_axis=2, concat_axis=0, tiled=True)
    hidden_part = project(joined_pair, reduce_weight)
    cotangent_block = gather_outer(output_grad)
    back_part = conv_half_back(cotangent_block, stride_kernel, SIDE)
    hidden_piece = lax.psum_scatter(
        hidden_part, ("section", "cin"), scatter_dimension=2, tiled=True
    )
    act_piece = smooth_gate(hidden_piece).astype(jnp.bfloat16)
    second_act = lax.all_gather(act_piece, ("section", "cin"), axis=2, tiled=True)
    back_piece = lax.psum_scatter(back_part, ("section", "cin"), scatter_dimension=2, tiled=True)
    masked_piece = (back_piece * gate_slope(hidden_piece)).astype(jnp.bfloat16)
    masked_second = lax.all_gather(masked_piece, ("section", "cin"), axis=2, tiled=True)
    stride_gradient = conv_half_weight(second_act, cotangent_block, SIDE)
    reduce_gradient = outer_rows(joined_pair, masked_second)
    joined_back = project_back(masked_second, reduce_weight)
    joined_home = lax.all_to_all(joined_back, "section", split_axis=0, concat_axis=2, tiled=True)
    back_joined = sum_outer(joined_home)
    input_gradient = (back_joined * gate_slope(joined_pre)).astype(jnp.bfloat16)
    input_wide = gather_outer(input_gradient)
    expand_local = outer_rows(first_block, input_wide)
    back_first = sum_inner(project_back(input_wide, expand_weight))
    masked_first = (back_first * gate_slope(first_hidden)).astype(jnp.bfloat16)
    masked_block = gather_inner(masked_first)
    inner_gradient = sum_outer(conv_same_back(masked_block, first_kernel, SIDE))
    first_local = conv_same_weight(feature_block, masked_block, SIDE)
    first_gradient, expand_gradient = (
        lax.psum(first_local.astype(jnp.bfloat16), "section").astype(jnp.float32),
        lax.psum(expand_local.astype(jnp.bfloat16), "section").astype(jnp.float32),
    )
    return (
        inner_gradient,
        input_gradient,
        first_gradient,
        expand_gradient,
        reduce_gradient,
        stride_gradient,
    )


def solution(mesh):
    return jax.shard_map(
        shards,
        mesh=mesh,
        in_specs=(
            P("section", None, ("cin", "cout")),
            P("section", None, ("cin", "cout")),
            P(None, "cin", "cout"),
            P("cout", "cin"),
            P(("cin", "section"), "cout"),
            P(None, "cout", ("section", "cin")),
            P(None, None, ("section", "cin", "cout")),
        ),
        out_specs=(
            P("section", None, ("cin", "cout")),
            P("section", None, ("cin", "cout")),
            P(None, "cin", "cout"),
            P("cout", "cin"),
            P(("cin", "section"), "cout"),
            P(None, "cout", ("section", "cin")),
        ),
        check_vma=False,
    )
```

profile of v0, /device:TPU:0, one launch (start us, length us, event | category | flops | bytes accessed | tf_op | source)
XLA Modules:
  0.0 1204.7 jit_solution(9107462076712635394)
XLA Ops:
  8.1 25.6 %all_gather.25 = bf16[1,784,640]{1,2,0:T(8,128)(2,1)S(1)} all-gather(bf16[1,784,160]{1,2,0:T(8,128)(2,1)} %param.7), channel_id=1, replica_groups=mesh['section'=2,'cin'=4,'cout'=4] {'cout'}, dimensions={2}, use_global_device_ids=true | all-gather | bytes 1254400 | tf_op jit(solution)/shard_map/all_gather | solution.py:137
  37.5 8.9 pad_slice_fusion.8
  48.5 4.0 fusion.84
  64.2 3.9 fusion.113
  70.2 3.9 fusion.117
  93.2 8.7 add_bitcast_fusion.1
  101.9 5.5 copy.150
  109.3 17.2 %all_gather.24 = bf16[2,196,640]{1,2,0:T(8,128)(2,1)S(1)} all-gather(bf16[2,196,160]{1,2,0:T(8,128)(2,1)S(1)} %copy-done.38), channel_id=1, replica_groups=mesh['section'=2,'cin'=4,'cout'=4] {'cout'}, dimensions={2}, use_global_device_ids=true | all-gather | bytes 627200 | tf_op jit(solution)/shard_map/all_gather | solution.py:137
  127.5 3.9 fusion.35
  131.4 19.5 %pad.39 = f32[2,30,30,1280]{3,2,1,0:T(8,128)} pad(f32[2,14,14,1280]{3,2,1,0:T(8,128)} %fusion.35, f32[]{:T(128)} %constant.3.clone.1), padding=0_0_0x0_3_1x0_3_1x0_0_0 | pad | bytes 11223044 | tf_op jit(solution)/shard_map/pad | solution.py:110
  150.9 4.0 fusion.33
  155.0 19.7 %pad.40 = f32[2,30,30,1280]{3,2,1,0:T(8,128)} pad(f32[2,14,14,1280]{3,2,1,0:T(8,128)} %fusion.33, f32[]{:T(128)} %constant.3.clone.1), padding=0_0_0x0_3_1x1_2_1x0_0_0 | pad | bytes 11223044 | tf_op jit(solution)/shard_map/pad | solution.py:110
  174.7 3.9 fusion.31
  178.6 19.5 %pad.41 = f32[2,30,30,1280]{3,2,1,0:T(8,128)} pad(f32[2,14,14,1280]{3,2,1,0:T(8,128)} %fusion.31, f32[]{:T(128)} %constant.3.clone.1), padding=0_0_0x0_3_1x2_1_1x0_0_0 | pad | bytes 11223044 | tf_op jit(solution)/shard_map/pad | solution.py:110
  200.5 14.1 %all_gather.26 = bf16[1,784,640]{1,2,0:T(8,128)(2,1)S(1)} all-gather(bf16[1,784,160]{1,2,0:T(8,128)(2,1)S(1)} %multiply_convert_fusion.3), channel_id=1, replica_groups=mesh['section'=2,'cin'=4,'cout'=4] {'cin'}, dimensions={2}, use_global_device_ids=true | all-gather | bytes 1254400 | tf_op jit(solution)/shard_map/all_gather | solution.py:141
  219.4 10.1 copy.153
  229.6 3.9 fusion.27
  233.6 19.5 %pad.52 = f32[2,28,28,1280]{3,2,1,0:T(8,128)} pad(f32[2,14,14,1280]{3,2,1,0:T(8,128)} %fusion.27, f32[]{:T(128)} %constant.3.clone.1), padding=0_0_0x0_1_1x0_1_1x0_0_0 | pad | bytes 10035204 | tf_op jit(solution)/shard_map/slice | solution.py:116
  253.1 3.9 fusion.25
  257.0 19.4 %pad.53 = f32[2,28,28,1280]{3,2,1,0:T(8,128)} pad(f32[2,14,14,1280]{3,2,1,0:T(8,128)} %fusion.25, f32[]{:T(128)} %constant.3.clone.1), padding=0_0_0x0_1_1x1_0_1x0_0_0 | pad | bytes 10035204 | tf_op jit(solution)/shard_map/slice | solution.py:116
  276.4 3.9 fusion.21
  280.3 19.4 %pad.55 = f32[2,28,28,1280]{3,2,1,0:T(8,128)} pad(f32[2,14,14,1280]{3,2,1,0:T(8,128)} %fusion.21, f32[]{:T(128)} %constant.3.clone.1), padding=0_0_0x1_0_1x0_1_1x0_0_0 | pad | bytes 10035204 | tf_op jit(solution)/shard_map/slice | solution.py:116
  299.7 3.9 fusion.19
  303.6 19.4 %pad.56 = f32[2,28,28,1280]{3,2,1,0:T(8,128)} pad(f32[2,14,14,1280]{3,2,1,0:T(8,128)} %fusion.19, f32[]{:T(128)} %constant.3.clone.1), padding=0_0_0x1_0_1x1_0_1x0_0_0 | pad | bytes 10035204 | tf_op jit(solution)/shard_map/slice | solution.py:116
  323.0 3.9 fusion.23
  326.9 19.4 %pad.73 = f32[2,28,29,1280]{3,2,1,0:T(8,128)} pad(f32[2,14,14,1280]{3,2,1,0:T(8,128)} %fusion.23, f32[]{:T(128)} %constant.3.clone.1), padding=0_0_0x1_0_1x0_2_1x0_0_0 | pad | bytes 10321924
  350.2 19.3 %pad.74 = f32[2,28,29,1280]{3,2,1,0:T(8,128)} pad(f32[2,14,14,1280]{3,2,1,0:T(8,128)} %fusion.29, f32[]{:T(128)} %constant.3.clone.1), padding=0_0_0x0_1_1x0_2_1x0_0_0 | pad | bytes 10321924
  370.2 14.4 %add_add_fusion = f32[2,30,30,1280]{3,2,1,0:T(8,128)} fusion(f32[2,30,30,1280]{3,2,1,0:T(8,128)} %pad.41, f32[2,30,30,1280]{3,2,1,0:T(8,128)} %pad.39, f32[2,30,30,1280]{3,2,1,0:T(8,128)} %pad.40), kind=kLoop, calls=%fused_computation | loop fusion | flops 4608000 | bytes 36864000 | tf_op jit(solution)/shard_map/add | solution.py:115
  384.6 12.4 %all-reduce.27.cloned.1.call-done = f32[1,784,1280]{1,0,2:T(1,128)} async-done(((f32[1,784,1280]{1,0,2:T(1,128)}), f32[1,784,1280]{1,0,2:T(1,128)}) %all-reduce.27.cloned.1.call-update) | async-done | bytes 4014096
  400.3 21.6 %fusion.4 = f32[2,28,28,1280]{3,2,1,0:T(8,128)S(1)} fusion(f32[2,28,28,1280]{3,2,1,0:T(8,128)} %pad.56, f32[2,28,28,1280]{3,2,1,0:T(8,128)} %pad.55, f32[2,28,28,1280]{3,2,1,0:T(8,128)} %pad.53, f32[2,28,28,1280]{3,2,1,0:T(8,128)} %pad.52, f32[2,30,30,1280]{3,2,1,0:T(8,128)} %add_add_fusion, f32[2,28,29,1280]{3,2,1,0:T(8,128)} %pad.74, ...), kind=kLoop, calls=%fused_computation.6 | loop fusion | flops 12042240 | bytes 64225280 | tf_op jit(solution)/shard_map/add | solution.py:115
  421.9 10.0 copy.147
  431.9 15.8 %copy.148 = f32[2,784,1280]{1,2,0:T(8,128)} copy(f32[2,784,1280]{2,0,1:T(2,128)} %bitcast.315) | data formatting | bytes 16056320 | tf_op jit(solution)/shard_map/reshape | solution.py:116
  448.3 11.0 copy.230
  459.8 16.2 %reduce = bf16[1280,784]{1,0:T(8,128)(2,1)} reduce(bf16[1280,1,784]{2,1,0:T(2,128)(2,1)} %bitcast.316, bf16[]{:T(256)} %broadcast.42), dimensions={1}, to_apply=%bitcast.305.reduce_sub_computation | reduce | bytes 4014082
  475.9 6.4 reshape.242
  482.4 8.5 all_to_all.33
  490.8 5.8 reshape.243
  496.7 4.1 copy.197
  500.8 4.2 copy.157
  505.0 8.2 fusion.17
  513.3 8.5 reduce-scatter.3.cloned.1.call-done
  521.9 79.2 %reduce-scatter.5.cloned.1.call-done = f32[2,784,160]{1,2,0:T(8,128)} async-done(((f32[2,784,1280]{1,2,0:T(8,128)}), f32[2,784,160]{1,2,0:T(8,128)}) %reduce-scatter.5.cloned.1.call-update) | async-done | bytes 1003536 | tf_op jit(solution)/shard_map/reduce_scatter | solution.py:173
  604.4 38.0 %all-gather.7.cloned.1.call-done = bf16[2,784,1280]{1,2,0:T(8,128)(2,1)} async-done(((bf16[2,784,160]{1,2,0:T(8,128)(2,1)}), bf16[2,784,1280]{1,2,0:T(8,128)(2,1)}) %all-gather.7.cloned.1.call-update) | async-done | bytes 4014096 | tf_op jit(solution)/shard_map/all_gather | solution.py:180
  642.4 5.6 fusion.37
  648.0 8.0 all_to_all.34
  656.0 5.6 copy.195
  661.7 7.3 reshape.236
  669.1 167.8 %all-reduce.29.cloned.1.call-done = f32[1,784,1280]{1,0,2:T(1,128)} async-done(((f32[1,784,1280]{1,0,2:T(1,128)}), f32[1,784,1280]{1,0,2:T(1,128)}) %all-reduce.29.cloned.1.call-update) | async-done | bytes 4014096
  841.3 48.0 %all-gather.9.cloned.1.call-done = bf16[1,784,1280]{1,2,0:T(8,128)(2,1)} async-done(((bf16[1,784,320]{1,2,0:T(8,128)(2,1)}), bf16[1,784,1280]{1,2,0:T(8,128)(2,1)}) %all-gather.9.cloned.1.call-update) | async-done | bytes 2007056 | tf_op jit(solution)/shard_map/all_gather | solution.py:137
  889.3 5.4 fusion.49
  894.7 5.5 copy.162
  901.4 4.7 convolution_convert_fusion
  906.1 68.2 %all-reduce.31.cloned.1.call-done = f32[1,784,640]{1,0,2:T(1,128)} async-done(((f32[1,784,640]{1,0,2:T(1,128)}), f32[1,784,640]{1,0,2:T(1,128)}) %all-reduce.31.cloned.1.call-update) | async-done | bytes 2007056
  976.1 14.4 %all_gather.30 = bf16[1,784,640]{1,2,0:T(8,128)(2,1)S(1)} all-gather(bf16[1,784,160]{1,2,0:T(8,128)(2,1)S(1)} %fusion.137), channel_id=1, replica_groups=mesh['section'=2,'cin'=4,'cout'=4] {'cin'}, dimensions={2}, use_global_device_ids=true | all-gather | bytes 1254400 | tf_op jit(solution)/shard_map/all_gather | solution.py:141
  992.6 8.8 pad_slice_fusion
  1035.9 4.2 add_bitcast_fusion
  1040.2 5.6 copy.166
  1069.5 13.4 %copy.169 = bf16[2,784,1280]{2,0,1:T(2,128)(2,1)} copy(bf16[2,784,1280]{1,2,0:T(8,128)(2,1)} %all-gather.11.cloned.1.call-done) | data formatting | bytes 8028160 | tf_op jit(solution)/shard_map/all_gather | solution.py:177
  1082.9 11.4 fusion.147
  1114.3 7.3 copy.168
  1133.0 10.4 copy-done.40
  1143.4 5.3 fusion.148
  1151.0 33.9 %all-reduce.35.cloned.1.call-done = (bf16[9,640,640]{2,1,0:T(8,128)(2,1)}, bf16[640,1280]{1,0:T(8,128)(2,1)}) async-done(((bf16[9,640,640]{2,1,0:T(8,128)(2,1)}, bf16[640,1280]{1,0:T(8,128)(2,1)}), (bf16[9,640,640]{2,1,0:T(8,128)(2,1)}, bf16[640,1280]{1,0:T(8,128)(2,1)})) %all-reduce.35.cloned.1.call-update) | async-done | bytes 9011216 | tf_op jit(solution)/shard_map/psum | solution.py:195
  1184.8 9.9 convert_element_type.43
  (202 shorter events, 162.2 us)
Async XLA Ops:
  8.0 497.0 %copy-start = (bf16[640,1280]{1,0:T(8,128)(2,1)S(1)}, bf16[640,1280]{1,0:T(8,128)(2,1)}, u32[]{:S(2)}) copy-start(bf16[640,1280]{1,0:T(8,128)(2,1)} %param.11) | copy-start | bytes 4915204
  8.0 190.7 %all-reduce.25.cloned.1.call-start = ((), (), s32[]{:S(2)}) async-start(), calls=%async_computation.10 | async-start | bytes 4587520
  33.7 1.6 copy-start.4
  48.5 4.0 copy-start.8
  107.4 0.7 copy-start.42
  107.4 1.2 copy-start.41
  107.4 1.9 copy-start.38
  107.4 289.6 %all-reduce.27.cloned.1.call-start = ((), (), s32[]{:S(2)}) async-start(), calls=%async_computation.11 | async-start | bytes 9175040
  126.5 4.9 copy-start.2
  198.8 16.9 %copy-start.39 = (bf16[640,1280]{1,0:T(8,128)(2,1)S(1)}, bf16[640,1280]{1,0:T(8,128)(2,1)}, u32[]{:S(2)}) copy-start(bf16[640,1280]{1,0:T(8,128)(2,1)} %param.10) | copy-start | bytes 4915204
  214.6 1.0 copy-start.28
  229.6 218.7 %all-gather.5.cloned.1.call-start = ((), (), s32[]{:S(2)}) async-start(), calls=%async_computation.5 | async-start | bytes 2867200 | tf_op jit(solution)/shard_map/all_gather | solution.py:137
  397.0 2.1 copy-start.25
  400.3 121.6 %reduce-scatter.3.cloned.1.call-start = ((), (), s32[]{:S(2)}) async-start(), calls=%async_computation.4 | async-start | bytes 10321920 | tf_op jit(solution)/shard_map/reduce_scatter | solution.py:178
  447.7 153.3 %reduce-scatter.5.cloned.1.call-start = ((), (), s32[]{:S(2)}) async-start(), calls=%async_computation.6 | async-start | bytes 10321920 | tf_op jit(solution)/shard_map/reduce_scatter | solution.py:173
  513.3 129.1 %all-gather.7.cloned.1.call-start = ((), (), s32[]{:S(2)}) async-start(), calls=%async_computation.7 | async-start | bytes 5160960 | tf_op jit(solution)/shard_map/all_gather | solution.py:180
  604.2 232.7 %all-reduce.29.cloned.1.call-start = ((), (), s32[]{:S(2)}) async-start(), calls=%async_computation.12 | async-start | bytes 9175040
  669.0 220.2 %all-gather.9.cloned.1.call-start = ((), (), s32[]{:S(2)}) async-start(), calls=%async_computation.8 | async-start | bytes 2867200 | tf_op jit(solution)/shard_map/all_gather | solution.py:137
  841.2 133.1 %all-reduce.31.cloned.1.call-start = ((), (), s32[]{:S(2)}) async-start(), calls=%async_computation.13 | async-start | bytes 4587520
  900.1 1.3 copy-start.29
  900.2 169.3 %all-gather.11.cloned.1.call-start = ((), (), s32[]{:S(2)}) async-start(), calls=%async_computation.9 | async-start | bytes 5160960 | tf_op jit(solution)/shard_map/all_gather | solution.py:177
  900.9 247.8 %all-reduce.33.cloned.1.call-start = ((), (), s32[]{:S(2)}) async-start(), calls=%async_computation.14 | async-start | bytes 4587520
  990.4 1.1 copy-start.6
  1015.2 1.6 copy-start.16
  1016.8 2.4 copy-start.17
  1019.2 2.4 copy-start.18
  1021.6 2.4 copy-start.19
  1024.0 2.4 copy-start.20
  1026.3 2.4 copy-start.21
  1028.7 2.4 copy-start.22
  1031.1 2.4 copy-start.7
  1033.5 2.4 copy-start.23
  1045.8 3.4 copy-start.15
  1051.3 1.2 copy-start.11
  1051.3 133.5 %all-reduce.35.cloned.1.call-start = ((), (), s32[]{:S(2)}) async-start(), calls=%async_computation.15 | async-start | bytes 18022400 | tf_op jit(solution)/shard_map/psum | solution.py:195
  1052.5 2.1 copy-start.9
  1054.6 2.1 copy-start.5
  1056.8 2.1 copy-start.14
  1058.8 2.1 copy-start.12
  1060.9 2.1 copy-start.10
  1063.0 2.1 copy-start.13
  1067.3 1.1 copy-start.3
  1114.2 7.4 copy-start.30
  1121.6 1.3 copy-start.31
  1122.9 1.3 copy-start.32
  1124.1 1.3 copy-start.33
  1125.4 1.3 copy-start.34
  1126.7 1.3 copy-start.35
  1127.9 1.3 copy-start.36
  1129.2 1.3 copy-start.37
  1131.7 11.6 copy-start.24
  1131.7 11.6 copy-start.26
  1133.0 10.4 copy-start.40
  1184.8 9.9 copy-start.27
  1194.7 2.0 copy-start.1
Sparse Core Ops, SparseCore 0:
  107.6 73.4 all-reduce.24
  229.7 167.2 all-reduce.26
  400.4 47.8 all-gather.4
  669.1 167.6 all-reduce.28
  841.4 47.8 all-gather.8
  900.3 74.0 all-reduce.30
  1051.5 92.4 all-reduce.32
  1147.1 37.7 all-reduce.34
Sparse Core Ops, SparseCore 1:
  447.8 74.0 reduce-scatter.2
  525.9 75.1 reduce-scatter.4
  604.3 38.1 all-gather.6
  903.4 44.9 all-gather.10
where the time goes:
time: 1220 us; the launch traced here: 1200 us
  waiting for transfers between devices  457 us (37%)
  local copies, waits for them, and re-layouts  407 us (33%)
  matrix products  162 us (13%)
  blocking collectives  87.8 us (7%)
  other arithmetic  70.9 us (6%)
  between operations  18.9 us (2%)
    unnamed x17, waiting for transfers between devices  249 us
    slice x5, local copies, waits for them, and re-layouts, conv_half_back(): canvas[:, 1:side + 1, 1:side + 1, :]  87.6 us
    unnamed x100, local copies, waits for them, and re-layouts  81.6 us
    reduce_scatter x1, waiting for transfers between devices, shards(): lax.psum_scatter(hidden_part, ('section', 'cin'), scatter_dimension=2, ti...  79.2 us
    pad x3, local copies, waits for them, and re-layouts, conv_half_back(): lax.pad(term, jnp.zeros((), term.dtype), ((0, 0, 0), (row, 3 - row, 1), (...  58.7 us
    all_gather x2, waiting for transfers between devices, gather_outer(): return lax.all_gather(shard, 'cout', axis=2, tiled=True)  48.3 us
    all_gather x2, blocking collectives, gather_outer(): return lax.all_gather(shard, 'cout', axis=2, tiled=True)  42.8 us
    dot_general x9, matrix products, conv_same(): jnp.dot(window, kernel[3 * row + column], preferred_element_type=jnp.floa...  39.5 us
  transfers between devices with their start and end apart: 12, of which 9 were waited for; matrix products, arithmetic and copies ran while one was open for 40% of the time, Pallas kernels for 0%

commit v1 on v0

v1 whole, which is shorter than its diff:
```python
import functools

import jax
import jax.numpy as jnp
from jax import lax
from jax.experimental import pallas as pl
from jax.experimental.pallas import tpu as pltpu
from jax.sharding import PartitionSpec as P

SIDE = 28
TAPS = 9
F32 = jnp.float32
BF16 = jnp.bfloat16
NN = (((1,), (0,)), ((), ()))
TN = (((0,), (0,)), ((), ()))
NT = (((1,), (1,)), ((), ()))


def smooth_gate(values):
    return values * jax.nn.sigmoid(values)


def gate_slope(values):
    logistic = jax.nn.sigmoid(values)
    return logistic * (1.0 + values * (1.0 - logistic))


def dot(left, right, dims):
    return lax.dot_general(left, right, dims, preferred_element_type=F32)


def lanes_of(count):
    return -(-count // 128) * 128


def params():
    return pltpu.CompilerParams(
        dimension_semantics=("arbitrary",), vmem_limit_bytes=56 * 1024 * 1024
    )


def cost(flops, moved):
    return pl.CostEstimate(flops=flops, bytes_accessed=moved, transcendentals=0)


def fill_columns(planes, image, side):
    rows, pixels = image.shape
    wide = planes.shape[2]
    column = lax.broadcasted_iota(jnp.int32, (rows, pixels), 1) % side
    zero = jnp.zeros_like(image)
    planes[0, :, :pixels] = jnp.where(column == side - 1, zero, image)
    planes[1, :, :pixels] = image
    planes[2, :, :pixels] = jnp.where(column == 0, zero, image)
    if wide > pixels:
        for k in range(3):
            planes[k, :, pixels:] = jnp.zeros((rows, wide - pixels), image.dtype)


def read_shifted(planes, dy, dx, side):
    wide = planes.shape[2]
    amount = (2 * wide - (side * dy + dx)) % wide
    return pltpu.roll(planes[dx + 1], amount, 1)


def partner(index, k, n):
    return index ^ k if n & (n - 1) == 0 else (index + k) % n


def source(index, k, n):
    return index ^ k if n & (n - 1) == 0 else (index + n - k) % n


def whole(shape):
    return pl.BlockSpec(shape, lambda *_: (0,) * len(shape))


def one_step(body, ins, outs, scratch, flops):
    moved = sum(v.size * v.dtype.itemsize for v in ins)
    moved += sum(v.size * v.dtype.itemsize for v in outs)
    return pl.pallas_call(
        body,
        out_shape=outs,
        in_specs=[pl.BlockSpec(memory_space=pltpu.VMEM)] * len(ins),
        out_specs=[pl.BlockSpec(memory_space=pltpu.VMEM)] * len(outs),
        scratch_shapes=scratch,
        compiler_params=pltpu.CompilerParams(vmem_limit_bytes=56 * 1024 * 1024),
        cost_estimate=cost(flops, moved),
    )(*ins)


def like(shape, dtype=BF16):
    return jax.ShapeDtypeStruct(shape, dtype)


def held_type(size):
    return BF16 if size % 16 == 0 else F32


def rows_at(index, size):
    return pl.ds(pl.multiple_of(index * size, 8), size)


def write_chunks(outs, total, me, n):
    size = outs[0].shape[0]
    for k in range(n):
        rows = rows_at(partner(me, k, n), size)
        outs[k][...] = total[rows, : outs[k].shape[1]].astype(BF16)


def conv_forward_body(x_ref, w_ref, *rest, side, n):
    outs, (planes, total) = rest[:n], rest[n:]
    t = pl.program_id(0)
    me = lax.axis_index("cin")

    @pl.when(t == 0)
    def _():
        fill_columns(planes, x_ref[...], side)
        total[...] = jnp.zeros_like(total)

    window = read_shifted(planes, t // 3 - 1, t % 3 - 1, side)
    total[...] += dot(w_ref[0], window, TN)

    @pl.when(t == TAPS - 1)
    def _():
        write_chunks(outs, total, me, n)


def conv_forward(x, kernel, side, n):
    depth, pixels = x.shape
    width = kernel.shape[2]
    wide = lanes_of(pixels + side + 1)
    return pl.pallas_call(
        functools.partial(conv_forward_body, side=side, n=n),
        out_shape=[like((width // n, pixels))] * n,
        grid=(TAPS,),
        in_specs=[
            whole((depth, pixels)),
            pl.BlockSpec((1, depth, width), lambda t: (t, 0, 0)),
        ],
        out_specs=[whole((width // n, pixels))] * n,
        scratch_shapes=[
            pltpu.VMEM((3, depth, wide), BF16),
            pltpu.VMEM((width, wide), F32),
        ],
        compiler_params=params(),
        cost_estimate=cost(2 * TAPS * depth * width * pixels, 2 * kernel.size + 4 * x.size),
    )(x, kernel)


def conv_back_body(m_ref, w_ref, *rest, side, n):
    outs, (planes, total) = rest[:n], rest[n:]
    t = pl.program_id(0)
    me = lax.axis_index("cout")

    @pl.when(t == 0)
    def _():
        fill_columns(planes, m_ref[...], side)
        total[...] = jnp.zeros_like(total)

    window = read_shifted(planes, 1 - t // 3, 1 - t % 3, side)
    total[...] += dot(w_ref[0], window, NN)

    @pl.when(t == TAPS - 1)
    def _():
        write_chunks(outs, total, me, n)


def conv_back(m, kernel, side, n):
    width, pixels = m.shape
    depth = kernel.shape[1]
    wide = lanes_of(pixels + side + 1)
    return pl.pallas_call(
        functools.partial(conv_back_body, side=side, n=n),
        out_shape=[like((depth // n, pixels))] * n,
        grid=(TAPS,),
        in_specs=[
            whole((width, pixels)),
            pl.BlockSpec((1, depth, width), lambda t: (t, 0, 0)),
        ],
        out_specs=[whole((depth // n, pixels))] * n,
        scratch_shapes=[
            pltpu.VMEM((3, width, wide), BF16),
            pltpu.VMEM((depth, wide), F32),
        ],
        compiler_params=params(),
        cost_estimate=cost(2 * TAPS * depth * width * pixels, 2 * kernel.size + 4 * m.size),
    )(m, kernel)


def conv_weight_body(xa_ref, xb_ref, ma_ref, mb_ref, o_ref, pa, pb, ga, gb, *, side):
    t = pl.program_id(0)
    pixels = ma_ref.shape[1]

    @pl.when(t == 0)
    def _():
        fill_columns(pa, xa_ref[...], side)
        fill_columns(pb, xb_ref[...], side)
        ga[...] = jnp.zeros_like(ga)
        gb[...] = jnp.zeros_like(gb)
        ga[:, :pixels] = ma_ref[...]
        gb[:, :pixels] = mb_ref[...]

    dy, dx = t // 3 - 1, t % 3 - 1
    o_ref[0] = dot(read_shifted(pa, dy, dx, side), ga[...], NT) + dot(
        read_shifted(pb, dy, dx, side), gb[...], NT
    )


def conv_weight(xa, xb, ma, mb, side):
    depth, pixels = xa.shape
    width = ma.shape[0]
    wide = lanes_of(pixels + side + 1)
    return pl.pallas_call(
        functools.partial(conv_weight_body, side=side),
        out_shape=jax.ShapeDtypeStruct((TAPS, depth, width), F32),
        grid=(TAPS,),
        in_specs=[pl.BlockSpec((depth, pixels), lambda t: (0, 0))] * 2
        + [pl.BlockSpec((width, pixels), lambda t: (0, 0))] * 2,
        out_specs=pl.BlockSpec((1, depth, width), lambda t: (t, 0, 0)),
        scratch_shapes=[pltpu.VMEM((3, depth, wide), BF16)] * 2
        + [pltpu.VMEM((width, wide), BF16)] * 2,
        compiler_params=params(),
        cost_estimate=cost(4 * TAPS * depth * width * pixels, 4 * TAPS * depth * width),
    )(xa, xb, ma, mb)


def fill_moved(moved, cots, half):
    count, rows, pixels = cots.shape
    wide = moved.shape[2] // count
    column = lax.broadcasted_iota(jnp.int32, (rows, wide), 1) % half
    for b in range(count):
        moved[0, :, b * wide : (b + 1) * wide] = jnp.zeros((rows, wide), moved.dtype)
        moved[0, :, b * wide : b * wide + pixels] = cots[b]
        image = moved[0, :, b * wide : (b + 1) * wide]
        inner = jnp.where(column == 0, jnp.zeros_like(image), image)
        moved[1, :, b * wide : (b + 1) * wide] = pltpu.roll(inner, wide - 1, 1)
        moved[2, :, b * wide : (b + 1) * wide] = pltpu.roll(image, wide - half, 1)
        moved[3, :, b * wide : (b + 1) * wide] = pltpu.roll(inner, wide - half - 1, 1)


def chosen(plane, small, large, side):
    half = side // 2
    i = lax.broadcasted_iota(jnp.int32, (small, large), 0)
    q = lax.broadcasted_iota(jnp.int32, (small, large), 1)
    row, column = i // half, i % half
    pixel = (2 * row + plane // 2) * side + 2 * column + plane % 2
    hit = (q == pixel) & (i < half * half)
    return jnp.where(hit, 1.0, 0.0).astype(BF16)


def half_back_body(g_ref, w_ref, kept, sent, moved, total, placed, *, side):
    t = pl.program_id(0)
    count = g_ref.shape[0]
    rows, pixels = placed.shape
    half = rows // 2
    wide = moved.shape[2] // count
    core = lax.axis_index("section")

    @pl.when(t == 0)
    def _():
        fill_moved(moved, g_ref[...], side // 2)
        total[...] = jnp.zeros_like(total)

    ty, tx = t // 3, t % 3
    plane = jnp.where(ty == 1, 0, 2) + jnp.where(tx == 1, 0, 1)
    move = jnp.where(ty == 0, 2, 0) + jnp.where(tx == 0, 1, 0)
    total[plane] += dot(w_ref[0], moved[move], NN)

    @pl.when(t == TAPS - 1)
    def _():
        for b in range(count):
            for k in range(4):
                term = dot(
                    total[k, :, b * wide : (b + 1) * wide].astype(BF16),
                    chosen(k, wide, pixels, side),
                    NN,
                )
                placed[...] = term if k == 0 else placed[...] + term
            kept[b * half : (b + 1) * half, :] = placed[rows_at(core, half), :].astype(BF16)
            sent[b * half : (b + 1) * half, :] = placed[rows_at(1 - core, half), :].astype(BF16)


def half_back(cots, kernel, side):
    count, width, small = cots.shape
    depth = kernel.shape[1]
    wide = lanes_of(small + side // 2 + 1)
    pixels = side * side
    out = (count * depth // 2, pixels)
    return pl.pallas_call(
        functools.partial(half_back_body, side=side),
        out_shape=[like(out)] * 2,
        grid=(TAPS,),
        in_specs=[
            whole((count, width, small)),
            pl.BlockSpec((1, depth, width), lambda t: (t, 0, 0)),
        ],
        out_specs=[whole(out)] * 2,
        scratch_shapes=[
            pltpu.VMEM((4, width, count * wide), BF16),
            pltpu.VMEM((4, depth, count * wide), F32),
            pltpu.VMEM((depth, pixels), F32),
        ],
        compiler_params=params(),
        cost_estimate=cost(2 * TAPS * depth * width * count * small * 2, 2 * kernel.size),
    )(cots, kernel)


def half_weight_body(a_ref, b_ref, g_ref, o_ref, moved, planes, *, side):
    t = pl.program_id(0)
    count = g_ref.shape[0]
    half = a_ref.shape[0] // count
    pixels = a_ref.shape[1]
    wide = moved.shape[2] // count
    core = lax.axis_index("section")

    @pl.when(t == 0)
    def _():
        fill_moved(moved, g_ref[...], side // 2)
        for k in range(4):
            pick = chosen(k, wide, pixels, side)
            for ref, place in ((a_ref, core), (b_ref, 1 - core)):
                for b in range(count):
                    planes[k, rows_at(place, half), b * wide : (b + 1) * wide] = dot(
                        ref[b * half : (b + 1) * half, :], pick, NT
                    ).astype(BF16)

    ty, tx = t // 3, t % 3
    plane = jnp.where(ty == 1, 0, 2) + jnp.where(tx == 1, 0, 1)
    move = jnp.where(ty == 0, 2, 0) + jnp.where(tx == 0, 1, 0)
    o_ref[0] = dot(planes[plane], moved[move], NT)


def half_weight(mine, other, cots, side):
    count, width, small = cots.shape
    rows, pixels = mine.shape
    depth = 2 * rows // count
    wide = lanes_of(small + side // 2 + 1)
    return pl.pallas_call(
        functools.partial(half_weight_body, side=side),
        out_shape=like((TAPS, depth, width), F32),
        grid=(TAPS,),
        in_specs=[
            whole((rows, pixels)),
            whole((rows, pixels)),
            whole((count, width, small)),
        ],
        out_specs=pl.BlockSpec((1, depth, width), lambda t: (t, 0, 0)),
        scratch_shapes=[
            pltpu.VMEM((4, width, count * wide), BF16),
            pltpu.VMEM((4, depth, count * wide), BF16),
        ],
        compiler_params=params(),
        cost_estimate=cost(
            2 * TAPS * depth * width * count * small * 2, 4 * TAPS * depth * width
        ),
    )(mine, other, cots)


def expand(first_block, weight, n):
    depth, width = weight.shape
    pixels = first_block.shape[1]

    def body(x_ref, w_ref, *rest):
        outs, total = rest[:n], rest[n]
        total[...] = dot(w_ref[...], x_ref[...], TN)
        write_chunks(outs, total, lax.axis_index("cout"), n)

    return one_step(
        body,
        [first_block, weight],
        [like((width // n, pixels))] * n,
        [pltpu.VMEM((width, pixels), F32)],
        2 * depth * width * pixels,
    )


def round_target(r, core, z, n):
    return z // (n // 2), z ^ r ^ (core * (n // 2))


def round_block(r, core, z, n):
    place = z ^ r
    return lax.rem(place, n // 2), core ^ (place // (n // 2))


def round_pairs(r, n, back):
    pairs = []
    for core in range(2):
        for z in range(n):
            to_core, to_z = round_target(r, core, z, n)
            pair = (core * n + z, to_core * n + to_z)
            pairs.append(pair[::-1] if back else pair)
    return pairs


def round_send(value, r, n, back=False):
    return lax.ppermute(value, ("section", "cout"), round_pairs(r, n, back))


def reduce_forward(parts, weight, n):
    size, pixels = parts[0].shape
    depth, width = weight.shape
    half = width // 2

    def body(*refs):
        ins, w_ref = refs[:n], refs[n]
        joined, kept, sent, total = refs[n + 1 :]
        core, z = lax.axis_index("section"), lax.axis_index("cout")
        for r in range(n):
            block, image = round_block(r, core, z, n)
            joined[image, rows_at(block, size), :] = ins[r][...]
        for image in range(2):
            total[...] = dot(w_ref[...], joined[image], TN)
            span = slice(image * half, (image + 1) * half)
            kept[span, :] = total[rows_at(core, half), :].astype(BF16)
            sent[span, :] = total[rows_at(1 - core, half), :].astype(BF16)

    return one_step(
        body,
        [*parts, weight],
        [like((2, depth, pixels)), like((2 * half, pixels)), like((2 * half, pixels))],
        [pltpu.VMEM((width, pixels), F32)],
        4 * depth * width * pixels,
    )


def add_halves(kept, got, n):
    rows, pixels = kept.shape
    size = rows // 2 // n

    def body(a_ref, b_ref, *rest):
        outs, total = rest[:n], rest[n]
        me = lax.axis_index("cin")
        total[...] = a_ref[...].astype(F32) + b_ref[...].astype(F32)
        for k in range(n):
            for image in range(2):
                start = image * (rows // 2) + partner(me, k, n) * size
                value = total[pl.ds(pl.multiple_of(start, 8), size), :]
                outs[k][image * size : (image + 1) * size, :] = value.astype(BF16)

    return one_step(
        body,
        [kept, got],
        [like((2 * size, pixels))] * n,
        [pltpu.VMEM((rows, pixels), F32)],
        rows * pixels,
    )


def join_pieces(parts, n):
    double, pixels = parts[0].shape
    size = double // 2

    def body(*refs):
        ins, out, held = refs[:n], refs[n], refs[n + 1]
        me = lax.axis_index("cin")
        for k in range(n):
            for image in range(2):
                start = image * n * size + source(me, k, n) * size
                value = ins[k][image * size : (image + 1) * size, :]
                held[pl.ds(pl.multiple_of(start, 8), size), :] = value.astype(held.dtype)
        out[...] = held[...].astype(BF16)

    return one_step(
        body,
        parts,
        [like((n * double, pixels))],
        [pltpu.VMEM((n * double, pixels), held_type(size))],
        double * pixels,
    )[0]


def place_halves(masked, mine, other, core):
    half = mine[0].shape[0]
    for image in range(2):
        masked[image, rows_at(core, half), :] = mine[image][...]
        masked[image, rows_at(1 - core, half), :] = other[image][...]


def reduce_back(mine, other, weight, n):
    depth, width = weight.shape
    pixels = mine[0].shape[1]
    size = depth // (n // 2)

    def body(*refs):
        a, b, w_ref = refs[0:2], refs[2:4], refs[4]
        outs, masked = refs[5 : 5 + n], refs[5 + n]
        core, z = lax.axis_index("section"), lax.axis_index("cout")
        place_halves(masked, a, b, core)
        for r in range(n):
            block, image = round_block(r, core, z, n)
            outs[r][...] = dot(w_ref[rows_at(block, size), :], masked[image], NN).astype(BF16)

    return one_step(
        body,
        [*mine, *other, weight],
        [like((size, pixels))] * n,
        [pltpu.VMEM((2, width, pixels), BF16)],
        4 * depth * width * pixels,
    )


def reduce_weight_gradient(joined, mine, other):
    _, depth, pixels = joined.shape
    width = 2 * mine[0].shape[0]

    def body(j_ref, *refs):
        a, b, out, masked = refs[0:2], refs[2:4], refs[4], refs[5]
        place_halves(masked, a, b, lax.axis_index("section"))
        out[...] = dot(j_ref[0], masked[0], NT) + dot(j_ref[1], masked[1], NT)

    return one_step(
        body,
        [joined, *mine, *other],
        [like((depth, width), F32)],
        [pltpu.VMEM((2, width, pixels), BF16)],
        4 * depth * width * pixels,
    )[0]


def expand_back(parts, weight, m, n):
    size, pixels = parts[0].shape
    depth, width = weight.shape

    def body(*refs):
        ins, w_ref, outs = refs[:n], refs[n], refs[n + 1 : n + 1 + m]
        held, total = refs[n + 1 + m :]
        z = lax.axis_index("cout")
        for k in range(n):
            held[rows_at(source(z, k, n), size), :] = ins[k][...]
        total[...] = dot(w_ref[...], held[...], NN)
        write_chunks(outs, total, lax.axis_index("cin"), m)

    outs = one_step(
        body,
        [*parts, weight],
        [like((depth // m, pixels))] * m + [like((width, pixels))],
        [pltpu.VMEM((depth, pixels), F32)],
        2 * depth * width * pixels,
    )
    return outs[:m], outs[m]


def outer_pair(a, b, c, d):
    depth, pixels = a.shape
    width = b.shape[0]

    def body(a_ref, b_ref, c_ref, d_ref, out):
        out[...] = dot(a_ref[...], b_ref[...], NT) + dot(c_ref[...], d_ref[...], NT)

    return one_step(
        body, [a, b, c, d], [like((depth, width), F32)], [], 4 * depth * width * pixels
    )[0]


def axis_size(name):
    return lax.axis_size(name)


def swap(value):
    return lax.ppermute(value, "section", [(0, 1), (1, 0)])


def hold(*groups):
    return lax.optimization_barrier(groups)


def exchange(parts, name):
    n = len(parts)
    return [parts[0]] + [
        lax.ppermute(parts[k], name, [(i, partner(i, k, n)) for i in range(n)])
        for k in range(1, n)
    ]


def spread(shard, name):
    return exchange([shard] * axis_size(name), name)


def add_up(parts):
    total = parts[0].astype(F32)
    for part in parts[1:]:
        total = total + part.astype(F32)
    return total


def turn(images):
    return jnp.transpose(images, (0, 2, 1))


def collect(shard, name, axis):
    n = axis_size(name)
    me = lax.axis_index(name)
    size = shard.shape[axis]
    shape = shard.shape[:axis] + (n * size,) + shard.shape[axis + 1 :]
    filled = lax.dynamic_update_slice_in_dim(jnp.zeros(shape, shard.dtype), shard, me * size, axis)
    for k in range(1, n):
        got = lax.ppermute(shard, name, [(i, partner(i, k, n)) for i in range(n)])
        filled = lax.dynamic_update_slice_in_dim(filled, got, source(me, k, n) * size, axis)
    return filled


def gather(shard, name):
    return lax.all_gather(shard, name, axis=0, tiled=True)


def shards(
    inner_features,
    block_input,
    first_kernel,
    expand_weight,
    reduce_weight,
    stride_kernel,
    output_grad,
):
    m, n = axis_size("cin"), axis_size("cout")
    features = turn(inner_features)[0]
    skip = turn(block_input)[0]
    cots = turn(output_grad)

    feature_block = gather(features, "cout")
    feature_block, cots = hold(feature_block, cots)
    cot_block = collect(cots, "cout", 1)
    first_parts = exchange(conv_forward(feature_block, first_kernel, SIDE, m), "cin")
    first_hidden = add_up(first_parts)
    first_act = smooth_gate(first_hidden).astype(BF16)
    first_block = gather(first_act, "cin")

    expand_parts = expand(first_block, expand_weight, n)
    expand_parts, cot_block = hold(expand_parts, cot_block)
    expand_got = exchange(expand_parts, "cout")
    back_kept, back_sent = half_back(cot_block, stride_kernel, SIDE)
    expand_got, back_kept, back_sent = hold(expand_got, back_kept, back_sent)
    joined_pre = skip.astype(F32) + add_up(expand_got)
    joined = smooth_gate(joined_pre).astype(BF16)

    joined_parts = [round_send(joined, r, n) for r in range(n)]
    back_parts = add_halves(back_kept, swap(back_sent), m)
    back_got = exchange(back_parts, "cin")
    joined_parts, back_got = hold(joined_parts, back_got)
    back_piece = add_up(back_got)
    joined_two, hidden_kept, hidden_sent = reduce_forward(joined_parts, reduce_weight, n)
    hidden_parts = add_halves(hidden_kept, swap(hidden_sent), m)
    hidden_piece = add_up(exchange(hidden_parts, "cin"))
    act_piece = smooth_gate(hidden_piece).astype(BF16)
    masked_piece = (back_piece * gate_slope(hidden_piece)).astype(BF16)

    size = masked_piece.shape[0] // 2
    masked_mine = [gather(masked_piece[i * size : (i + 1) * size], "cin") for i in range(2)]
    masked_other = [swap(v) for v in masked_mine]
    back_rounds = reduce_back(masked_mine, masked_other, reduce_weight, n)
    back_rounds, act_piece, joined_two = hold(back_rounds, act_piece, joined_two)
    back_got = [round_send(back_rounds[r], r, n, True) for r in range(n)]
    act_parts = spread(act_piece, "cin")
    reduce_gradient = reduce_weight_gradient(joined_two, masked_mine, masked_other)
    back_got, act_parts, reduce_gradient = hold(back_got, act_parts, reduce_gradient)
    back_joined = add_up(back_got)
    input_gradient = (back_joined * gate_slope(joined_pre)).astype(BF16)

    act_parts, input_gradient = hold(act_parts, input_gradient)
    input_parts = spread(input_gradient, "cout")
    act_mine = join_pieces(act_parts, m)
    stride_gradient = half_weight(act_mine, swap(act_mine), cot_block, SIDE)
    input_parts, stride_gradient = hold(input_parts, stride_gradient)

    first_back, input_wide = expand_back(input_parts, expand_weight, m, n)
    first_back, input_wide, first_block = hold(first_back, input_wide, first_block)
    first_got = exchange(first_back, "cin")
    expand_gradient = outer_pair(first_block, input_wide, swap(first_block), swap(input_wide))
    first_got, expand_gradient = hold(first_got, expand_gradient)
    masked_first = (add_up(first_got) * gate_slope(first_hidden)).astype(BF16)
    masked_block = gather(masked_first, "cin")
    inner_parts = conv_back(masked_block, first_kernel, SIDE, n)
    inner_parts, masked_block, feature_block = hold(inner_parts, masked_block, feature_block)
    inner_got = exchange(inner_parts, "cout")
    first_gradient = conv_weight(
        feature_block, swap(feature_block), masked_block, swap(masked_block), SIDE
    )
    inner_got, first_gradient = hold(inner_got, first_gradient)
    inner_gradient = add_up(inner_got)
    return (
        turn(inner_gradient[None]),
        turn(input_gradient[None]),
        first_gradient,
        expand_gradient,
        reduce_gradient,
        stride_gradient,
    )


def solution(mesh):
    return jax.shard_map(
        shards,
        mesh=mesh,
        in_specs=(
            P("section", None, ("cin", "cout")),
            P("section", None, ("cin", "cout")),
            P(None, "cin", "cout"),
            P("cout", "cin"),
            P(("cin", "section"), "cout"),
            P(None, "cout", ("section", "cin")),
            P(None, None, ("section", "cin", "cout")),
        ),
        out_specs=(
            P("section", None, ("cin", "cout")),
            P("section", None, ("cin", "cout")),
            P(None, "cin", "cout"),
            P("cout", "cin"),
            P(("cin", "section"), "cout"),
            P(None, "cout", ("section", "cin")),
        ),
        check_vma=False,
    )
```

time: 1220 us -> 517 us (0.42)
  local copies, waits for them, and re-layouts: 407 us -> 51 us
  waiting for transfers between devices: 457 us -> 122 us
  Pallas kernels: 0 us -> 165 us
  matrix products: 162 us -> 0 us
  starting transfers between devices: 0.9 us -> 78.7 us
  other arithmetic: 70.9 us -> 8.74 us
  between operations: 18.9 us -> 1.34 us
    unnamed x17 -> x0, waiting for transfers between devices: 249 us -> none
    pallas_call x0 -> x14, Pallas kernels: none -> 165 us  [the longest x9 59.8 us: one_step(): pl.pallas_call(body, out_shape=outs, in_specs=[pl.BlockSpec(memory_space=...]
    dot_general x51 -> x0, matrix products: 162 us -> none  [the longest x9 39.5 us: conv_same(): jnp.dot(window, kernel[3 * row + column], preferred_element_type=jnp.floa...]
    slice x17 -> x1, local copies, waits for them, and re-layouts: 126 us -> 0.84 us  [shards(): masked_piece[i * size:(i + 1) * size]]
    ppermute x0 -> x44, waiting for transfers between devices: none -> 122 us  [the longest x24 76.7 us: exchange(): lax.ppermute(parts[k], name, [(i, partner(i, k, n)) for i in range(n)])]
    reduce_scatter x2 -> x0, waiting for transfers between devices: 87.7 us -> none  [the longest x1 79.2 us: shards(): lax.psum_scatter(hidden_part, ('section', 'cin'), scatter_dimension=2, ti...]
    reshape x33 -> x0, local copies, waits for them, and re-layouts: 87.1 us -> none  [the longest x8 16.1 us: conv_same(): padded[:, row:row + side, column:column + side, :]]
    all_gather x4 -> x0, waiting for transfers between devices: 86.3 us -> none  [the longest x2 48.3 us: gather_outer(): return lax.all_gather(shard, 'cout', axis=2, tiled=True)]
  transfers between devices with their start and end apart: 12 -> 44, of which waited for: 9 -> 14; matrix products, arithmetic and copies ran while one was open for 40% -> 5% of each run, Pallas kernels for 0% -> 22%
where the time goes in v1:
time: 517 us; the launch traced here: 511 us
  Pallas kernels  165 us (32%)
  waiting for transfers between devices  122 us (24%)
  blocking collectives  84.8 us (16%)
  starting transfers between devices  78.7 us (15%)
  local copies, waits for them, and re-layouts  51 us (10%)
  other arithmetic  8.74 us (2%)
    all_gather x5, blocking collectives, gather(): return lax.all_gather(shard, name, axis=0, tiled=True)  84.8 us
    ppermute x24, waiting for transfers between devices, exchange(): lax.ppermute(parts[k], name, [(i, partner(i, k, n)) for i in range(n)])  76.7 us
    pallas_call x9, Pallas kernels, one_step(): pl.pallas_call(body, out_shape=outs, in_specs=[pl.BlockSpec(memory_space=...  59.8 us
    ppermute x8, waiting for transfers between devices, round_send(): return lax.ppermute(value, ('section', 'cout'), round_pairs(r, n, back))  40.9 us
    ppermute x24, starting transfers between devices, exchange(): lax.ppermute(parts[k], name, [(i, partner(i, k, n)) for i in range(n)])  33.2 us
    pallas_call x1, Pallas kernels, conv_weight(): pl.pallas_call(functools.partial(conv_weight_body, side=side), out_shape=...  25.4 us
    pallas_call x1, Pallas kernels, half_back(): pl.pallas_call(functools.partial(half_back_body, side=side), out_shape=[l...  24.5 us
    ppermute x9, local copies, waits for them, and re-layouts, swap(): return lax.ppermute(value, 'section', [(0, 1), (1, 0)])  23.6 us
  transfers between devices with their start and end apart: 44, of which 14 were waited for; matrix products, arithmetic and copies ran while one was open for 5% of the time, Pallas kernels for 22%

profile of v1, /device:TPU:0, one launch (start us, length us, event | category | flops | bytes accessed | tf_op | source)
XLA Modules:
  0.0 511.4 jit_solution(9246129526967360400)
XLA Ops:
  0.6 26.6 %all-gather = bf16[1,640,784]{2,1,0:T(8,128)(2,1)} all-gather(bf16[1,160,784]{2,1,0:T(8,128)(2,1)} %bitcast.22), channel_id=2, replica_groups=mesh['section'=2,'cin'=4,'cout'=4] {'cout'}, dimensions={1}, use_global_device_ids=true | all-gather | bytes 1254400 | tf_op jit(solution)/shard_map/all_gather | solution.py:604
  27.2 2.3 collective-permute-start.5
  29.5 2.1 collective-permute-start.3
  31.6 16.6 %shard_map.118 = (bf16[160,784]{1,0:T(8,128)(2,1)}, bf16[160,784]{1,0:T(8,128)(2,1)}, bf16[160,784]{1,0:T(8,128)(2,1)}, bf16[160,784]{1,0:T(8,128)(2,1)}) custom-call(bf16[640,784]{1,0:T(8,128)(2,1)} %bitcast.18, bf16[9,640,640]{2,1,0:T(8,128)(2,1)} %w_ref.7), custom_call_target="tpu_custom_call" | custom-call | flops 5780275200 | bytes 9379840 | tf_op jit(solution)/shard_map/pallas_call | solution.py:132
  48.2 1.5 collective-permute-start
  49.8 1.5 collective-permute-start.1
  52.0 6.2 %collective-permute-done = bf16[160,784]{1,0:T(8,128)(2,1)S(1)} collective-permute-done((bf16[160,784]{1,0:T(8,128)(2,1)}, bf16[160,784]{1,0:T(8,128)(2,1)S(1)}, u32[]{:S(2)}, u32[]{:S(2)}) %collective-permute-start) | collective-permute-done | bytes 250912 | tf_op jit(solution)/shard_map/ppermute | solution.py:571
  58.2 4.5 collective-permute-done.1
  63.4 14.7 %all_gather.16.x_ref.a_ref = bf16[640,784]{1,0:T(8,128)(2,1)} all-gather(bf16[160,784]{1,0:T(8,128)(2,1)S(1)} %multiply_convert_fusion.5), channel_id=1, replica_groups=mesh['section'=2,'cin'=4,'cout'=4] {'cin'}, dimensions={0}, use_global_device_ids=true | all-gather | bytes 1254400 | tf_op jit(solution)/shard_map/all_gather | solution.py:604
  78.1 5.7 %shard_map.119 = (bf16[320,784]{1,0:T(8,128)(2,1)}, bf16[320,784]{1,0:T(8,128)(2,1)}, bf16[320,784]{1,0:T(8,128)(2,1)}, bf16[320,784]{1,0:T(8,128)(2,1)}) custom-call(bf16[640,784]{1,0:T(8,128)(2,1)} %all_gather.16.x_ref.a_ref, bf16[640,1280]{1,0:T(8,128)(2,1)} %refs_4_.5), custom_call_target="tpu_custom_call" | custom-call | flops 1284505600 | bytes 4648960 | tf_op jit(solution)/shard_map/pallas_call | solution.py:80
  84.1 2.6 collective-permute-start.7
  88.1 24.5 %shard_map.120 = (bf16[1280,784]{1,0:T(8,128)(2,1)}, bf16[1280,784]{1,0:T(8,128)(2,1)}) custom-call(bf16[2,640,196]{2,1,0:T(8,128)(2,1)} %copy-done.23, bf16[9,1280,640]{2,1,0:T(8,128)(2,1)} %w_ref.6), custom_call_target="tpu_custom_call" | custom-call | flops 11560550400 | bytes 14745600 | tf_op jit(solution)/shard_map/pallas_call | solution.py:289
  112.6 12.9 %collective-permute-done.7 = bf16[320,784]{1,0:T(8,128)(2,1)S(1)} collective-permute-done((bf16[320,784]{1,0:T(8,128)(2,1)}, bf16[320,784]{1,0:T(8,128)(2,1)S(1)}, u32[]{:S(2)}, u32[]{:S(2)}) %collective-permute-start.7) | collective-permute-done | bytes 501792 | tf_op jit(solution)/shard_map/ppermute | solution.py:571
  125.6 4.5 copy.13
  130.7 2.0 collective-permute-start.12
  132.7 8.1 %collective-permute-start.11 = (bf16[320,784]{1,0:T(8,128)(2,1)S(1)}, bf16[320,784]{1,0:T(8,128)(2,1)S(1)}, u32[]{:S(2)}, u32[]{:S(2)}) collective-permute-start(bf16[320,784]{1,0:T(8,128)(2,1)S(1)} %multiply_convert_fusion.3), channel_id=1, source_target_pairs={{0,2},{1,3},{2,16},{3,17},{16,0},{17,1},{18,18},{19,19},{4,6},{5,7... | collective-permute-start | bytes 1505288 | tf_op jit(solution)/shard_map/ppermute | solution.py:397
  142.3 4.3 copy.14.b_ref
  146.6 4.6 shard_map.121
  156.6 10.0 %collective-permute-done.10.refs_1_ = bf16[320,784]{1,0:T(8,128)(2,1)} collective-permute-done((bf16[320,784]{1,0:T(8,128)(2,1)S(1)}, bf16[320,784]{1,0:T(8,128)(2,1)}, u32[]{:S(2)}, u32[]{:S(2)}) %collective-permute-start.10) | collective-permute-done | bytes 501792 | tf_op jit(solution)/shard_map/ppermute | solution.py:397
  166.6 8.2 %collective-permute-done.15 = bf16[320,784]{1,0:T(8,128)(2,1)S(1)} collective-permute-done((bf16[320,784]{1,0:T(8,128)(2,1)}, bf16[320,784]{1,0:T(8,128)(2,1)S(1)}, u32[]{:S(2)}, u32[]{:S(2)}) %collective-permute-start.15) | collective-permute-done | bytes 501792 | tf_op jit(solution)/shard_map/ppermute | solution.py:571
  174.9 10.7 %shard_map.122 = (bf16[2,640,784]{2,1,0:T(8,128)(2,1)}, bf16[1280,784]{1,0:T(8,128)(2,1)}, bf16[1280,784]{1,0:T(8,128)(2,1)}) custom-call(bf16[320,784]{1,0:T(8,128)(2,1)} %collective-permute-done.9.refs_0_, bf16[320,784]{1,0:T(8,128)(2,1)} %collective-permute-done.10.refs_1_, bf16[320,784]{1,0:T(8,128)(2,1)} %copy-done.40, bf16[320,784]{1,0:T(8,128)(2,1)} %copy-done.39, ...), custom_call_target="tpu_custom_call" | custom-call | flops 2569011200 | bytes 9666560 | tf_op jit(solution)/shard_map/pallas_call | solution.py:80
  185.6 3.1 copy.15
  188.7 19.5 %collective-permute-start.17 = (bf16[1280,784]{0,1:T(8,128)(2,1)S(1)}, bf16[1280,784]{0,1:T(8,128)(2,1)}, u32[]{:S(2)}, u32[]{:S(2)}) collective-permute-start(bf16[1280,784]{0,1:T(8,128)(2,1)S(1)} %copy.15), channel_id=1, source_target_pairs={{0,16},{16,0},{1,17},{17,1},{2,18},{18,2},{3,19},{19,3},{4,20},{20... | collective-permute-start | bytes 6021128 | tf_op jit(solution)/shard_map/ppermute | solution.py:561
  208.2 3.8 collective-permute-done.17
  212.0 4.1 copy.16.b_ref
  216.1 4.8 shard_map.123
  224.4 12.6 %collective-permute-done.18 = bf16[320,784]{1,0:T(8,128)(2,1)S(1)} collective-permute-done((bf16[320,784]{1,0:T(8,128)(2,1)}, bf16[320,784]{1,0:T(8,128)(2,1)S(1)}, u32[]{:S(2)}, u32[]{:S(2)}) %collective-permute-start.18) | collective-permute-done | bytes 501792 | tf_op jit(solution)/shard_map/ppermute | solution.py:571
  237.0 12.0 %collective-permute-done.19 = bf16[320,784]{1,0:T(8,128)(2,1)S(1)} collective-permute-done((bf16[320,784]{1,0:T(8,128)(2,1)}, bf16[320,784]{1,0:T(8,128)(2,1)S(1)}, u32[]{:S(2)}, u32[]{:S(2)}) %collective-permute-start.19) | collective-permute-done | bytes 501792 | tf_op jit(solution)/shard_map/ppermute | solution.py:571
  249.0 2.0 multiply_convert_fusion.1
  251.9 12.9 %all_gather.18.refs_1_ = bf16[640,784]{1,0:T(8,128)(2,1)S(1)} all-gather(bf16[160,784]{1,0:T(8,128)(2,1)S(1)} %get-tuple-element.212), channel_id=1, replica_groups=mesh['section'=2,'cin'=4,'cout'=4] {'cin'}, dimensions={0}, use_global_device_ids=true | all-gather | bytes 1254400 | tf_op jit(solution)/shard_map/all_gather | solution.py:604
  264.8 1.7 copy.18
  266.5 15.5 %all_gather.17.refs_0_ = bf16[640,784]{1,0:T(8,128)(2,1)S(1)} all-gather(bf16[160,784]{1,0:T(8,128)(2,1)} %get-tuple-element.213), channel_id=1, replica_groups=mesh['section'=2,'cin'=4,'cout'=4] {'cin'}, dimensions={0}, use_global_device_ids=true | all-gather | bytes 1254400 | tf_op jit(solution)/shard_map/all_gather | solution.py:604
  282.1 1.9 copy.17
  284.0 2.4 copy.20.refs_3_
  286.8 1.6 copy.19.refs_2_
  288.4 7.6 %shard_map.124 = (bf16[320,784]{1,0:T(8,128)(2,1)}, bf16[320,784]{1,0:T(8,128)(2,1)}, bf16[320,784]{1,0:T(8,128)(2,1)}, bf16[320,784]{1,0:T(8,128)(2,1)}) custom-call(bf16[640,784]{1,0:T(8,128)(2,1)} %copy-done.2, bf16[640,784]{1,0:T(8,128)(2,1)} %copy-done.1, bf16[640,784]{1,0:T(8,128)(2,1)} %copy.19.refs_2_, bf16[640,784]{1,0:T(8,128)(2,1)} %copy.20.refs_3_, ...), custom_call_target="tpu_custom_call" | custom-call | flops 2569011200 | bytes 7659520 | tf_op jit(solution)/shard_map/pallas_call | solution.py:80
  296.0 1.9 collective-permute-start.23
  298.4 5.2 %collective-permute-start.25 = (bf16[320,784]{1,0:T(8,128)(2,1)}, bf16[320,784]{1,0:T(8,128)(2,1)S(1)}, u32[]{:S(2)}, u32[]{:S(2)}) collective-permute-start(bf16[320,784]{1,0:T(8,128)(2,1)} %get-tuple-element.156), channel_id=1, source_target_pairs={{2,0},{3,1},{16,2},{17,3},{0,16},{1,17},{18,18},{19,19},{6,4},{7,5... | collective-permute-start | bytes 1505288 | tf_op jit(solution)/shard_map/ppermute | solution.py:397
  307.0 6.4 %collective-permute-done.24 = bf16[320,784]{1,0:T(8,128)(2,1)S(1)} collective-permute-done((bf16[320,784]{1,0:T(8,128)(2,1)}, bf16[320,784]{1,0:T(8,128)(2,1)S(1)}, u32[]{:S(2)}, u32[]{:S(2)}) %collective-permute-start.24) | collective-permute-done | bytes 501792 | tf_op jit(solution)/shard_map/ppermute | solution.py:397
  314.0 8.5 %shard_map.125 = f32[640,1280]{1,0:T(8,128)} custom-call(bf16[2,640,784]{2,1,0:T(8,128)(2,1)} %get-tuple-element.159.j_ref, bf16[640,784]{1,0:T(8,128)(2,1)} %copy-done.2, bf16[640,784]{1,0:T(8,128)(2,1)} %copy-done.1, bf16[640,784]{1,0:T(8,128)(2,1)} %copy.19.refs_2_, bf16[640,784]{1,0:T(8,128)(2,1)} %copy.20.refs_3_), custom_call_target="tpu_custom_call" | custom-call | flops 2569011200 | bytes 9297920 | tf_op jit(solution)/shard_map/pallas_call | solution.py:80
  322.5 23.0 %collective-permute-done.25 = bf16[320,784]{1,0:T(8,128)(2,1)S(1)} collective-permute-done((bf16[320,784]{1,0:T(8,128)(2,1)}, bf16[320,784]{1,0:T(8,128)(2,1)S(1)}, u32[]{:S(2)}, u32[]{:S(2)}) %collective-permute-start.25) | collective-permute-done | bytes 501792 | tf_op jit(solution)/shard_map/ppermute | solution.py:397
  346.3 2.4 multiply_convert_fusion.refs_0_
  348.8 3.5 shard_map.126.a_ref
  352.3 4.5 copy.23
  356.8 2.2 collective-permute-start.32
  359.0 5.9 %collective-permute-start.31 = (bf16[320,784]{1,0:T(8,128)(2,1)S(1)}, bf16[320,784]{1,0:T(8,128)(2,1)}, u32[]{:S(2)}, u32[]{:S(2)}) collective-permute-start(bf16[320,784]{1,0:T(8,128)(2,1)S(1)} %multiply_convert_fusion.refs_0_), channel_id=1, source_target_pairs={{0,2},{1,3},{2,0},{3,1},{4,6},{5,7},{6,4},{7,5},{8,10},{9,11},{10,... | collective-permute-start | bytes 1505288 | tf_op jit(solution)/shard_map/ppermute | solution.py:571
  364.9 2.9 copy.24.b_ref
  367.9 22.8 %shard_map.127 = f32[9,1280,640]{2,1,0:T(8,128)} custom-call(bf16[1280,784]{1,0:T(8,128)(2,1)} %shard_map.126.a_ref, bf16[1280,784]{1,0:T(8,128)(2,1)} %copy.24.b_ref, bf16[2,640,196]{2,1,0:T(8,128)(2,1)} %copy-done.23), custom_call_target="tpu_custom_call" | custom-call | flops 11560550400 | bytes 29491200 | tf_op jit(solution)/shard_map/pallas_call | solution.py:338
  390.6 20.3 %collective-permute-done.31.refs_2_ = bf16[320,784]{1,0:T(8,128)(2,1)} collective-permute-done((bf16[320,784]{1,0:T(8,128)(2,1)S(1)}, bf16[320,784]{1,0:T(8,128)(2,1)}, u32[]{:S(2)}, u32[]{:S(2)}) %collective-permute-start.31) | collective-permute-done | bytes 501792 | tf_op jit(solution)/shard_map/ppermute | solution.py:571
  410.9 6.0 %shard_map.128 = (bf16[160,784]{1,0:T(8,128)(2,1)}, bf16[160,784]{1,0:T(8,128)(2,1)}, bf16[160,784]{1,0:T(8,128)(2,1)}, bf16[160,784]{1,0:T(8,128)(2,1)}, bf16[1280,784]{1,0:T(8,128)(2,1)}) custom-call(bf16[320,784]{1,0:T(8,128)(2,1)} %copy-done.27, bf16[320,784]{1,0:T(8,128)(2,1)} %collective-permute-done.30.refs_1_, ...), custom_call_target="tpu_custom_call" | custom-call | flops 1284505600 | bytes 6656000 | tf_op jit(solution)/shard_map/pallas_call | solution.py:80
  416.9 4.2 copy.26
  421.2 1.7 copy.25
  426.8 1.6 copy.27.c_ref
  428.4 3.2 copy.28.d_ref
  431.7 8.4 %shard_map.129 = f32[640,1280]{1,0:T(8,128)} custom-call(bf16[640,784]{1,0:T(8,128)(2,1)} %all_gather.16.x_ref.a_ref, bf16[1280,784]{1,0:T(8,128)(2,1)} %get-tuple-element.187.b_ref, bf16[640,784]{1,0:T(8,128)(2,1)} %copy.27.c_ref, bf16[1280,784]{1,0:T(8,128)(2,1)} %copy.28.d_ref), custom_call_target="tpu_custom_call" | custom-call | flops 2569011200 | bytes 9297920 | tf_op jit(solution)/shard_map/pallas_call | solution.py:80
  440.1 1.5 multiply_convert_fusion.4
  441.6 15.1 %all_gather.19.m_ref.ma_ref = bf16[640,784]{1,0:T(8,128)(2,1)} all-gather(bf16[160,784]{1,0:T(8,128)(2,1)S(1)} %multiply_convert_fusion.4), channel_id=1, replica_groups=mesh['section'=2,'cin'=4,'cout'=4] {'cin'}, dimensions={0}, use_global_device_ids=true | all-gather | bytes 1254400 | tf_op jit(solution)/shard_map/all_gather | solution.py:604
  456.7 16.0 %shard_map.130 = (bf16[160,784]{1,0:T(8,128)(2,1)}, bf16[160,784]{1,0:T(8,128)(2,1)}, bf16[160,784]{1,0:T(8,128)(2,1)}, bf16[160,784]{1,0:T(8,128)(2,1)}) custom-call(bf16[640,784]{1,0:T(8,128)(2,1)} %all_gather.19.m_ref.ma_ref, bf16[9,640,640]{2,1,0:T(8,128)(2,1)} %w_ref.7), custom_call_target="tpu_custom_call" | custom-call | flops 5780275200 | bytes 9379840 | tf_op jit(solution)/shard_map/pallas_call | solution.py:172
  472.7 1.7 copy.30
  476.0 3.0 collective-permute-start.40
  480.4 1.6 copy.32.mb_ref
  482.0 1.7 copy.31.xb_ref
  483.7 25.4 %shard_map.131 = f32[9,640,640]{2,1,0:T(8,128)} custom-call(bf16[640,784]{1,0:T(8,128)(2,1)} %bitcast.19, bf16[640,784]{1,0:T(8,128)(2,1)} %copy.31.xb_ref, bf16[640,784]{1,0:T(8,128)(2,1)} %all_gather.19.m_ref.ma_ref, bf16[640,784]{1,0:T(8,128)(2,1)} %copy.32.mb_ref), custom_call_target="tpu_custom_call" | custom-call | flops 11560550400 | bytes 14745600 | tf_op jit(solution)/shard_map/pallas_call | solution.py:213
  509.2 2.0 add_bitcast_fusion
  (157 shorter events, 27.9 us)
Async XLA Ops:
  0.6 26.6 %copy-start.38 = (bf16[2,196,160]{1,2,0:T(8,128)(2,1)S(1)}, bf16[2,196,160]{1,2,0:T(8,128)(2,1)}, u32[]{:S(2)}) copy-start(bf16[2,196,160]{1,2,0:T(8,128)(2,1)} %param.13) | copy-start | bytes 376324
  27.2 24.8 %collective-permute-start.5 = (bf16[2,160,196]{2,1,0:T(8,128)(2,1)S(1)}, bf16[2,160,196]{2,1,0:T(8,128)(2,1)S(1)}, u32[]{:S(2)}, u32[]{:S(2)}) collective-permute-start(bf16[2,160,196]{2,1,0:T(8,128)(2,1)S(1)} %bitcast.23), channel_id=1, source_target_pairs={{0,3},{1,2},{2,1},{3,0},{4,7},{5,6},{6,5},{7,4},{8,11},{9,10},{10,... | collective-permute-start | bytes 376328 | tf_op jit(solution)/shard_map/ppermute | solution.py:598
  29.5 22.4 %collective-permute-start.4 = (bf16[2,160,196]{2,1,0:T(8,128)(2,1)S(1)}, bf16[2,160,196]{2,1,0:T(8,128)(2,1)S(1)}, u32[]{:S(2)}, u32[]{:S(2)}) collective-permute-start(bf16[2,160,196]{2,1,0:T(8,128)(2,1)S(1)} %bitcast.24), channel_id=1, source_target_pairs={{0,2},{1,3},{2,0},{3,1},{4,6},{5,7},{6,4},{7,5},{8,10},{9,11},{10,... | collective-permute-start | bytes 376328 | tf_op jit(solution)/shard_map/ppermute | solution.py:598
  29.5 21.9 %collective-permute-start.3 = (bf16[2,160,196]{2,1,0:T(8,128)(2,1)S(1)}, bf16[2,160,196]{2,1,0:T(8,128)(2,1)S(1)}, u32[]{:S(2)}, u32[]{:S(2)}) collective-permute-start(bf16[2,160,196]{2,1,0:T(8,128)(2,1)S(1)} %bitcast.25), channel_id=1, source_target_pairs={{0,1},{1,0},{2,3},{3,2},{4,5},{5,4},{6,7},{7,6},{8,9},{9,8},{10,11... | collective-permute-start | bytes 376328 | tf_op jit(solution)/shard_map/ppermute | solution.py:598
  48.2 9.9 %collective-permute-start = (bf16[160,784]{1,0:T(8,128)(2,1)}, bf16[160,784]{1,0:T(8,128)(2,1)S(1)}, u32[]{:S(2)}, u32[]{:S(2)}) collective-permute-start(bf16[160,784]{1,0:T(8,128)(2,1)} %get-tuple-element.110), channel_id=1, source_target_pairs={{0,4},{4,0},{8,12},{12,8},{1,5},{5,1},{9,13},{13,9},{2,6},{6,2},{1... | collective-permute-start | bytes 752648 | tf_op jit(solution)/shard_map/ppermute | solution.py:571
  49.8 12.9 %collective-permute-start.1 = (bf16[160,784]{1,0:T(8,128)(2,1)}, bf16[160,784]{1,0:T(8,128)(2,1)S(1)}, u32[]{:S(2)}, u32[]{:S(2)}) collective-permute-start(bf16[160,784]{1,0:T(8,128)(2,1)} %get-tuple-element.111), channel_id=1, source_target_pairs={{0,8},{4,12},{8,0},{12,4},{1,9},{5,13},{9,1},{13,5},{2,10},{6,14},... | collective-permute-start | bytes 752648 | tf_op jit(solution)/shard_map/ppermute | solution.py:571
  51.4 11.3 %collective-permute-start.2 = (bf16[160,784]{1,0:T(8,128)(2,1)}, bf16[160,784]{1,0:T(8,128)(2,1)S(1)}, u32[]{:S(2)}, u32[]{:S(2)}) collective-permute-start(bf16[160,784]{1,0:T(8,128)(2,1)} %get-tuple-element.112), channel_id=1, source_target_pairs={{0,12},{4,8},{8,4},{12,0},{1,13},{5,9},{9,5},{13,1},{2,14},{6,10},... | collective-permute-start | bytes 752648 | tf_op jit(solution)/shard_map/ppermute | solution.py:571
  52.0 31.8 %copy-start.23 = (bf16[2,640,196]{2,1,0:T(8,128)(2,1)}, bf16[2,640,196]{2,1,0:T(8,128)(2,1)S(1)}, u32[]{:S(2)}) copy-start(bf16[2,640,196]{2,1,0:T(8,128)(2,1)S(1)} %constant_dynamic-update-slice_fusion.g_ref) | copy-start | bytes 1505284
  58.2 19.9 %copy-start.17 = (bf16[160,784]{1,0:T(8,128)(2,1)}, bf16[160,784]{1,0:T(8,128)(2,1)S(1)}, u32[]{:S(2)}) copy-start(bf16[160,784]{1,0:T(8,128)(2,1)S(1)} %collective-permute-done) | copy-start | bytes 752644
  83.7 28.9 %collective-permute-start.6 = (bf16[320,784]{1,0:T(8,128)(2,1)}, bf16[320,784]{1,0:T(8,128)(2,1)S(1)}, u32[]{:S(2)}, u32[]{:S(2)}) collective-permute-start(bf16[320,784]{1,0:T(8,128)(2,1)} %get-tuple-element.119), channel_id=1, source_target_pairs={{0,1},{1,0},{2,3},{3,2},{4,5},{5,4},{6,7},{7,6},{8,9},{9,8},{10,11... | collective-permute-start | bytes 1505288 | tf_op jit(solution)/shard_map/ppermute | solution.py:571
  84.1 41.5 %collective-permute-start.7 = (bf16[320,784]{1,0:T(8,128)(2,1)}, bf16[320,784]{1,0:T(8,128)(2,1)S(1)}, u32[]{:S(2)}, u32[]{:S(2)}) collective-permute-start(bf16[320,784]{1,0:T(8,128)(2,1)} %get-tuple-element.120), channel_id=1, source_target_pairs={{0,2},{1,3},{2,0},{3,1},{4,6},{5,7},{6,4},{7,5},{8,10},{9,11},{10,... | collective-permute-start | bytes 1505288 | tf_op jit(solution)/shard_map/ppermute | solution.py:571
  86.7 38.9 %collective-permute-start.8 = (bf16[320,784]{1,0:T(8,128)(2,1)}, bf16[320,784]{1,0:T(8,128)(2,1)S(1)}, u32[]{:S(2)}, u32[]{:S(2)}) collective-permute-start(bf16[320,784]{1,0:T(8,128)(2,1)} %get-tuple-element.121), channel_id=1, source_target_pairs={{0,3},{1,2},{2,1},{3,0},{4,7},{5,6},{6,5},{7,4},{8,11},{9,10},{10,... | collective-permute-start | bytes 1505288 | tf_op jit(solution)/shard_map/ppermute | solution.py:571
  112.6 17.5 %copy-start.9 = (bf16[320,784]{1,0:T(8,128)(2,1)}, bf16[320,784]{1,0:T(8,128)(2,1)S(1)}, u32[]{:S(2)}) copy-start(bf16[320,784]{1,0:T(8,128)(2,1)S(1)} %collective-permute-done.6) | copy-start | bytes 1505284
  130.1 12.2 %collective-permute-start.13 = (bf16[1280,784]{0,1:T(8,128)(2,1)}, bf16[1280,784]{0,1:T(8,128)(2,1)}, u32[]{:S(2)}, u32[]{:S(2)}) collective-permute-start(bf16[1280,784]{0,1:T(8,128)(2,1)} %copy.13), channel_id=1, source_target_pairs={{0,16},{16,0},{1,17},{17,1},{2,18},{18,2},{3,19},{19,3},{4,20},{20... | collective-permute-start | bytes 6021128 | tf_op jit(solution)/shard_map/ppermute | solution.py:561
  130.7 21.9 %collective-permute-start.12 = (bf16[320,784]{1,0:T(8,128)(2,1)S(1)}, bf16[320,784]{1,0:T(8,128)(2,1)S(1)}, u32[]{:S(2)}, u32[]{:S(2)}) collective-permute-start(bf16[320,784]{1,0:T(8,128)(2,1)S(1)} %multiply_convert_fusion.3), channel_id=1, source_target_pairs={{0,3},{1,2},{2,17},{3,16},{16,1},{17,0},{18,19},{19,18},{4,7},{5,6... | collective-permute-start | bytes 1505288 | tf_op jit(solution)/shard_map/ppermute | solution.py:397
  132.7 21.6 %collective-permute-start.11 = (bf16[320,784]{1,0:T(8,128)(2,1)S(1)}, bf16[320,784]{1,0:T(8,128)(2,1)S(1)}, u32[]{:S(2)}, u32[]{:S(2)}) collective-permute-start(bf16[320,784]{1,0:T(8,128)(2,1)S(1)} %multiply_convert_fusion.3), channel_id=1, source_target_pairs={{0,2},{1,3},{2,16},{3,17},{16,0},{17,1},{18,18},{19,19},{4,6},{5,7... | collective-permute-start | bytes 1505288 | tf_op jit(solution)/shard_map/ppermute | solution.py:397
  140.8 25.8 %collective-permute-start.10 = (bf16[320,784]{1,0:T(8,128)(2,1)S(1)}, bf16[320,784]{1,0:T(8,128)(2,1)}, u32[]{:S(2)}, u32[]{:S(2)}) collective-permute-start(bf16[320,784]{1,0:T(8,128)(2,1)S(1)} %multiply_convert_fusion.3), channel_id=1, source_target_pairs={{0,1},{1,0},{2,19},{3,18},{16,3},{17,2},{18,17},{19,16},{4,5},{5,4... | collective-permute-start | bytes 1505288 | tf_op jit(solution)/shard_map/ppermute | solution.py:397
  140.9 25.8 %collective-permute-start.9 = (bf16[320,784]{1,0:T(8,128)(2,1)S(1)}, bf16[320,784]{1,0:T(8,128)(2,1)}, u32[]{:S(2)}, u32[]{:S(2)}) collective-permute-start(bf16[320,784]{1,0:T(8,128)(2,1)S(1)} %multiply_convert_fusion.3), channel_id=1, source_target_pairs={{0,0},{1,1},{2,18},{3,19},{16,2},{17,3},{18,16},{19,17},{4,4},{5,5... | collective-permute-start | bytes 1505288 | tf_op jit(solution)/shard_map/ppermute | solution.py:397
  151.2 15.4 %collective-permute-start.14 = (bf16[320,784]{1,0:T(8,128)(2,1)}, bf16[320,784]{1,0:T(8,128)(2,1)S(1)}, u32[]{:S(2)}, u32[]{:S(2)}) collective-permute-start(bf16[320,784]{1,0:T(8,128)(2,1)} %get-tuple-element.132), channel_id=1, source_target_pairs={{0,4},{4,0},{8,12},{12,8},{1,5},{5,1},{9,13},{13,9},{2,6},{6,2},{1... | collective-permute-start | bytes 1505288 | tf_op jit(solution)/shard_map/ppermute | solution.py:571
  152.7 22.2 %copy-start.39 = (bf16[320,784]{1,0:T(8,128)(2,1)}, bf16[320,784]{1,0:T(8,128)(2,1)S(1)}, u32[]{:S(2)}) copy-start(bf16[320,784]{1,0:T(8,128)(2,1)S(1)} %collective-permute-done.12.refs_3_) | copy-start | bytes 1505284
  152.7 22.2 %collective-permute-start.15 = (bf16[320,784]{1,0:T(8,128)(2,1)}, bf16[320,784]{1,0:T(8,128)(2,1)S(1)}, u32[]{:S(2)}, u32[]{:S(2)}) collective-permute-start(bf16[320,784]{1,0:T(8,128)(2,1)} %get-tuple-element.133), channel_id=1, source_target_pairs={{0,8},{4,12},{8,0},{12,4},{1,9},{5,13},{9,1},{13,5},{2,10},{6,14},... | collective-permute-start | bytes 1505288 | tf_op jit(solution)/shard_map/ppermute | solution.py:571
  155.1 19.7 %collective-permute-start.16 = (bf16[320,784]{1,0:T(8,128)(2,1)}, bf16[320,784]{1,0:T(8,128)(2,1)S(1)}, u32[]{:S(2)}, u32[]{:S(2)}) collective-permute-start(bf16[320,784]{1,0:T(8,128)(2,1)} %get-tuple-element.134), channel_id=1, source_target_pairs={{0,12},{4,8},{8,4},{12,0},{1,13},{5,9},{9,5},{13,1},{2,14},{6,10},... | collective-permute-start | bytes 1505288 | tf_op jit(solution)/shard_map/ppermute | solution.py:571
  166.6 18.9 %copy-start.29 = (bf16[320,784]{1,0:T(8,128)(2,1)}, bf16[320,784]{1,0:T(8,128)(2,1)S(1)}, u32[]{:S(2)}) copy-start(bf16[320,784]{1,0:T(8,128)(2,1)S(1)} %collective-permute-done.14) | copy-start | bytes 1505284
  188.7 23.3 %collective-permute-start.17 = (bf16[1280,784]{0,1:T(8,128)(2,1)S(1)}, bf16[1280,784]{0,1:T(8,128)(2,1)}, u32[]{:S(2)}, u32[]{:S(2)}) collective-permute-start(bf16[1280,784]{0,1:T(8,128)(2,1)S(1)} %copy.15), channel_id=1, source_target_pairs={{0,16},{16,0},{1,17},{17,1},{2,18},{18,2},{3,19},{19,3},{4,20},{20... | collective-permute-start | bytes 6021128 | tf_op jit(solution)/shard_map/ppermute | solution.py:561
  216.1 32.9 %copy-start.28 = (bf16[320,784]{1,0:T(8,128)(2,1)S(1)}, bf16[320,784]{1,0:T(8,128)(2,1)}, u32[]{:S(2)}) copy-start(bf16[320,784]{1,0:T(8,128)(2,1)} %get-tuple-element.135) | copy-start | bytes 1505284
  216.1 32.9 %copy-start.30 = (bf16[320,784]{1,0:T(8,128)(2,1)S(1)}, bf16[320,784]{1,0:T(8,128)(2,1)}, u32[]{:S(2)}) copy-start(bf16[320,784]{1,0:T(8,128)(2,1)} %copy-done.29) | copy-start | bytes 1505284
  216.1 32.9 %copy-start.32 = (bf16[320,784]{1,0:T(8,128)(2,1)S(1)}, bf16[320,784]{1,0:T(8,128)(2,1)}, u32[]{:S(2)}) copy-start(bf16[320,784]{1,0:T(8,128)(2,1)} %copy-done.31) | copy-start | bytes 1505284
  216.1 32.9 %copy-start.34 = (bf16[320,784]{1,0:T(8,128)(2,1)S(1)}, bf16[320,784]{1,0:T(8,128)(2,1)}, u32[]{:S(2)}) copy-start(bf16[320,784]{1,0:T(8,128)(2,1)} %copy-done.33) | copy-start | bytes 1505284
  220.9 16.1 %collective-permute-start.18 = (bf16[320,784]{1,0:T(8,128)(2,1)}, bf16[320,784]{1,0:T(8,128)(2,1)S(1)}, u32[]{:S(2)}, u32[]{:S(2)}) collective-permute-start(bf16[320,784]{1,0:T(8,128)(2,1)} %get-tuple-element.146), channel_id=1, source_target_pairs={{0,4},{4,0},{8,12},{12,8},{1,5},{5,1},{9,13},{13,9},{2,6},{6,2},{1... | collective-permute-start | bytes 1505288 | tf_op jit(solution)/shard_map/ppermute | solution.py:571
  221.5 27.5 %collective-permute-start.19 = (bf16[320,784]{1,0:T(8,128)(2,1)}, bf16[320,784]{1,0:T(8,128)(2,1)S(1)}, u32[]{:S(2)}, u32[]{:S(2)}) collective-permute-start(bf16[320,784]{1,0:T(8,128)(2,1)} %get-tuple-element.147), channel_id=1, source_target_pairs={{0,8},{4,12},{8,0},{12,4},{1,9},{5,13},{9,1},{13,5},{2,10},{6,14},... | collective-permute-start | bytes 1505288 | tf_op jit(solution)/shard_map/ppermute | solution.py:571
  222.9 26.1 %collective-permute-start.20 = (bf16[320,784]{1,0:T(8,128)(2,1)}, bf16[320,784]{1,0:T(8,128)(2,1)S(1)}, u32[]{:S(2)}, u32[]{:S(2)}) collective-permute-start(bf16[320,784]{1,0:T(8,128)(2,1)} %get-tuple-element.148), channel_id=1, source_target_pairs={{0,12},{4,8},{8,4},{12,0},{1,13},{5,9},{9,5},{13,1},{2,14},{6,10},... | collective-permute-start | bytes 1505288 | tf_op jit(solution)/shard_map/ppermute | solution.py:571
  251.0 62.4 %copy-start.5 = (bf16[320,784]{1,0:T(8,128)(2,1)}, bf16[320,784]{1,0:T(8,128)(2,1)S(1)}, u32[]{:S(2)}) copy-start(bf16[320,784]{1,0:T(8,128)(2,1)S(1)} %get-tuple-element.169.refs_0_) | copy-start | bytes 1505284
  264.8 17.3 %copy-start.1 = (bf16[640,784]{1,0:T(8,128)(2,1)}, bf16[640,784]{1,0:T(8,128)(2,1)S(1)}, u32[]{:S(2)}) copy-start(bf16[640,784]{1,0:T(8,128)(2,1)S(1)} %all_gather.18.refs_1_) | copy-start | bytes 3010564
  266.5 17.4 %collective-permute-start.22 = (bf16[640,784]{0,1:T(8,128)(2,1)}, bf16[640,784]{0,1:T(8,128)(2,1)}, u32[]{:S(2)}, u32[]{:S(2)}) collective-permute-start(bf16[640,784]{0,1:T(8,128)(2,1)} %copy.18), channel_id=1, source_target_pairs={{0,16},{16,0},{1,17},{17,1},{2,18},{18,2},{3,19},{19,3},{4,20},{20... | collective-permute-start | bytes 3010568 | tf_op jit(solution)/shard_map/ppermute | solution.py:561
  284.0 2.8 collective-permute-start.21
  296.0 50.3 %copy-start.8 = (bf16[320,784]{1,0:T(8,128)(2,1)S(1)}, bf16[320,784]{1,0:T(8,128)(2,1)}, u32[]{:S(2)}) copy-start(bf16[320,784]{1,0:T(8,128)(2,1)} %get-tuple-element.125) | copy-start | bytes 1505284
  296.0 50.3 %copy-start.10 = (bf16[320,784]{1,0:T(8,128)(2,1)S(1)}, bf16[320,784]{1,0:T(8,128)(2,1)}, u32[]{:S(2)}) copy-start(bf16[320,784]{1,0:T(8,128)(2,1)} %copy-done.9) | copy-start | bytes 1505284
  296.0 50.3 %copy-start.12 = (bf16[320,784]{1,0:T(8,128)(2,1)S(1)}, bf16[320,784]{1,0:T(8,128)(2,1)}, u32[]{:S(2)}) copy-start(bf16[320,784]{1,0:T(8,128)(2,1)} %copy-done.11) | copy-start | bytes 1505284
  296.0 50.3 %copy-start.14 = (bf16[320,784]{1,0:T(8,128)(2,1)S(1)}, bf16[320,784]{1,0:T(8,128)(2,1)}, u32[]{:S(2)}) copy-start(bf16[320,784]{1,0:T(8,128)(2,1)} %copy-done.13) | copy-start | bytes 1505284
  296.0 10.4 %collective-permute-start.23 = (bf16[320,784]{1,0:T(8,128)(2,1)}, bf16[320,784]{1,0:T(8,128)(2,1)S(1)}, u32[]{:S(2)}, u32[]{:S(2)}) collective-permute-start(bf16[320,784]{1,0:T(8,128)(2,1)} %get-tuple-element.154), channel_id=1, source_target_pairs={{0,0},{1,1},{18,2},{19,3},{2,16},{3,17},{16,18},{17,19},{4,4},{5,5... | collective-permute-start | bytes 1505288 | tf_op jit(solution)/shard_map/ppermute | solution.py:397
  297.8 15.6 %collective-permute-start.24 = (bf16[320,784]{1,0:T(8,128)(2,1)}, bf16[320,784]{1,0:T(8,128)(2,1)S(1)}, u32[]{:S(2)}, u32[]{:S(2)}) collective-permute-start(bf16[320,784]{1,0:T(8,128)(2,1)} %get-tuple-element.155), channel_id=1, source_target_pairs={{1,0},{0,1},{19,2},{18,3},{3,16},{2,17},{17,18},{16,19},{5,4},{4,5... | collective-permute-start | bytes 1505288 | tf_op jit(solution)/shard_map/ppermute | solution.py:397
  298.4 47.1 %collective-permute-start.25 = (bf16[320,784]{1,0:T(8,128)(2,1)}, bf16[320,784]{1,0:T(8,128)(2,1)S(1)}, u32[]{:S(2)}, u32[]{:S(2)}) collective-permute-start(bf16[320,784]{1,0:T(8,128)(2,1)} %get-tuple-element.156), channel_id=1, source_target_pairs={{2,0},{3,1},{16,2},{17,3},{0,16},{1,17},{18,18},{19,19},{6,4},{7,5... | collective-permute-start | bytes 1505288 | tf_op jit(solution)/shard_map/ppermute | solution.py:397
  303.6 41.9 %collective-permute-start.26 = (bf16[320,784]{1,0:T(8,128)(2,1)}, bf16[320,784]{1,0:T(8,128)(2,1)S(1)}, u32[]{:S(2)}, u32[]{:S(2)}) collective-permute-start(bf16[320,784]{1,0:T(8,128)(2,1)} %get-tuple-element.157), channel_id=1, source_target_pairs={{3,0},{2,1},{17,2},{16,3},{1,16},{0,17},{19,18},{18,19},{7,4},{6,5... | collective-permute-start | bytes 1505288 | tf_op jit(solution)/shard_map/ppermute | solution.py:397
  304.9 40.6 %collective-permute-start.29 = (bf16[320,784]{1,0:T(8,128)(2,1)S(1)}, bf16[320,784]{1,0:T(8,128)(2,1)S(1)}, u32[]{:S(2)}, u32[]{:S(2)}) collective-permute-start(bf16[320,784]{1,0:T(8,128)(2,1)S(1)} %get-tuple-element.169.refs_0_), channel_id=1, source_target_pairs={{0,12},{4,8},{8,4},{12,0},{1,13},{5,9},{9,5},{13,1},{2,14},{6,10},... | collective-permute-start | bytes 1505288 | tf_op jit(solution)/shard_map/ppermute | solution.py:571
  306.3 39.1 %collective-permute-start.28 = (bf16[320,784]{1,0:T(8,128)(2,1)S(1)}, bf16[320,784]{1,0:T(8,128)(2,1)S(1)}, u32[]{:S(2)}, u32[]{:S(2)}) collective-permute-start(bf16[320,784]{1,0:T(8,128)(2,1)S(1)} %get-tuple-element.169.refs_0_), channel_id=1, source_target_pairs={{0,8},{4,12},{8,0},{12,4},{1,9},{5,13},{9,1},{13,5},{2,10},{6,14},... | collective-permute-start | bytes 1505288 | tf_op jit(solution)/shard_map/ppermute | solution.py:571
  313.4 32.8 %collective-permute-start.27 = (bf16[320,784]{1,0:T(8,128)(2,1)S(1)}, bf16[320,784]{1,0:T(8,128)(2,1)S(1)}, u32[]{:S(2)}, u32[]{:S(2)}) collective-permute-start(bf16[320,784]{1,0:T(8,128)(2,1)S(1)} %get-tuple-element.169.refs_0_), channel_id=1, source_target_pairs={{0,4},{4,0},{8,12},{12,8},{1,5},{5,1},{9,13},{13,9},{2,6},{6,2},{1... | collective-permute-start | bytes 1505288 | tf_op jit(solution)/shard_map/ppermute | solution.py:571
  348.8 16.2 %copy-start.27 = (bf16[320,784]{1,0:T(8,128)(2,1)}, bf16[320,784]{1,0:T(8,128)(2,1)S(1)}, u32[]{:S(2)}) copy-start(bf16[320,784]{1,0:T(8,128)(2,1)S(1)} %multiply_convert_fusion.refs_0_) | copy-start | bytes 1505284
  356.7 8.2 %collective-permute-start.33 = (bf16[1280,784]{0,1:T(8,128)(2,1)}, bf16[1280,784]{0,1:T(8,128)(2,1)S(1)}, u32[]{:S(2)}, u32[]{:S(2)}) collective-permute-start(bf16[1280,784]{0,1:T(8,128)(2,1)} %copy.23), channel_id=1, source_target_pairs={{0,16},{16,0},{1,17},{17,1},{2,18},{18,2},{3,19},{19,3},{4,20},{20... | collective-permute-start | bytes 6021128 | tf_op jit(solution)/shard_map/ppermute | solution.py:561
  356.8 33.9 %collective-permute-start.32 = (bf16[320,784]{1,0:T(8,128)(2,1)S(1)}, bf16[320,784]{1,0:T(8,128)(2,1)S(1)}, u32[]{:S(2)}, u32[]{:S(2)}) collective-permute-start(bf16[320,784]{1,0:T(8,128)(2,1)S(1)} %multiply_convert_fusion.refs_0_), channel_id=1, source_target_pairs={{0,3},{1,2},{2,1},{3,0},{4,7},{5,6},{6,5},{7,4},{8,11},{9,10},{10,... | collective-permute-start | bytes 1505288 | tf_op jit(solution)/shard_map/ppermute | solution.py:571
  359.0 51.9 %collective-permute-start.31 = (bf16[320,784]{1,0:T(8,128)(2,1)S(1)}, bf16[320,784]{1,0:T(8,128)(2,1)}, u32[]{:S(2)}, u32[]{:S(2)}) collective-permute-start(bf16[320,784]{1,0:T(8,128)(2,1)S(1)} %multiply_convert_fusion.refs_0_), channel_id=1, source_target_pairs={{0,2},{1,3},{2,0},{3,1},{4,6},{5,7},{6,4},{7,5},{8,10},{9,11},{10,... | collective-permute-start | bytes 1505288 | tf_op jit(solution)/shard_map/ppermute | solution.py:571
  364.9 46.0 %collective-permute-start.30 = (bf16[320,784]{1,0:T(8,128)(2,1)S(1)}, bf16[320,784]{1,0:T(8,128)(2,1)}, u32[]{:S(2)}, u32[]{:S(2)}) collective-permute-start(bf16[320,784]{1,0:T(8,128)(2,1)S(1)} %multiply_convert_fusion.refs_0_), channel_id=1, source_target_pairs={{0,1},{1,0},{2,3},{3,2},{4,5},{5,4},{6,7},{7,6},{8,9},{9,8},{10,11... | collective-permute-start | bytes 1505288 | tf_op jit(solution)/shard_map/ppermute | solution.py:571
  390.6 20.3 %copy-start.41 = (bf16[320,784]{1,0:T(8,128)(2,1)}, bf16[320,784]{1,0:T(8,128)(2,1)S(1)}, u32[]{:S(2)}) copy-start(bf16[320,784]{1,0:T(8,128)(2,1)S(1)} %collective-permute-done.32.refs_3_) | copy-start | bytes 1505284
  421.1 7.3 %collective-permute-start.38 = (bf16[1280,784]{0,1:T(8,128)(2,1)}, bf16[1280,784]{0,1:T(8,128)(2,1)S(1)}, u32[]{:S(2)}, u32[]{:S(2)}) collective-permute-start(bf16[1280,784]{0,1:T(8,128)(2,1)} %copy.26), channel_id=1, source_target_pairs={{0,16},{16,0},{1,17},{17,1},{2,18},{18,2},{3,19},{19,3},{4,20},{20... | collective-permute-start | bytes 6021128 | tf_op jit(solution)/shard_map/ppermute | solution.py:561
  422.9 3.9 collective-permute-start.37
  423.3 16.8 %collective-permute-start.34 = (bf16[160,784]{1,0:T(8,128)(2,1)}, bf16[160,784]{1,0:T(8,128)(2,1)S(1)}, u32[]{:S(2)}, u32[]{:S(2)}) collective-permute-start(bf16[160,784]{1,0:T(8,128)(2,1)} %get-tuple-element.183), channel_id=1, source_target_pairs={{0,4},{4,0},{8,12},{12,8},{1,5},{5,1},{9,13},{13,9},{2,6},{6,2},{1... | collective-permute-start | bytes 752648 | tf_op jit(solution)/shard_map/ppermute | solution.py:571
  424.4 15.7 %collective-permute-start.35 = (bf16[160,784]{1,0:T(8,128)(2,1)}, bf16[160,784]{1,0:T(8,128)(2,1)}, u32[]{:S(2)}, u32[]{:S(2)}) collective-permute-start(bf16[160,784]{1,0:T(8,128)(2,1)} %get-tuple-element.184), channel_id=1, source_target_pairs={{0,8},{4,12},{8,0},{12,4},{1,9},{5,13},{9,1},{13,5},{2,10},{6,14},... | collective-permute-start | bytes 752648 | tf_op jit(solution)/shard_map/ppermute | solution.py:571
  425.3 14.7 %collective-permute-start.36 = (bf16[160,784]{1,0:T(8,128)(2,1)}, bf16[160,784]{1,0:T(8,128)(2,1)}, u32[]{:S(2)}, u32[]{:S(2)}) collective-permute-start(bf16[160,784]{1,0:T(8,128)(2,1)} %get-tuple-element.185), channel_id=1, source_target_pairs={{0,12},{4,8},{8,4},{12,0},{1,13},{5,9},{9,5},{13,1},{2,14},{6,10},... | collective-permute-start | bytes 752648 | tf_op jit(solution)/shard_map/ppermute | solution.py:571
  456.7 16.0 %copy-start.4 = (bf16[640,784]{1,0:T(8,128)(2,1)S(1)}, bf16[640,784]{1,0:T(8,128)(2,1)}, u32[]{:S(2)}) copy-start(bf16[640,784]{1,0:T(8,128)(2,1)} %all_gather.19.m_ref.ma_ref) | copy-start | bytes 3010564
  474.3 6.0 %collective-permute-start.43 = (bf16[640,784]{0,1:T(8,128)(2,1)}, bf16[640,784]{0,1:T(8,128)(2,1)S(1)}, u32[]{:S(2)}, u32[]{:S(2)}) collective-permute-start(bf16[640,784]{0,1:T(8,128)(2,1)} %copy.30), channel_id=1, source_target_pairs={{0,16},{16,0},{1,17},{17,1},{2,18},{18,2},{3,19},{19,3},{4,20},{20... | collective-permute-start | bytes 3010568 | tf_op jit(solution)/shard_map/ppermute | solution.py:561
  475.4 6.6 %collective-permute-start.42 = (bf16[640,784]{0,1:T(8,128)(2,1)S(1)}, bf16[640,784]{0,1:T(8,128)(2,1)S(1)}, u32[]{:S(2)}, u32[]{:S(2)}) collective-permute-start(bf16[640,784]{0,1:T(8,128)(2,1)S(1)} %copy.29), channel_id=1, source_target_pairs={{0,16},{16,0},{1,17},{17,1},{2,18},{18,2},{3,19},{19,3},{4,20},{20... | collective-permute-start | bytes 3010568 | tf_op jit(solution)/shard_map/ppermute | solution.py:561
  476.0 33.2 %collective-permute-start.39 = (bf16[160,784]{1,0:T(8,128)(2,1)}, bf16[160,784]{1,0:T(8,128)(2,1)S(1)}, u32[]{:S(2)}, u32[]{:S(2)}) collective-permute-start(bf16[160,784]{1,0:T(8,128)(2,1)} %get-tuple-element.197), channel_id=1, source_target_pairs={{0,1},{1,0},{2,3},{3,2},{4,5},{5,4},{6,7},{7,6},{8,9},{9,8},{10,11... | collective-permute-start | bytes 752648 | tf_op jit(solution)/shard_map/ppermute | solution.py:571
  476.0 33.2 %collective-permute-start.40 = (bf16[160,784]{1,0:T(8,128)(2,1)}, bf16[160,784]{1,0:T(8,128)(2,1)}, u32[]{:S(2)}, u32[]{:S(2)}) collective-permute-start(bf16[160,784]{1,0:T(8,128)(2,1)} %get-tuple-element.198), channel_id=1, source_target_pairs={{0,2},{1,3},{2,0},{3,1},{4,6},{5,7},{6,4},{7,5},{8,10},{9,11},{10,... | collective-permute-start | bytes 752648 | tf_op jit(solution)/shard_map/ppermute | solution.py:571
  478.9 30.3 %collective-permute-start.41 = (bf16[160,784]{1,0:T(8,128)(2,1)}, bf16[160,784]{1,0:T(8,128)(2,1)}, u32[]{:S(2)}, u32[]{:S(2)}) collective-permute-start(bf16[160,784]{1,0:T(8,128)(2,1)} %get-tuple-element.199), channel_id=1, source_target_pairs={{0,3},{1,2},{2,1},{3,0},{4,7},{5,6},{6,5},{7,4},{8,11},{9,10},{10,... | collective-permute-start | bytes 752648 | tf_op jit(solution)/shard_map/ppermute | solution.py:571
  483.7 25.5 %copy-start.37 = (bf16[160,784]{1,0:T(8,128)(2,1)S(1)}, bf16[160,784]{1,0:T(8,128)(2,1)}, u32[]{:S(2)}) copy-start(bf16[160,784]{1,0:T(8,128)(2,1)} %get-tuple-element.202) | copy-start | bytes 752644
  (22 other events, 132.6 us)

commit v2 on v1

--- a/solution.py
+++ b/solution.py
@@ -44,16 +44,15 @@
 
 
 def fill_columns(planes, image, side):
-    rows, pixels = image.shape
-    wide = planes.shape[2]
-    column = lax.broadcasted_iota(jnp.int32, (rows, pixels), 1) % side
+    column = lax.broadcasted_iota(jnp.int32, image.shape, 1) % side
     zero = jnp.zeros_like(image)
-    planes[0, :, :pixels] = jnp.where(column == side - 1, zero, image)
-    planes[1, :, :pixels] = image
-    planes[2, :, :pixels] = jnp.where(column == 0, zero, image)
-    if wide > pixels:
+    span = image.shape[1]
+    planes[0, :, :span] = jnp.where(column == side - 1, zero, image)
+    planes[1, :, :span] = image
+    planes[2, :, :span] = jnp.where(column == 0, zero, image)
+    if planes.shape[2] > span:
         for k in range(3):
-            planes[k, :, pixels:] = jnp.zeros((rows, wide - pixels), image.dtype)
+            planes[k, :, span:] = jnp.zeros((image.shape[0], planes.shape[2] - span), image.dtype)
 
 
 def read_shifted(planes, dy, dx, side):
@@ -100,15 +99,26 @@
     return pl.ds(pl.multiple_of(index * size, 8), size)
 
 
-def write_chunks(outs, total, me, n):
-    size = outs[0].shape[0]
+def write_chunks(outs, total, me, n, start=0):
+    size, width = outs[0].shape
     for k in range(n):
         rows = rows_at(partner(me, k, n), size)
-        outs[k][...] = total[rows, : outs[k].shape[1]].astype(BF16)
+        outs[k][...] = total[rows, start : start + width].astype(BF16)
+
+
+def spans(wide):
+    first = wide // 256 * 128
+    return ((0, first), (first, wide))
+
+
+def stack_row(windows, planes, dy, step, side):
+    depth = planes.shape[1]
+    for k in range(3):
+        windows[k * depth : (k + 1) * depth, :] = read_shifted(planes, dy, step * (k - 1), side)
 
 
 def conv_forward_body(x_ref, w_ref, *rest, side, n):
-    outs, (planes, total) = rest[:n], rest[n:]
+    outs, (planes, windows, total) = rest[:-3], rest[-3:]
     t = pl.program_id(0)
     me = lax.axis_index("cin")
 
@@ -117,110 +127,118 @@
         fill_columns(planes, x_ref[...], side)
         total[...] = jnp.zeros_like(total)
 
-    window = read_shifted(planes, t // 3 - 1, t % 3 - 1, side)
-    total[...] += dot(w_ref[0], window, TN)
-
-    @pl.when(t == TAPS - 1)
+    stack_row(windows, planes, t - 1, 1, side)
+    total[...] += dot(w_ref[...].reshape(windows.shape[0], w_ref.shape[2]), windows[...], TN)
+
+    @pl.when(t == 2)
     def _():
-        write_chunks(outs, total, me, n)
+        pixel = lax.broadcasted_iota(jnp.int32, total.shape, 1)
+        total[...] = jnp.where(pixel < side * side, total[...], 0.0)
+        for j, (start, _) in enumerate(spans(total.shape[1])):
+            write_chunks(outs[j * n : (j + 1) * n], total, me, n, start)
 
 
 def conv_forward(x, kernel, side, n):
     depth, pixels = x.shape
+    wide = lanes_of(pixels + side + 1)
     width = kernel.shape[2]
-    wide = lanes_of(pixels + side + 1)
-    return pl.pallas_call(
+    parts = [(width // n, stop - start) for start, stop in spans(wide) for _ in range(n)]
+    outs = pl.pallas_call(
         functools.partial(conv_forward_body, side=side, n=n),
-        out_shape=[like((width // n, pixels))] * n,
-        grid=(TAPS,),
+        out_shape=[like(part) for part in parts],
+        grid=(3,),
         in_specs=[
             whole((depth, pixels)),
-            pl.BlockSpec((1, depth, width), lambda t: (t, 0, 0)),
+            pl.BlockSpec((3, depth, width), lambda t: (t, 0, 0)),
         ],
-        out_specs=[whole((width // n, pixels))] * n,
+        out_specs=[whole(part) for part in parts],
         scratch_shapes=[
             pltpu.VMEM((3, depth, wide), BF16),
+            pltpu.VMEM((3 * depth, wide), BF16),
             pltpu.VMEM((width, wide), F32),
         ],
         compiler_params=params(),
-        cost_estimate=cost(2 * TAPS * depth * width * pixels, 2 * kernel.size + 4 * x.size),
+        cost_estimate=cost(2 * TAPS * depth * width * wide, 2 * kernel.size + 4 * x.size),
     )(x, kernel)
-
-
-def conv_back_body(m_ref, w_ref, *rest, side, n):
-    outs, (planes, total) = rest[:n], rest[n:]
+    return outs[:n], outs[n:]
+
+
+def conv_back_body(m_ref, w_ref, *refs, side, n):
+    outs, padded, (planes, total) = refs[:n], refs[n], refs[n + 1 :]
     t = pl.program_id(0)
     me = lax.axis_index("cout")
 
     @pl.when(t == 0)
     def _():
         fill_columns(planes, m_ref[...], side)
+        padded[...] = planes[1]
         total[...] = jnp.zeros_like(total)
 
-    window = read_shifted(planes, 1 - t // 3, 1 - t % 3, side)
-    total[...] += dot(w_ref[0], window, NN)
-
-    @pl.when(t == TAPS - 1)
+    term = None
+    for k in range(3):
+        part = dot(w_ref[k], read_shifted(planes, 1 - t, 1 - k, side), NN)
+        term = part if term is None else term + part
+    total[...] += term
+
+    @pl.when(t == 2)
     def _():
         write_chunks(outs, total, me, n)
 
 
 def conv_back(m, kernel, side, n):
     width, pixels = m.shape
+    wide = lanes_of(pixels + side + 1)
     depth = kernel.shape[1]
-    wide = lanes_of(pixels + side + 1)
-    return pl.pallas_call(
+    outs = pl.pallas_call(
         functools.partial(conv_back_body, side=side, n=n),
-        out_shape=[like((depth // n, pixels))] * n,
-        grid=(TAPS,),
+        out_shape=[like((depth // n, pixels))] * n + [like((width, wide))],
+        grid=(3,),
         in_specs=[
             whole((width, pixels)),
-            pl.BlockSpec((1, depth, width), lambda t: (t, 0, 0)),
+            pl.BlockSpec((3, depth, width), lambda t: (t, 0, 0)),
         ],
-        out_specs=[whole((depth // n, pixels))] * n,
+        out_specs=[whole((depth // n, pixels))] * n + [whole((width, wide))],
         scratch_shapes=[
             pltpu.VMEM((3, width, wide), BF16),
             pltpu.VMEM((depth, wide), F32),
         ],
         compiler_params=params(),
-        cost_estimate=cost(2 * TAPS * depth * width * pixels, 2 * kernel.size + 4 * m.size),
+        cost_estimate=cost(2 * TAPS * depth * width * wide, 2 * kernel.size + 4 * width * wide),
     )(m, kernel)
-
-
-def conv_weight_body(xa_ref, xb_ref, ma_ref, mb_ref, o_ref, pa, pb, ga, gb, *, side):
+    return outs[:n], outs[n]
+
+
+def conv_weight_body(xa_ref, xb_ref, ma_ref, mb_ref, o_ref, pa, pb, both, *, side):
     t = pl.program_id(0)
-    pixels = ma_ref.shape[1]
+    wide = pa.shape[2]
 
     @pl.when(t == 0)
     def _():
         fill_columns(pa, xa_ref[...], side)
         fill_columns(pb, xb_ref[...], side)
-        ga[...] = jnp.zeros_like(ga)
-        gb[...] = jnp.zeros_like(gb)
-        ga[:, :pixels] = ma_ref[...]
-        gb[:, :pixels] = mb_ref[...]
+        both[:, :wide] = ma_ref[...]
+        both[:, wide:] = mb_ref[...]
 
     dy, dx = t // 3 - 1, t % 3 - 1
-    o_ref[0] = dot(read_shifted(pa, dy, dx, side), ga[...], NT) + dot(
-        read_shifted(pb, dy, dx, side), gb[...], NT
-    )
+    window = jnp.concatenate(
+        [read_shifted(pa, dy, dx, side), read_shifted(pb, dy, dx, side)], axis=1
+    )
+    o_ref[0] = dot(window, both[...], NT)
 
 
 def conv_weight(xa, xb, ma, mb, side):
     depth, pixels = xa.shape
-    width = ma.shape[0]
-    wide = lanes_of(pixels + side + 1)
+    width, wide = ma.shape
     return pl.pallas_call(
         functools.partial(conv_weight_body, side=side),
-        out_shape=jax.ShapeDtypeStruct((TAPS, depth, width), F32),
+        out_shape=like((TAPS, depth, width), F32),
         grid=(TAPS,),
-        in_specs=[pl.BlockSpec((depth, pixels), lambda t: (0, 0))] * 2
-        + [pl.BlockSpec((width, pixels), lambda t: (0, 0))] * 2,
+        in_specs=[whole((depth, pixels))] * 2 + [whole((width, wide))] * 2,
         out_specs=pl.BlockSpec((1, depth, width), lambda t: (t, 0, 0)),
         scratch_shapes=[pltpu.VMEM((3, depth, wide), BF16)] * 2
-        + [pltpu.VMEM((width, wide), BF16)] * 2,
+        + [pltpu.VMEM((width, 2 * wide), BF16)],
         compiler_params=params(),
-        cost_estimate=cost(4 * TAPS * depth * width * pixels, 4 * TAPS * depth * width),
+        cost_estimate=cost(4 * TAPS * depth * width * wide, 4 * TAPS * depth * width),
     )(xa, xb, ma, mb)
 
 
@@ -284,7 +302,7 @@
     count, width, small = cots.shape
     depth = kernel.shape[1]
     wide = lanes_of(small + side // 2 + 1)
-    pixels = side * side
+    pixels = lanes_of(side * side + side + 1)
     out = (count * depth // 2, pixels)
     return pl.pallas_call(
         functools.partial(half_back_body, side=side),
@@ -305,11 +323,12 @@
     )(cots, kernel)
 
 
-def half_weight_body(a_ref, b_ref, g_ref, o_ref, moved, planes, *, side):
+def half_weight_body(*refs, side):
+    mine, other, g_ref, o_ref, (moved, planes) = refs[0:2], refs[2:4], refs[4], refs[5], refs[6:]
     t = pl.program_id(0)
     count = g_ref.shape[0]
-    half = a_ref.shape[0] // count
-    pixels = a_ref.shape[1]
+    half = mine[0].shape[0] // count
+    pixels = sum(ref.shape[1] for ref in mine)
     wide = moved.shape[2] // count
     core = lax.axis_index("section")
 
@@ -318,11 +337,14 @@
         fill_moved(moved, g_ref[...], side // 2)
         for k in range(4):
             pick = chosen(k, wide, pixels, side)
-            for ref, place in ((a_ref, core), (b_ref, 1 - core)):
+            for pair, place in ((mine, core), (other, 1 - core)):
                 for b in range(count):
-                    planes[k, rows_at(place, half), b * wide : (b + 1) * wide] = dot(
-                        ref[b * half : (b + 1) * half, :], pick, NT
-                    ).astype(BF16)
+                    rows = slice(b * half, (b + 1) * half)
+                    plane = None
+                    for ref, (start, stop) in zip(pair, spans(pixels)):
+                        term = dot(ref[rows, :], pick[:, start:stop], NT)
+                        plane = term if plane is None else plane + term
+                    planes[k, rows_at(place, half), b * wide : (b + 1) * wide] = plane.astype(BF16)
 
     ty, tx = t // 3, t % 3
     plane = jnp.where(ty == 1, 0, 2) + jnp.where(tx == 1, 0, 1)
@@ -332,18 +354,13 @@
 
 def half_weight(mine, other, cots, side):
     count, width, small = cots.shape
-    rows, pixels = mine.shape
-    depth = 2 * rows // count
+    depth = 2 * mine[0].shape[0] // count
     wide = lanes_of(small + side // 2 + 1)
     return pl.pallas_call(
         functools.partial(half_weight_body, side=side),
         out_shape=like((TAPS, depth, width), F32),
         grid=(TAPS,),
-        in_specs=[
-            whole((rows, pixels)),
-            whole((rows, pixels)),
-            whole((count, width, small)),
-        ],
+        in_specs=[whole(v.shape) for v in (*mine, *other, cots)],
         out_specs=pl.BlockSpec((1, depth, width), lambda t: (t, 0, 0)),
         scratch_shapes=[
             pltpu.VMEM((4, width, count * wide), BF16),
@@ -353,7 +370,7 @@
         cost_estimate=cost(
             2 * TAPS * depth * width * count * small * 2, 4 * TAPS * depth * width
         ),
-    )(mine, other, cots)
+    )(*mine, *other, cots)
 
 
 def expand(first_block, weight, n):
@@ -471,20 +488,21 @@
 
 
 def place_halves(masked, mine, other, core):
-    half = mine[0].shape[0]
+    half = mine.shape[0] // 2
     for image in range(2):
-        masked[image, rows_at(core, half), :] = mine[image][...]
-        masked[image, rows_at(1 - core, half), :] = other[image][...]
+        rows = slice(image * half, (image + 1) * half)
+        masked[image, rows_at(core, half), :] = mine[rows, :]
+        masked[image, rows_at(1 - core, half), :] = other[rows, :]
 
 
 def reduce_back(mine, other, weight, n):
     depth, width = weight.shape
-    pixels = mine[0].shape[1]
+    pixels = mine.shape[1]
     size = depth // (n // 2)
 
     def body(*refs):
-        a, b, w_ref = refs[0:2], refs[2:4], refs[4]
-        outs, masked = refs[5 : 5 + n], refs[5 + n]
+        a, b, w_ref = refs[:3]
+        outs, masked = refs[3 : 3 + n], refs[3 + n]
         core, z = lax.axis_index("section"), lax.axis_index("cout")
         place_halves(masked, a, b, core)
         for r in range(n):
@@ -493,7 +511,7 @@
 
     return one_step(
         body,
-        [*mine, *other, weight],
+        [mine, other, weight],
         [like((size, pixels))] * n,
         [pltpu.VMEM((2, width, pixels), BF16)],
         4 * depth * width * pixels,
@@ -501,19 +519,24 @@
 
 
 def reduce_weight_gradient(joined, mine, other):
-    _, depth, pixels = joined.shape
-    width = 2 * mine[0].shape[0]
-
-    def body(j_ref, *refs):
-        a, b, out, masked = refs[0:2], refs[2:4], refs[4], refs[5]
-        place_halves(masked, a, b, lax.axis_index("section"))
-        out[...] = dot(j_ref[0], masked[0], NT) + dot(j_ref[1], masked[1], NT)
+    _, depth, _ = joined[0].shape
+    width = mine[0].shape[0]
+    pixels = sum(v.shape[1] for v in mine)
+
+    def body(*refs):
+        js, a, b, out = refs[0:2], refs[2:4], refs[4:6], refs[6]
+        core = lax.axis_index("section")
+        for j in range(2):
+            masked = refs[7 + j]
+            place_halves(masked, a[j], b[j], core)
+            term = dot(js[j][0], masked[0], NT) + dot(js[j][1], masked[1], NT)
+            out[...] = term if j == 0 else out[...] + term
 
     return one_step(
         body,
-        [joined, *mine, *other],
+        [*joined, *mine, *other],
         [like((depth, width), F32)],
-        [pltpu.VMEM((2, width, pixels), BF16)],
+        [pltpu.VMEM((2, width, v.shape[1]), BF16) for v in mine],
         4 * depth * width * pixels,
     )[0]
 
@@ -541,15 +564,22 @@
     return outs[:m], outs[m]
 
 
-def outer_pair(a, b, c, d):
-    depth, pixels = a.shape
-    width = b.shape[0]
-
-    def body(a_ref, b_ref, c_ref, d_ref, out):
-        out[...] = dot(a_ref[...], b_ref[...], NT) + dot(c_ref[...], d_ref[...], NT)
+def outer_sum(lefts, rights):
+    depth, width = lefts[0].shape[0], rights[0].shape[0]
+    count = len(lefts)
+
+    def body(*refs):
+        a, b, out = refs[:count], refs[count : 2 * count], refs[2 * count]
+        for j in range(count):
+            term = dot(a[j][...], b[j][...], NT)
+            out[...] = term if j == 0 else out[...] + term
 
     return one_step(
-        body, [a, b, c, d], [like((depth, width), F32)], [], 4 * depth * width * pixels
+        body,
+        [*lefts, *rights],
+        [like((depth, width), F32)],
+        [],
+        2 * width * sum(v.size for v in lefts),
     )[0]
 
 
@@ -561,8 +591,8 @@
     return lax.ppermute(value, "section", [(0, 1), (1, 0)])
 
 
-def hold(*groups):
-    return lax.optimization_barrier(groups)
+def after(value, *earlier):
+    return lax.optimization_barrier((value, earlier))[0]
 
 
 def exchange(parts, name):
@@ -604,7 +634,7 @@
     return lax.all_gather(shard, name, axis=0, tiled=True)
 
 
-def shards(
+def both_blocks(
     inner_features,
     block_input,
     first_kernel,
@@ -614,73 +644,107 @@
     output_grad,
 ):
     m, n = axis_size("cin"), axis_size("cout")
-    features = turn(inner_features)[0]
-    skip = turn(block_input)[0]
+    pixels = SIDE * SIDE
+    wide = lanes_of(pixels + SIDE + 1)
+    cuts = spans(wide)
+    skip = jnp.pad(turn(block_input)[0], ((0, 0), (0, wide - pixels)))
     cots = turn(output_grad)
 
-    feature_block = gather(features, "cout")
-    feature_block, cots = hold(feature_block, cots)
-    cot_block = collect(cots, "cout", 1)
-    first_parts = exchange(conv_forward(feature_block, first_kernel, SIDE, m), "cin")
-    first_hidden = add_up(first_parts)
-    first_act = smooth_gate(first_hidden).astype(BF16)
-    first_block = gather(first_act, "cin")
-
-    expand_parts = expand(first_block, expand_weight, n)
-    expand_parts, cot_block = hold(expand_parts, cot_block)
-    expand_got = exchange(expand_parts, "cout")
-    back_kept, back_sent = half_back(cot_block, stride_kernel, SIDE)
-    expand_got, back_kept, back_sent = hold(expand_got, back_kept, back_sent)
-    joined_pre = skip.astype(F32) + add_up(expand_got)
-    joined = smooth_gate(joined_pre).astype(BF16)
-
-    joined_parts = [round_send(joined, r, n) for r in range(n)]
-    back_parts = add_halves(back_kept, swap(back_sent), m)
+    feature_block = gather(turn(inner_features)[0], "cout")
+    first_parts = conv_forward(feature_block, first_kernel, SIDE, m)
+    cot_block = collect(after(cots, first_parts), "cout", 1)
+    first_got = []
+    for j in range(2):
+        first_got.append(exchange(first_parts[j], "cin"))
+
+    hidden, first_block, expand_got = [], [], []
+    ready = None
+    for j in range(2):
+        got = first_got[j] if j == 0 else after(first_got[j], ready)
+        hidden.append(add_up(got))
+        act = smooth_gate(hidden[j]).astype(BF16)
+        first_block.append(gather(act, "cin"))
+        ready = expand(first_block[j], expand_weight, n)
+        expand_got.append(exchange(ready, "cout"))
+
+    back_kept, back_sent = half_back(after(cot_block, ready), stride_kernel, SIDE)
+    feature_other = swap(after(feature_block, ready))
+    first_other = [swap(after(v, ready)) for v in first_block]
+
+    joined_pre, joined_got = [], []
+    for j in range(2):
+        start, stop = cuts[j]
+        got = after(expand_got[j], back_kept)
+        joined_pre.append(skip[:, start:stop].astype(F32) + add_up(got))
+        joined = smooth_gate(joined_pre[j]).astype(BF16)
+        joined_got.append([round_send(joined, r, n) for r in range(n)])
+    back_other = swap(back_sent)
+    back_parts = add_halves(back_kept, back_other, m)
     back_got = exchange(back_parts, "cin")
-    joined_parts, back_got = hold(joined_parts, back_got)
+
+    joined_two, hidden_got = [], []
+    for j in range(2):
+        got = after(joined_got[j], back_parts)
+        if j > 0:
+            got = after(got, parts, feature_other, first_other)
+        two, kept, sent = reduce_forward(got, reduce_weight, n)
+        joined_two.append(two)
+        other_sent = swap(sent)
+        parts = add_halves(kept, other_sent, m)
+        hidden_got.append(exchange(parts, "cin"))
     back_piece = add_up(back_got)
-    joined_two, hidden_kept, hidden_sent = reduce_forward(joined_parts, reduce_weight, n)
-    hidden_parts = add_halves(hidden_kept, swap(hidden_sent), m)
-    hidden_piece = add_up(exchange(hidden_parts, "cin"))
-    act_piece = smooth_gate(hidden_piece).astype(BF16)
-    masked_piece = (back_piece * gate_slope(hidden_piece)).astype(BF16)
-
-    size = masked_piece.shape[0] // 2
-    masked_mine = [gather(masked_piece[i * size : (i + 1) * size], "cin") for i in range(2)]
-    masked_other = [swap(v) for v in masked_mine]
-    back_rounds = reduce_back(masked_mine, masked_other, reduce_weight, n)
-    back_rounds, act_piece, joined_two = hold(back_rounds, act_piece, joined_two)
-    back_got = [round_send(back_rounds[r], r, n, True) for r in range(n)]
-    act_parts = spread(act_piece, "cin")
-    reduce_gradient = reduce_weight_gradient(joined_two, masked_mine, masked_other)
-    back_got, act_parts, reduce_gradient = hold(back_got, act_parts, reduce_gradient)
-    back_joined = add_up(back_got)
-    input_gradient = (back_joined * gate_slope(joined_pre)).astype(BF16)
-
-    act_parts, input_gradient = hold(act_parts, input_gradient)
-    input_parts = spread(input_gradient, "cout")
-    act_mine = join_pieces(act_parts, m)
-    stride_gradient = half_weight(act_mine, swap(act_mine), cot_block, SIDE)
-    input_parts, stride_gradient = hold(input_parts, stride_gradient)
-
-    first_back, input_wide = expand_back(input_parts, expand_weight, m, n)
-    first_back, input_wide, first_block = hold(first_back, input_wide, first_block)
-    first_got = exchange(first_back, "cin")
-    expand_gradient = outer_pair(first_block, input_wide, swap(first_block), swap(input_wide))
-    first_got, expand_gradient = hold(first_got, expand_gradient)
-    masked_first = (add_up(first_got) * gate_slope(first_hidden)).astype(BF16)
-    masked_block = gather(masked_first, "cin")
-    inner_parts = conv_back(masked_block, first_kernel, SIDE, n)
-    inner_parts, masked_block, feature_block = hold(inner_parts, masked_block, feature_block)
+    act_piece, mine, other, round_got = [], [], [], []
+    for j in range(2):
+        start, stop = cuts[j]
+        got = hidden_got[j] if j == 0 else after(hidden_got[j], ready)
+        piece = add_up(got)
+        act_piece.append(smooth_gate(piece).astype(BF16))
+        masked = (back_piece[:, start:stop] * gate_slope(piece)).astype(BF16)
+        mask_got = spread(masked, "cin")
+        if j == 0:
+            mask_got = after(mask_got, parts)
+        mine.append(join_pieces(mask_got, m))
+        other.append(swap(mine[j]))
+        ready = reduce_back(mine[j], other[j], reduce_weight, n)
+        round_got.append([round_send(ready[r], r, n, True) for r in range(n)])
+    act_got = [spread(v, "cin") for v in after(act_piece, ready)]
+
+    input_gradient, input_got = [], []
+    for j in range(2):
+        slope = gate_slope(joined_pre[j])
+        got = after(round_got[0], ready) if j == 0 else after(round_got[1], act_mine)
+        input_gradient.append((add_up(got) * slope).astype(BF16))
+        input_got.append(spread(input_gradient[j], "cout"))
+        if j > 0:
+            break
+        reduce_gradient = reduce_weight_gradient(after(joined_two, input_gradient[0]), mine, other)
+        act_got = after(act_got, reduce_gradient)
+        act_mine = [join_pieces(v, m) for v in act_got]
+    act_other = [swap(v) for v in act_mine]
+    stride_gradient = half_weight(act_mine, act_other, cot_block, SIDE)
+
+    input_wide, back_got = [], []
+    for j in range(2):
+        got = after(input_got[j], stride_gradient, *input_wide)
+        parts, block = expand_back(got, expand_weight, m, n)
+        input_wide.append(block)
+        back_got.append(exchange(parts, "cin"))
+    input_other = [swap(v) for v in after(input_wide, parts)]
+    expand_gradient = outer_sum([*first_block, *first_other], [*input_wide, *input_other])
+    masked_first = []
+    for j in range(2):
+        got = after(back_got[j], expand_gradient)
+        masked_first.append((add_up(got) * gate_slope(hidden[j])).astype(BF16))
+    masked_block = gather(jnp.concatenate(masked_first, axis=1)[:, :pixels], "cin")
+    inner_parts, padded = conv_back(masked_block, first_kernel, SIDE, n)
     inner_got = exchange(inner_parts, "cout")
-    first_gradient = conv_weight(
-        feature_block, swap(feature_block), masked_block, swap(masked_block), SIDE
-    )
-    inner_got, first_gradient = hold(inner_got, first_gradient)
-    inner_gradient = add_up(inner_got)
+    padded_other = swap(padded)
+    first_gradient = conv_weight(feature_block, feature_other, padded, padded_other, SIDE)
+    inner_gradient = add_up(after(inner_got, first_gradient))
+    outward = jnp.concatenate(input_gradient, axis=1)[:, :pixels]
     return (
         turn(inner_gradient[None]),
-        turn(input_gradient[None]),
+        turn(outward[None]),
         first_gradient,
         expand_gradient,
         reduce_gradient,
@@ -690,7 +754,7 @@
 
 def solution(mesh):
     return jax.shard_map(
-        shards,
+        both_blocks,
         mesh=mesh,
         in_specs=(
             P("section", None, ("cin", "cout")),

time: 517 us -> 564 us (1.091)
  starting transfers between devices: 78.7 us -> 160 us
  local copies, waits for them, and re-layouts: 51 us -> 16.1 us
  blocking collectives: 84.8 us -> 62.3 us
  Pallas kernels: 165 us -> 177 us
  waiting for transfers between devices: 122 us -> 132 us
    ppermute x24 -> x48, starting transfers between devices: 33.2 us -> 78.8 us  [exchange(): lax.ppermute(parts[k], name, [(i, partner(i, k, n)) for i in range(n)])]
    ppermute x24 -> x48, waiting for transfers between devices: 76.7 us -> 99.9 us  [exchange(): lax.ppermute(parts[k], name, [(i, partner(i, k, n)) for i in range(n)])]
    all_gather x5 -> x4, blocking collectives: 84.8 us -> 62.3 us  [gather(): return lax.all_gather(shard, name, axis=0, tiled=True)]
    ppermute x9 -> x1, local copies, waits for them, and re-layouts: 23.6 us -> 1.67 us  [swap(): return lax.ppermute(value, 'section', [(0, 1), (1, 0)])]
    ppermute x8 -> x16, starting transfers between devices: 20.5 us -> 39.4 us  [round_send(): return lax.ppermute(value, ('section', 'cout'), round_pairs(r, n, back))]
    ppermute x9 -> x13, starting transfers between devices: 20.6 us -> 37.7 us  [swap(): return lax.ppermute(value, 'section', [(0, 1), (1, 0)])]
    pallas_call x9 -> x17, Pallas kernels: 59.8 us -> 76.5 us  [one_step(): pl.pallas_call(body, out_shape=outs, in_specs=[pl.BlockSpec(memory_space=...]
    optimization_barrier x5 -> x1, local copies, waits for them, and re-layouts: 13 us -> 1.66 us  [after(): return lax.optimization_barrier((value, earlier))[0]]
  transfers between devices with their start and end apart: 44 -> 80, of which waited for: 14 -> 25; matrix products, arithmetic and copies ran while one was open for 5% -> 2% of each run, Pallas kernels for 22% -> 20%
where the time goes in v2:
time: 564 us; the launch traced here: 558 us
  Pallas kernels  177 us (31%)
  starting transfers between devices  160 us (28%)
  waiting for transfers between devices  132 us (23%)
  blocking collectives  62.3 us (11%)
  local copies, waits for them, and re-layouts  16.1 us (3%)
  other arithmetic  7.78 us (1%)
    ppermute x48, waiting for transfers between devices, exchange(): lax.ppermute(parts[k], name, [(i, partner(i, k, n)) for i in range(n)])  99.9 us
    ppermute x48, starting transfers between devices, exchange(): lax.ppermute(parts[k], name, [(i, partner(i, k, n)) for i in range(n)])  78.8 us
    pallas_call x17, Pallas kernels, one_step(): pl.pallas_call(body, out_shape=outs, in_specs=[pl.BlockSpec(memory_space=...  76.5 us
    all_gather x4, blocking collectives, gather(): return lax.all_gather(shard, name, axis=0, tiled=True)  62.3 us
    ppermute x16, starting transfers between devices, round_send(): return lax.ppermute(value, ('section', 'cout'), round_pairs(r, n, back))  39.4 us
    ppermute x13, starting transfers between devices, swap(): return lax.ppermute(value, 'section', [(0, 1), (1, 0)])  37.7 us
    ppermute x16, waiting for transfers between devices, round_send(): return lax.ppermute(value, ('section', 'cout'), round_pairs(r, n, back))  32.4 us
    pallas_call x1, Pallas kernels, conv_weight(): pl.pallas_call(functools.partial(conv_weight_body, side=side), out_shape=...  25.5 us
  transfers between devices with their start and end apart: 80, of which 25 were waited for; matrix products, arithmetic and copies ran while one was open for 2% of the time, Pallas kernels for 20%

profile of v2, /device:TPU:0, one launch (start us, length us, event | category | flops | bytes accessed | tf_op | source)
XLA Modules:
  0.0 557.9 jit_solution(17511364539444447697)
XLA Ops:
  0.6 26.4 %all-gather = bf16[1,640,784]{2,1,0:T(8,128)(2,1)} all-gather(bf16[1,160,784]{2,1,0:T(8,128)(2,1)} %bitcast.21), channel_id=2, replica_groups=mesh['section'=2,'cin'=4,'cout'=4] {'cout'}, dimensions={1}, use_global_device_ids=true | all-gather | bytes 1254400 | tf_op jit(solution)/shard_map/all_gather | solution.py:634
  27.1 14.0 %shard_map.118 = (bf16[160,384]{1,0:T(8,128)(2,1)}, bf16[160,384]{1,0:T(8,128)(2,1)}, bf16[160,384]{1,0:T(8,128)(2,1)}, bf16[160,384]{1,0:T(8,128)(2,1)}, bf16[1...) custom-call(bf16[640,784]{1,0:T(8,128)(2,1)} %bitcast.18, ...), custom_call_target="tpu_custom_call" | custom-call | flops 6606028800 | bytes 9379840 | tf_op jit(solution)/shard_map/pallas_call | solution.py:146
  44.6 2.3 collective-permute-start.2
  47.2 1.9 collective-permute-start
  53.2 10.7 %all_gather.13.x_ref.refs_0_ = bf16[640,384]{1,0:T(8,128)(2,1)} all-gather(bf16[160,384]{1,0:T(8,128)(2,1)S(1)} %multiply_convert_fusion.9), channel_id=1, replica_groups=mesh['section'=2,'cin'=4,'cout'=4] {'cin'}, dimensions={0}, use_global_device_ids=true | all-gather | bytes 614400 | tf_op jit(solution)/shard_map/all_gather | solution.py:634
  63.9 3.8 shard_map.119
  69.5 4.6 collective-permute-done.5
  74.7 10.9 %all_gather.14.x_ref.refs_1_ = bf16[640,512]{1,0:T(8,128)(2,1)} all-gather(bf16[160,512]{1,0:T(8,128)(2,1)S(1)} %multiply_convert_fusion.7), channel_id=1, replica_groups=mesh['section'=2,'cin'=4,'cout'=4] {'cin'}, dimensions={0}, use_global_device_ids=true | all-gather | bytes 819200 | tf_op jit(solution)/shard_map/all_gather | solution.py:634
  85.7 4.0 shard_map.120
  89.8 24.1 %shard_map.121 = (bf16[1280,896]{1,0:T(8,128)(2,1)}, bf16[1280,896]{1,0:T(8,128)(2,1)}) custom-call(bf16[2,640,196]{2,1,0:T(8,128)(2,1)} %copy-done.19, bf16[9,1280,640]{2,1,0:T(8,128)(2,1)} %w_ref.8), custom_call_target="tpu_custom_call" | custom-call | flops 11560550400 | bytes 14745600 | tf_op jit(solution)/shard_map/pallas_call | solution.py:307
  114.0 2.8 collective-permute-start.14
  118.3 9.2 %collective-permute-done.13 = bf16[320,384]{1,0:T(8,128)(2,1)S(1)} collective-permute-done((bf16[320,384]{1,0:T(8,128)(2,1)S(1)}, bf16[320,384]{1,0:T(8,128)(2,1)S(1)}, u32[]{:S(2)}, u32[]{:S(2)}) %collective-permute-start.13) | collective-permute-done | bytes 245792 | tf_op jit(solution)/shard_map/ppermute | solution.py:601
  127.6 6.8 %collective-permute-done.14 = bf16[320,384]{1,0:T(8,128)(2,1)S(1)} collective-permute-done((bf16[320,384]{1,0:T(8,128)(2,1)S(1)}, bf16[320,384]{1,0:T(8,128)(2,1)S(1)}, u32[]{:S(2)}, u32[]{:S(2)}) %collective-permute-start.14) | collective-permute-done | bytes 245792 | tf_op jit(solution)/shard_map/ppermute | solution.py:601
  134.4 2.4 collective-permute-start.29
  139.2 2.0 collective-permute-done.27
  141.2 3.1 collective-permute-start.18
  144.3 21.7 %collective-permute-done.28 = bf16[320,512]{1,0:T(8,128)(2,1)S(1)} collective-permute-done((bf16[320,512]{1,0:T(8,128)(2,1)S(1)}, bf16[320,512]{1,0:T(8,128)(2,1)S(1)}, u32[]{:S(2)}, u32[]{:S(2)}) %collective-permute-start.28) | collective-permute-done | bytes 327712 | tf_op jit(solution)/shard_map/ppermute | solution.py:601
  166.0 3.7 collective-permute-start.16
  171.4 9.6 %collective-permute-start.34 = (bf16[640,784]{0,1:T(8,128)(2,1)}, bf16[640,784]{0,1:T(8,128)(2,1)S(1)}, u32[]{:S(2)}, u32[]{:S(2)}) collective-permute-start(bf16[640,784]{0,1:T(8,128)(2,1)} %copy.13), channel_id=1, source_target_pairs={{0,16},{16,0},{1,17},{17,1},{2,18},{18,2},{3,19},{19,3},{4,20},{20... | collective-permute-start | bytes 3010568 | tf_op jit(solution)/shard_map/ppermute | solution.py:591
  181.0 4.6 shard_map.122
  185.6 6.2 %shard_map.123 = (bf16[2,640,384]{2,1,0:T(8,128)(2,1)}, bf16[1280,384]{1,0:T(8,128)(2,1)}, bf16[1280,384]{1,0:T(8,128)(2,1)}) custom-call(bf16[320,384]{1,0:T(8,128)(2,1)} %collective-permute-done.16.refs_0_, bf16[320,384]{1,0:T(8,128)(2,1)} %collective-permute-done.17.refs_1_, bf16[320,384]{1,0:T(8,128)(2,1)} %collective-permute-done.18.refs_2_, ...), custom_call_target="tpu_custom_call" | custom-call | flops 1258291200 | bytes 5570560 | tf_op jit(solution)/shard_map/pallas_call | solution.py:79
  191.8 2.6 collective-permute-start.20
  194.7 2.5 collective-permute-start.33
  200.7 2.4 collective-permute-done.33.refs_3_
  203.1 3.6 collective-permute-start.36
  206.8 2.5 collective-permute-done.32.refs_2_
  209.3 9.2 %collective-permute-start.35 = (bf16[640,384]{1,0:T(8,128)(2,1)S(1)}, bf16[640,384]{1,0:T(8,128)(2,1)}, u32[]{:S(2)}, u32[]{:S(2)}) collective-permute-start(bf16[640,384]{1,0:T(8,128)(2,1)S(1)} %copy-done.36), channel_id=1, source_target_pairs={{0,16},{16,0},{1,17},{17,1},{2,18},{18,2},{3,19},{19,3},{4,20},{20... | collective-permute-start | bytes 1474568 | tf_op jit(solution)/shard_map/ppermute | solution.py:591
  221.9 2.9 shard_map.124
  226.3 6.8 %shard_map.125 = (bf16[2,640,512]{2,1,0:T(8,128)(2,1)}, bf16[1280,512]{1,0:T(8,128)(2,1)}, bf16[1280,512]{1,0:T(8,128)(2,1)}) custom-call(bf16[320,512]{1,0:T(8,128)(2,1)} %collective-permute-done.30.refs_0_, bf16[320,512]{1,0:T(8,128)(2,1)} %copy-done.73, bf16[320,512]{1,0:T(8,128)(2,1)} %copy-done.71, bf16[320,512]{1,0:T(8,128)(2,1)} %collective-permute-done.33.refs_3_, ...), custom_call_target="tpu_custom_call" | custom-call | flops 1677721600 | bytes 6881280 | tf_op jit(solution)/shard_map/pallas_call | solution.py:79
  233.2 10.5 %collective-permute-start.37 = (bf16[1280,512]{1,0:T(8,128)(2,1)}, bf16[1280,512]{1,0:T(8,128)(2,1)S(1)}, u32[]{:S(2)}, u32[]{:S(2)}) collective-permute-start(bf16[1280,512]{1,0:T(8,128)(2,1)} %get-tuple-element.202), channel_id=1, source_target_pairs={{0,16},{16,0},{1,17},{17,1},{2,18},{18,2},{3,19},{19,3},{4,20},{20... | collective-permute-start | bytes 3932168 | tf_op jit(solution)/shard_map/ppermute | solution.py:591
  248.4 4.2 collective-permute-done.21
  252.7 6.8 %collective-permute-done.22 = bf16[320,384]{1,0:T(8,128)(2,1)S(1)} collective-permute-done((bf16[320,384]{1,0:T(8,128)(2,1)}, bf16[320,384]{1,0:T(8,128)(2,1)S(1)}, u32[]{:S(2)}, u32[]{:S(2)}) %collective-permute-start.22) | collective-permute-done | bytes 245792 | tf_op jit(solution)/shard_map/ppermute | solution.py:601
  264.5 3.2 shard_map.126
  267.7 2.0 collective-permute-done.26.refs_3_
  269.7 4.4 collective-permute-done.25.refs_2_
  274.8 2.4 shard_map.127.refs_0_.refs_2_
  281.8 4.8 shard_map.128
  287.9 7.3 %collective-permute-done.44 = bf16[320,512]{1,0:T(8,128)(2,1)S(1)} collective-permute-done((bf16[320,512]{1,0:T(8,128)(2,1)S(1)}, bf16[320,512]{1,0:T(8,128)(2,1)S(1)}, u32[]{:S(2)}, u32[]{:S(2)}) %collective-permute-start.44) | collective-permute-done | bytes 327712 | tf_op jit(solution)/shard_map/ppermute | solution.py:601
  299.3 8.0 %collective-permute-done.48.refs_3_ = bf16[320,512]{1,0:T(8,128)(2,1)S(1)} collective-permute-done((bf16[320,512]{1,0:T(8,128)(2,1)S(1)}, bf16[320,512]{1,0:T(8,128)(2,1)S(1)}, u32[]{:S(2)}, u32[]{:S(2)}) %collective-permute-start.48) | collective-permute-done | bytes 327712 | tf_op jit(solution)/shard_map/ppermute | solution.py:601
  307.3 5.3 collective-permute-done.47.refs_2_
  314.1 2.5 shard_map.129.refs_0_.refs_3_
  317.5 12.1 %collective-permute-start.41 = (bf16[320,384]{1,0:T(8,128)(2,1)S(1)}, bf16[320,384]{1,0:T(8,128)(2,1)S(1)}, u32[]{:S(2)}, u32[]{:S(2)}) collective-permute-start(bf16[320,384]{1,0:T(8,128)(2,1)S(1)} %copy-done.85), channel_id=1, source_target_pairs={{2,0},{3,1},{16,2},{17,3},{0,16},{1,17},{18,18},{19,19},{6,4},{7,5... | collective-permute-start | bytes 737288 | tf_op jit(solution)/shard_map/ppermute | solution.py:414
  329.7 4.1 collective-permute-start.42
  334.9 5.0 shard_map.130
  347.4 2.3 collective-permute-done.55.refs_3_
  350.6 8.4 %shard_map.131 = f32[640,1280]{1,0:T(8,128)} custom-call(bf16[2,640,384]{2,1,0:T(8,128)(2,1)} %get-tuple-element.231.refs_0_, bf16[2,640,512]{2,1,0:T(8,128)(2,1)} %get-tuple-element.232.refs_1_, bf16[1280,384]{1,0:T(8,128)(2,1)} %shard_map.127.refs_0_.refs_2_, bf16[1280,512]{1,0:T(8,128)(2,1)} %shard_map.129.refs_0_.refs_3_, bf16[1280,384]{1,0:T(8,128)(2,1)} %copy-done.62, ...), custom_call_target="tpu_custom_call" | custom-call | flops 2936012800 | bytes 10158080 | tf_op jit(solution)/shard_map/pallas_call | solution.py:79
  360.8 6.4 %collective-permute-done.53.refs_1_ = bf16[320,384]{1,0:T(8,128)(2,1)S(1)} collective-permute-done((bf16[320,384]{1,0:T(8,128)(2,1)S(1)}, bf16[320,384]{1,0:T(8,128)(2,1)S(1)}, u32[]{:S(2)}, u32[]{:S(2)}) %collective-permute-start.53) | collective-permute-done | bytes 245792 | tf_op jit(solution)/shard_map/ppermute | solution.py:601
  369.2 2.5 shard_map.133.refs_1_
  372.6 2.4 shard_map.132.refs_0_
  376.7 3.1 collective-permute-start.66
  379.8 2.7 collective-permute-start.67
  382.5 8.1 %collective-permute-done.65 = bf16[320,512]{1,0:T(8,128)(2,1)S(1)} collective-permute-done((bf16[320,512]{1,0:T(8,128)(2,1)S(1)}, bf16[320,512]{1,0:T(8,128)(2,1)S(1)}, u32[]{:S(2)}, u32[]{:S(2)}) %collective-permute-start.65) | collective-permute-done | bytes 327712 | tf_op jit(solution)/shard_map/ppermute | solution.py:414
  390.7 18.1 %collective-permute-done.66 = bf16[320,512]{1,0:T(8,128)(2,1)S(1)} collective-permute-done((bf16[320,512]{1,0:T(8,128)(2,1)S(1)}, bf16[320,512]{1,0:T(8,128)(2,1)S(1)}, u32[]{:S(2)}, u32[]{:S(2)}) %collective-permute-start.66) | collective-permute-done | bytes 327712 | tf_op jit(solution)/shard_map/ppermute | solution.py:414
  408.8 12.4 %collective-permute-start.50 = (bf16[320,384]{1,0:T(8,128)(2,1)S(1)}, bf16[320,384]{1,0:T(8,128)(2,1)S(1)}, u32[]{:S(2)}, u32[]{:S(2)}) collective-permute-start(bf16[320,384]{1,0:T(8,128)(2,1)S(1)} %multiply_convert_fusion.4.refs_0_), channel_id=1, source_target_pairs={{0,1},{1,0},{2,3},{3,2},{4,5},{5,4},{6,7},{7,6},{8,9},{9,8},{10,11... | collective-permute-start | bytes 737288 | tf_op jit(solution)/shard_map/ppermute | solution.py:601
  422.3 16.0 %collective-permute-start.69 = (bf16[320,512]{1,0:T(8,128)(2,1)S(1)}, bf16[320,512]{1,0:T(8,128)(2,1)S(1)}, u32[]{:S(2)}, u32[]{:S(2)}) collective-permute-start(bf16[320,512]{1,0:T(8,128)(2,1)S(1)} %multiply_convert_fusion.refs_0_), channel_id=1, source_target_pairs={{0,2},{1,3},{2,0},{3,1},{4,6},{5,7},{6,4},{7,5},{8,10},{9,11},{10,... | collective-permute-start | bytes 983048 | tf_op jit(solution)/shard_map/ppermute | solution.py:601
  439.4 22.9 %shard_map.134 = f32[9,1280,640]{2,1,0:T(8,128)} custom-call(bf16[1280,384]{1,0:T(8,128)(2,1)} %shard_map.132.refs_0_, bf16[1280,512]{1,0:T(8,128)(2,1)} %shard_map.133.refs_1_, bf16[1280,384]{1,0:T(8,128)(2,1)} %copy-done.63, bf16[1280,512]{1,0:T(8,128)(2,1)} %copy-done.59, bf16[2,640,196]{2,1,0:T(8,128)(2,1)} %copy-done.19), custom_call_target="tpu_custom_call" | custom-call | flops 11560550400 | bytes 29491200 | tf_op jit(solution)/shard_map/pallas_call | solution.py:359
  463.7 4.2 shard_map.135
  468.9 4.4 shard_map.136
  477.2 3.8 collective-permute-done.73
  484.7 8.3 %shard_map.137 = f32[640,1280]{1,0:T(8,128)} custom-call(bf16[640,384]{1,0:T(8,128)(2,1)} %all_gather.13.x_ref.refs_0_, bf16[640,512]{1,0:T(8,128)(2,1)} %all_gather.14.x_ref.refs_1_, bf16[640,384]{1,0:T(8,128)(2,1)} %collective-permute-done.35.refs_2_, bf16[640,512]{1,0:T(8,128)(2,1)} %copy-done.66, bf16[1280,384]{1,0:T(8,128)(2,1)} %get-tuple-element.263.refs_4_, ...), custom_call_target="tpu_custom_call" | custom-call | flops 2936012800 | bytes 10158080 | tf_op jit(solution)/shard_map/pallas_call | solution.py:79
  494.3 14.2 %all_gather.15.m_ref = bf16[640,784]{1,0:T(8,128)(2,1)} all-gather(bf16[160,784]{1,0:T(8,128)(2,1)S(1)} %pad_maximum_fusion.1), channel_id=1, replica_groups=mesh['section'=2,'cin'=4,'cout'=4] {'cin'}, dimensions={0}, use_global_device_ids=true | all-gather | bytes 1254400 | tf_op jit(solution)/shard_map/all_gather | solution.py:634
  508.6 14.5 %shard_map.138 = (bf16[160,784]{1,0:T(8,128)(2,1)}, bf16[160,784]{1,0:T(8,128)(2,1)}, bf16[160,784]{1,0:T(8,128)(2,1)}, bf16[160,784]{1,0:T(8,128)(2,1)}, bf16[640,896]{1,0:T(8,128)(2,1)}) custom-call(bf16[640,784]{1,0:T(8,128)(2,1)} %all_gather.15.m_ref, bf16[9,640,640]{2,1,0:T(8,128)(2,1)} %w_ref.9), custom_call_target="tpu_custom_call" | custom-call | flops 6606028800 | bytes 9666560 | tf_op jit(solution)/shard_map/pallas_call | solution.py:192
  527.3 2.8 collective-permute-start.78
  531.2 25.5 %shard_map.139 = f32[9,640,640]{2,1,0:T(8,128)} custom-call(bf16[640,784]{1,0:T(8,128)(2,1)} %bitcast.19, bf16[640,784]{1,0:T(8,128)(2,1)} %copy.14.xb_ref, bf16[640,896]{1,0:T(8,128)(2,1)} %get-tuple-element.277.ma_ref, bf16[640,896]{1,0:T(8,128)(2,1)} %copy-done.61), custom_call_target="tpu_custom_call" | custom-call | flops 13212057600 | bytes 14745600 | tf_op jit(solution)/shard_map/pallas_call | solution.py:232
  (335 shorter events, 82.6 us)
Async XLA Ops:
  44.6 24.8 %collective-permute-start.2 = (bf16[2,160,196]{2,1,0:T(8,128)(2,1)S(1)}, bf16[2,160,196]{2,1,0:T(8,128)(2,1)S(1)}, u32[]{:S(2)}, u32[]{:S(2)}) collective-permute-start(bf16[2,160,196]{2,1,0:T(8,128)(2,1)S(1)} %bitcast.22), channel_id=1, source_target_pairs={{0,3},{1,2},{2,1},{3,0},{4,7},{5,6},{6,5},{7,4},{8,11},{9,10},{10,... | collective-permute-start | bytes 376328 | tf_op jit(solution)/shard_map/ppermute | solution.py:628
  46.8 22.5 %collective-permute-start.1 = (bf16[2,160,196]{2,1,0:T(8,128)(2,1)S(1)}, bf16[2,160,196]{2,1,0:T(8,128)(2,1)S(1)}, u32[]{:S(2)}, u32[]{:S(2)}) collective-permute-start(bf16[2,160,196]{2,1,0:T(8,128)(2,1)S(1)} %bitcast.23), channel_id=1, source_target_pairs={{0,2},{1,3},{2,0},{3,1},{4,6},{5,7},{6,4},{7,5},{8,10},{9,11},{10,... | collective-permute-start | bytes 376328 | tf_op jit(solution)/shard_map/ppermute | solution.py:628
  47.2 20.6 %collective-permute-start = (bf16[2,160,196]{2,1,0:T(8,128)(2,1)S(1)}, bf16[2,160,196]{2,1,0:T(8,128)(2,1)S(1)}, u32[]{:S(2)}, u32[]{:S(2)}) collective-permute-start(bf16[2,160,196]{2,1,0:T(8,128)(2,1)S(1)} %bitcast.25), channel_id=1, source_target_pairs={{0,1},{1,0},{2,3},{3,2},{4,5},{5,4},{6,7},{7,6},{8,9},{9,8},{10,11... | collective-permute-start | bytes 376328 | tf_op jit(solution)/shard_map/ppermute | solution.py:628
  50.2 19.2 %collective-permute-start.3 = (bf16[160,512]{1,0:T(8,128)(2,1)}, bf16[160,512]{1,0:T(8,128)(2,1)S(1)}, u32[]{:S(2)}, u32[]{:S(2)}) collective-permute-start(bf16[160,512]{1,0:T(8,128)(2,1)} %get-tuple-element.149), channel_id=1, source_target_pairs={{0,4},{4,0},{8,12},{12,8},{1,5},{5,1},{9,13},{13,9},{2,6},{6,2},{1... | collective-permute-start | bytes 491528 | tf_op jit(solution)/shard_map/ppermute | solution.py:601
  50.6 18.8 %collective-permute-start.4 = (bf16[160,512]{1,0:T(8,128)(2,1)}, bf16[160,512]{1,0:T(8,128)(2,1)S(1)}, u32[]{:S(2)}, u32[]{:S(2)}) collective-permute-start(bf16[160,512]{1,0:T(8,128)(2,1)} %get-tuple-element.150), channel_id=1, source_target_pairs={{0,8},{4,12},{8,0},{12,4},{1,9},{5,13},{9,1},{13,5},{2,10},{6,14},... | collective-permute-start | bytes 491528 | tf_op jit(solution)/shard_map/ppermute | solution.py:601
  113.8 57.5 %collective-permute-start.9 = (bf16[1280,896]{1,0:T(8,128)(2,1)}, bf16[1280,896]{1,0:T(8,128)(2,1)}, u32[]{:S(2)}, u32[]{:S(2)}) collective-permute-start(bf16[1280,896]{1,0:T(8,128)(2,1)} %get-tuple-element.167), channel_id=1, source_target_pairs={{0,16},{16,0},{1,17},{17,1},{2,18},{18,2},{3,19},{19,3},{4,20},{20... | collective-permute-start | bytes 6881288 | tf_op jit(solution)/shard_map/ppermute | solution.py:591
  113.9 13.7 %collective-permute-start.13 = (bf16[320,384]{1,0:T(8,128)(2,1)S(1)}, bf16[320,384]{1,0:T(8,128)(2,1)S(1)}, u32[]{:S(2)}, u32[]{:S(2)}) collective-permute-start(bf16[320,384]{1,0:T(8,128)(2,1)S(1)} %copy-done.90), channel_id=1, source_target_pairs={{0,1},{1,0},{2,3},{3,2},{4,5},{5,4},{6,7},{7,6},{8,9},{9,8},{10,11... | collective-permute-start | bytes 737288 | tf_op jit(solution)/shard_map/ppermute | solution.py:601
  114.0 20.4 %collective-permute-start.14 = (bf16[320,384]{1,0:T(8,128)(2,1)S(1)}, bf16[320,384]{1,0:T(8,128)(2,1)S(1)}, u32[]{:S(2)}, u32[]{:S(2)}) collective-permute-start(bf16[320,384]{1,0:T(8,128)(2,1)S(1)} %copy-done.89), channel_id=1, source_target_pairs={{0,2},{1,3},{2,0},{3,1},{4,6},{5,7},{6,4},{7,5},{8,10},{9,11},{10,... | collective-permute-start | bytes 737288 | tf_op jit(solution)/shard_map/ppermute | solution.py:601
  116.8 20.0 %collective-permute-start.15 = (bf16[320,384]{1,0:T(8,128)(2,1)S(1)}, bf16[320,384]{1,0:T(8,128)(2,1)S(1)}, u32[]{:S(2)}, u32[]{:S(2)}) collective-permute-start(bf16[320,384]{1,0:T(8,128)(2,1)S(1)} %copy-done.87), channel_id=1, source_target_pairs={{0,3},{1,2},{2,1},{3,0},{4,7},{5,6},{6,5},{7,4},{8,11},{9,10},{10,... | collective-permute-start | bytes 737288 | tf_op jit(solution)/shard_map/ppermute | solution.py:601
  118.3 22.9 %collective-permute-start.27 = (bf16[320,512]{1,0:T(8,128)(2,1)S(1)}, bf16[320,512]{1,0:T(8,128)(2,1)S(1)}, u32[]{:S(2)}, u32[]{:S(2)}) collective-permute-start(bf16[320,512]{1,0:T(8,128)(2,1)S(1)} %copy-done.75), channel_id=1, source_target_pairs={{0,1},{1,0},{2,3},{3,2},{4,5},{5,4},{6,7},{7,6},{8,9},{9,8},{10,11... | collective-permute-start | bytes 983048 | tf_op jit(solution)/shard_map/ppermute | solution.py:601
  127.6 38.4 %collective-permute-start.28 = (bf16[320,512]{1,0:T(8,128)(2,1)S(1)}, bf16[320,512]{1,0:T(8,128)(2,1)S(1)}, u32[]{:S(2)}, u32[]{:S(2)}) collective-permute-start(bf16[320,512]{1,0:T(8,128)(2,1)S(1)} %copy-done.74), channel_id=1, source_target_pairs={{0,2},{1,3},{2,0},{3,1},{4,6},{5,7},{6,4},{7,5},{8,10},{9,11},{10,... | collective-permute-start | bytes 983048 | tf_op jit(solution)/shard_map/ppermute | solution.py:601
  134.4 31.6 %collective-permute-start.29 = (bf16[320,512]{1,0:T(8,128)(2,1)S(1)}, bf16[320,512]{1,0:T(8,128)(2,1)S(1)}, u32[]{:S(2)}, u32[]{:S(2)}) collective-permute-start(bf16[320,512]{1,0:T(8,128)(2,1)S(1)} %copy-done.72), channel_id=1, source_target_pairs={{0,3},{1,2},{2,1},{3,0},{4,7},{5,6},{6,5},{7,4},{8,11},{9,10},{10,... | collective-permute-start | bytes 983048 | tf_op jit(solution)/shard_map/ppermute | solution.py:601
  137.7 47.8 %collective-permute-start.19 = (bf16[320,384]{1,0:T(8,128)(2,1)}, bf16[320,384]{1,0:T(8,128)(2,1)}, u32[]{:S(2)}, u32[]{:S(2)}) collective-permute-start(bf16[320,384]{1,0:T(8,128)(2,1)} %multiply_convert_fusion.5), channel_id=1, source_target_pairs={{0,3},{1,2},{2,17},{3,16},{16,1},{17,0},{18,19},{19,18},{4,7},{5,6... | collective-permute-start | bytes 737288 | tf_op jit(solution)/shard_map/ppermute | solution.py:414
  141.2 44.4 %collective-permute-start.18 = (bf16[320,384]{1,0:T(8,128)(2,1)}, bf16[320,384]{1,0:T(8,128)(2,1)}, u32[]{:S(2)}, u32[]{:S(2)}) collective-permute-start(bf16[320,384]{1,0:T(8,128)(2,1)} %multiply_convert_fusion.5), channel_id=1, source_target_pairs={{0,2},{1,3},{2,16},{3,17},{16,0},{17,1},{18,18},{19,19},{4,6},{5,7... | collective-permute-start | bytes 737288 | tf_op jit(solution)/shard_map/ppermute | solution.py:414
  166.0 19.6 %collective-permute-start.17 = (bf16[320,384]{1,0:T(8,128)(2,1)}, bf16[320,384]{1,0:T(8,128)(2,1)}, u32[]{:S(2)}, u32[]{:S(2)}) collective-permute-start(bf16[320,384]{1,0:T(8,128)(2,1)} %multiply_convert_fusion.5), channel_id=1, source_target_pairs={{0,1},{1,0},{2,19},{3,18},{16,3},{17,2},{18,17},{19,16},{4,5},{5,4... | collective-permute-start | bytes 737288 | tf_op jit(solution)/shard_map/ppermute | solution.py:414
  166.0 19.6 %collective-permute-start.16 = (bf16[320,384]{1,0:T(8,128)(2,1)}, bf16[320,384]{1,0:T(8,128)(2,1)}, u32[]{:S(2)}, u32[]{:S(2)}) collective-permute-start(bf16[320,384]{1,0:T(8,128)(2,1)} %multiply_convert_fusion.5), channel_id=1, source_target_pairs={{0,0},{1,1},{2,18},{3,19},{16,2},{17,3},{18,16},{19,17},{4,4},{5,5... | collective-permute-start | bytes 737288 | tf_op jit(solution)/shard_map/ppermute | solution.py:414
  171.4 54.9 %collective-permute-start.34 = (bf16[640,784]{0,1:T(8,128)(2,1)}, bf16[640,784]{0,1:T(8,128)(2,1)S(1)}, u32[]{:S(2)}, u32[]{:S(2)}) collective-permute-start(bf16[640,784]{0,1:T(8,128)(2,1)} %copy.13), channel_id=1, source_target_pairs={{0,16},{16,0},{1,17},{17,1},{2,18},{18,2},{3,19},{19,3},{4,20},{20... | collective-permute-start | bytes 3010568 | tf_op jit(solution)/shard_map/ppermute | solution.py:591
  191.8 29.0 %collective-permute-start.20 = (bf16[1280,384]{1,0:T(8,128)(2,1)}, bf16[1280,384]{1,0:T(8,128)(2,1)S(1)}, u32[]{:S(2)}, u32[]{:S(2)}) collective-permute-start(bf16[1280,384]{1,0:T(8,128)(2,1)} %get-tuple-element.181), channel_id=1, source_target_pairs={{0,16},{16,0},{1,17},{17,1},{2,18},{18,2},{3,19},{19,3},{4,20},{20... | collective-permute-start | bytes 2949128 | tf_op jit(solution)/shard_map/ppermute | solution.py:591
  197.2 12.0 %collective-permute-start.32 = (bf16[320,512]{1,0:T(8,128)(2,1)S(1)}, bf16[320,512]{1,0:T(8,128)(2,1)S(1)}, u32[]{:S(2)}, u32[]{:S(2)}) collective-permute-start(bf16[320,512]{1,0:T(8,128)(2,1)S(1)} %multiply_convert_fusion.2), channel_id=1, source_target_pairs={{0,2},{1,3},{2,16},{3,17},{16,0},{17,1},{18,18},{19,19},{4,6},{5,7... | collective-permute-start | bytes 983048 | tf_op jit(solution)/shard_map/ppermute | solution.py:414
  199.1 19.3 %collective-permute-start.31 = (bf16[320,512]{1,0:T(8,128)(2,1)S(1)}, bf16[320,512]{1,0:T(8,128)(2,1)S(1)}, u32[]{:S(2)}, u32[]{:S(2)}) collective-permute-start(bf16[320,512]{1,0:T(8,128)(2,1)S(1)} %multiply_convert_fusion.2), channel_id=1, source_target_pairs={{0,1},{1,0},{2,19},{3,18},{16,3},{17,2},{18,17},{19,16},{4,5},{5,4... | collective-permute-start | bytes 983048 | tf_op jit(solution)/shard_map/ppermute | solution.py:414
  203.1 23.1 %collective-permute-start.36 = (bf16[640,512]{1,0:T(8,128)(2,1)S(1)}, bf16[640,512]{1,0:T(8,128)(2,1)S(1)}, u32[]{:S(2)}, u32[]{:S(2)}) collective-permute-start(bf16[640,512]{1,0:T(8,128)(2,1)S(1)} %copy-done.18), channel_id=1, source_target_pairs={{0,16},{16,0},{1,17},{17,1},{2,18},{18,2},{3,19},{19,3},{4,20},{20... | collective-permute-start | bytes 1966088 | tf_op jit(solution)/shard_map/ppermute | solution.py:591
  209.3 15.5 %collective-permute-start.35 = (bf16[640,384]{1,0:T(8,128)(2,1)S(1)}, bf16[640,384]{1,0:T(8,128)(2,1)}, u32[]{:S(2)}, u32[]{:S(2)}) collective-permute-start(bf16[640,384]{1,0:T(8,128)(2,1)S(1)} %copy-done.36), channel_id=1, source_target_pairs={{0,16},{16,0},{1,17},{17,1},{2,18},{18,2},{3,19},{19,3},{4,20},{20... | collective-permute-start | bytes 1474568 | tf_op jit(solution)/shard_map/ppermute | solution.py:591
  219.8 24.9 %collective-permute-start.10 = (bf16[320,896]{1,0:T(8,128)(2,1)}, bf16[320,896]{1,0:T(8,128)(2,1)S(1)}, u32[]{:S(2)}, u32[]{:S(2)}) collective-permute-start(bf16[320,896]{1,0:T(8,128)(2,1)} %get-tuple-element.169), channel_id=1, source_target_pairs={{0,4},{4,0},{8,12},{12,8},{1,5},{5,1},{9,13},{13,9},{2,6},{6,2},{1... | collective-permute-start | bytes 1720328 | tf_op jit(solution)/shard_map/ppermute | solution.py:601
  220.8 24.8 %collective-permute-start.11 = (bf16[320,896]{1,0:T(8,128)(2,1)}, bf16[320,896]{1,0:T(8,128)(2,1)S(1)}, u32[]{:S(2)}, u32[]{:S(2)}) collective-permute-start(bf16[320,896]{1,0:T(8,128)(2,1)} %get-tuple-element.170), channel_id=1, source_target_pairs={{0,8},{4,12},{8,0},{12,4},{1,9},{5,13},{9,1},{13,5},{2,10},{6,14},... | collective-permute-start | bytes 1720328 | tf_op jit(solution)/shard_map/ppermute | solution.py:601
  224.8 22.3 %collective-permute-start.12 = (bf16[320,896]{1,0:T(8,128)(2,1)}, bf16[320,896]{1,0:T(8,128)(2,1)}, u32[]{:S(2)}, u32[]{:S(2)}) collective-permute-start(bf16[320,896]{1,0:T(8,128)(2,1)} %get-tuple-element.171), channel_id=1, source_target_pairs={{0,12},{4,8},{8,4},{12,0},{1,13},{5,9},{9,5},{13,1},{2,14},{6,10},... | collective-permute-start | bytes 1720328 | tf_op jit(solution)/shard_map/ppermute | solution.py:601
  233.2 30.2 %collective-permute-start.37 = (bf16[1280,512]{1,0:T(8,128)(2,1)}, bf16[1280,512]{1,0:T(8,128)(2,1)S(1)}, u32[]{:S(2)}, u32[]{:S(2)}) collective-permute-start(bf16[1280,512]{1,0:T(8,128)(2,1)} %get-tuple-element.202), channel_id=1, source_target_pairs={{0,16},{16,0},{1,17},{17,1},{2,18},{18,2},{3,19},{19,3},{4,20},{20... | collective-permute-start | bytes 3932168 | tf_op jit(solution)/shard_map/ppermute | solution.py:591
  244.7 14.8 %collective-permute-start.22 = (bf16[320,384]{1,0:T(8,128)(2,1)}, bf16[320,384]{1,0:T(8,128)(2,1)S(1)}, u32[]{:S(2)}, u32[]{:S(2)}) collective-permute-start(bf16[320,384]{1,0:T(8,128)(2,1)} %get-tuple-element.184), channel_id=1, source_target_pairs={{0,8},{4,12},{8,0},{12,4},{1,9},{5,13},{9,1},{13,5},{2,10},{6,14},... | collective-permute-start | bytes 737288 | tf_op jit(solution)/shard_map/ppermute | solution.py:601
  245.6 13.9 %collective-permute-start.23 = (bf16[320,384]{1,0:T(8,128)(2,1)S(1)}, bf16[320,384]{1,0:T(8,128)(2,1)S(1)}, u32[]{:S(2)}, u32[]{:S(2)}) collective-permute-start(bf16[320,384]{1,0:T(8,128)(2,1)S(1)} %copy-done.91), channel_id=1, source_target_pairs={{0,12},{4,8},{8,4},{12,0},{1,13},{5,9},{9,5},{13,1},{2,14},{6,10},... | collective-permute-start | bytes 737288 | tf_op jit(solution)/shard_map/ppermute | solution.py:601
  261.4 12.7 %collective-permute-start.25 = (bf16[320,384]{1,0:T(8,128)(2,1)S(1)}, bf16[320,384]{1,0:T(8,128)(2,1)S(1)}, u32[]{:S(2)}, u32[]{:S(2)}) collective-permute-start(bf16[320,384]{1,0:T(8,128)(2,1)S(1)} %get-tuple-element.207.refs_0_), channel_id=1, source_target_pairs={{0,8},{4,12},{8,0},{12,4},{1,9},{5,13},{9,1},{13,5},{2,10},{6,14},... | collective-permute-start | bytes 737288 | tf_op jit(solution)/shard_map/ppermute | solution.py:601
  262.5 11.6 %collective-permute-start.24 = (bf16[320,384]{1,0:T(8,128)(2,1)S(1)}, bf16[320,384]{1,0:T(8,128)(2,1)S(1)}, u32[]{:S(2)}, u32[]{:S(2)}) collective-permute-start(bf16[320,384]{1,0:T(8,128)(2,1)S(1)} %get-tuple-element.207.refs_0_), channel_id=1, source_target_pairs={{0,4},{4,0},{8,12},{12,8},{1,5},{5,1},{9,13},{13,9},{2,6},{6,2},{1... | collective-permute-start | bytes 737288 | tf_op jit(solution)/shard_map/ppermute | solution.py:601
  277.3 10.6 %collective-permute-start.43 = (bf16[320,512]{1,0:T(8,128)(2,1)S(1)}, bf16[320,512]{1,0:T(8,128)(2,1)S(1)}, u32[]{:S(2)}, u32[]{:S(2)}) collective-permute-start(bf16[320,512]{1,0:T(8,128)(2,1)S(1)} %copy-done.79), channel_id=1, source_target_pairs={{0,4},{4,0},{8,12},{12,8},{1,5},{5,1},{9,13},{13,9},{2,6},{6,2},{1... | collective-permute-start | bytes 983048 | tf_op jit(solution)/shard_map/ppermute | solution.py:601
  278.4 16.8 %collective-permute-start.44 = (bf16[320,512]{1,0:T(8,128)(2,1)S(1)}, bf16[320,512]{1,0:T(8,128)(2,1)S(1)}, u32[]{:S(2)}, u32[]{:S(2)}) collective-permute-start(bf16[320,512]{1,0:T(8,128)(2,1)S(1)} %copy-done.78), channel_id=1, source_target_pairs={{0,8},{4,12},{8,0},{12,4},{1,9},{5,13},{9,1},{13,5},{2,10},{6,14},... | collective-permute-start | bytes 983048 | tf_op jit(solution)/shard_map/ppermute | solution.py:601
  279.4 15.9 %collective-permute-start.45 = (bf16[320,512]{1,0:T(8,128)(2,1)S(1)}, bf16[320,512]{1,0:T(8,128)(2,1)S(1)}, u32[]{:S(2)}, u32[]{:S(2)}) collective-permute-start(bf16[320,512]{1,0:T(8,128)(2,1)S(1)} %copy-done.76), channel_id=1, source_target_pairs={{0,12},{4,8},{8,4},{12,0},{1,13},{5,9},{9,5},{13,1},{2,14},{6,10},... | collective-permute-start | bytes 983048 | tf_op jit(solution)/shard_map/ppermute | solution.py:601
  295.7 11.6 %collective-permute-start.48 = (bf16[320,512]{1,0:T(8,128)(2,1)S(1)}, bf16[320,512]{1,0:T(8,128)(2,1)S(1)}, u32[]{:S(2)}, u32[]{:S(2)}) collective-permute-start(bf16[320,512]{1,0:T(8,128)(2,1)S(1)} %get-tuple-element.283.refs_0_), channel_id=1, source_target_pairs={{0,12},{4,8},{8,4},{12,0},{1,13},{5,9},{9,5},{13,1},{2,14},{6,10},... | collective-permute-start | bytes 983048 | tf_op jit(solution)/shard_map/ppermute | solution.py:601
  297.2 15.4 %collective-permute-start.47 = (bf16[320,512]{1,0:T(8,128)(2,1)S(1)}, bf16[320,512]{1,0:T(8,128)(2,1)S(1)}, u32[]{:S(2)}, u32[]{:S(2)}) collective-permute-start(bf16[320,512]{1,0:T(8,128)(2,1)S(1)} %get-tuple-element.283.refs_0_), channel_id=1, source_target_pairs={{0,8},{4,12},{8,0},{12,4},{1,9},{5,13},{9,1},{13,5},{2,10},{6,14},... | collective-permute-start | bytes 983048 | tf_op jit(solution)/shard_map/ppermute | solution.py:601
  298.2 14.5 %collective-permute-start.46 = (bf16[320,512]{1,0:T(8,128)(2,1)S(1)}, bf16[320,512]{1,0:T(8,128)(2,1)S(1)}, u32[]{:S(2)}, u32[]{:S(2)}) collective-permute-start(bf16[320,512]{1,0:T(8,128)(2,1)S(1)} %get-tuple-element.283.refs_0_), channel_id=1, source_target_pairs={{0,4},{4,0},{8,12},{12,8},{1,5},{5,1},{9,13},{13,9},{2,6},{6,2},{1... | collective-permute-start | bytes 983048 | tf_op jit(solution)/shard_map/ppermute | solution.py:601
  316.6 17.2 %collective-permute-start.49 = (bf16[1280,512]{1,0:T(8,128)(2,1)}, bf16[1280,512]{1,0:T(8,128)(2,1)S(1)}, u32[]{:S(2)}, u32[]{:S(2)}) collective-permute-start(bf16[1280,512]{1,0:T(8,128)(2,1)} %shard_map.129.refs_0_.refs_3_), channel_id=1, source_target_pairs={{0,16},{16,0},{1,17},{17,1},{2,18},{18,2},{3,19},{19,3},{4,20},{20... | collective-permute-start | bytes 3932168 | tf_op jit(solution)/shard_map/ppermute | solution.py:591
  316.6 24.7 %collective-permute-start.39 = (bf16[320,384]{1,0:T(8,128)(2,1)S(1)}, bf16[320,384]{1,0:T(8,128)(2,1)S(1)}, u32[]{:S(2)}, u32[]{:S(2)}) collective-permute-start(bf16[320,384]{1,0:T(8,128)(2,1)S(1)} %copy-done.88), channel_id=1, source_target_pairs={{0,0},{1,1},{18,2},{19,3},{2,16},{3,17},{16,18},{17,19},{4,4},{5,5... | collective-permute-start | bytes 737288 | tf_op jit(solution)/shard_map/ppermute | solution.py:414
  317.4 24.8 %collective-permute-start.40 = (bf16[320,384]{1,0:T(8,128)(2,1)S(1)}, bf16[320,384]{1,0:T(8,128)(2,1)S(1)}, u32[]{:S(2)}, u32[]{:S(2)}) collective-permute-start(bf16[320,384]{1,0:T(8,128)(2,1)S(1)} %copy-done.86), channel_id=1, source_target_pairs={{1,0},{0,1},{19,2},{18,3},{3,16},{2,17},{17,18},{16,19},{5,4},{4,5... | collective-permute-start | bytes 737288 | tf_op jit(solution)/shard_map/ppermute | solution.py:414
  317.5 27.4 %collective-permute-start.41 = (bf16[320,384]{1,0:T(8,128)(2,1)S(1)}, bf16[320,384]{1,0:T(8,128)(2,1)S(1)}, u32[]{:S(2)}, u32[]{:S(2)}) collective-permute-start(bf16[320,384]{1,0:T(8,128)(2,1)S(1)} %copy-done.85), channel_id=1, source_target_pairs={{2,0},{3,1},{16,2},{17,3},{0,16},{1,17},{18,18},{19,19},{6,4},{7,5... | collective-permute-start | bytes 737288 | tf_op jit(solution)/shard_map/ppermute | solution.py:414
  329.7 16.2 %collective-permute-start.42 = (bf16[320,384]{1,0:T(8,128)(2,1)S(1)}, bf16[320,384]{1,0:T(8,128)(2,1)S(1)}, u32[]{:S(2)}, u32[]{:S(2)}) collective-permute-start(bf16[320,384]{1,0:T(8,128)(2,1)S(1)} %copy-done.84), channel_id=1, source_target_pairs={{3,0},{2,1},{17,2},{16,3},{1,16},{0,17},{19,18},{18,19},{7,4},{6,5... | collective-permute-start | bytes 737288 | tf_op jit(solution)/shard_map/ppermute | solution.py:414
  341.3 19.5 %collective-permute-start.54 = (bf16[320,384]{1,0:T(8,128)(2,1)S(1)}, bf16[320,384]{1,0:T(8,128)(2,1)S(1)}, u32[]{:S(2)}, u32[]{:S(2)}) collective-permute-start(bf16[320,384]{1,0:T(8,128)(2,1)S(1)} %get-tuple-element.233.refs_0_), channel_id=1, source_target_pairs={{0,8},{4,12},{8,0},{12,4},{1,9},{5,13},{9,1},{13,5},{2,10},{6,14},... | collective-permute-start | bytes 737288 | tf_op jit(solution)/shard_map/ppermute | solution.py:601
  342.2 25.0 %collective-permute-start.58 = (bf16[320,512]{1,0:T(8,128)(2,1)S(1)}, bf16[320,512]{1,0:T(8,128)(2,1)S(1)}, u32[]{:S(2)}, u32[]{:S(2)}) collective-permute-start(bf16[320,512]{1,0:T(8,128)(2,1)S(1)} %get-tuple-element.237.refs_0_), channel_id=1, source_target_pairs={{0,12},{4,8},{8,4},{12,0},{1,13},{5,9},{9,5},{13,1},{2,14},{6,10},... | collective-permute-start | bytes 983048 | tf_op jit(solution)/shard_map/ppermute | solution.py:601
  344.9 22.8 %collective-permute-start.57 = (bf16[320,512]{1,0:T(8,128)(2,1)S(1)}, bf16[320,512]{1,0:T(8,128)(2,1)S(1)}, u32[]{:S(2)}, u32[]{:S(2)}) collective-permute-start(bf16[320,512]{1,0:T(8,128)(2,1)S(1)} %get-tuple-element.237.refs_0_), channel_id=1, source_target_pairs={{0,8},{4,12},{8,0},{12,4},{1,9},{5,13},{9,1},{13,5},{2,10},{6,14},... | collective-permute-start | bytes 983048 | tf_op jit(solution)/shard_map/ppermute | solution.py:601
  345.9 21.9 %collective-permute-start.56 = (bf16[320,512]{1,0:T(8,128)(2,1)S(1)}, bf16[320,512]{1,0:T(8,128)(2,1)S(1)}, u32[]{:S(2)}, u32[]{:S(2)}) collective-permute-start(bf16[320,512]{1,0:T(8,128)(2,1)S(1)} %get-tuple-element.237.refs_0_), channel_id=1, source_target_pairs={{0,4},{4,0},{8,12},{12,8},{1,5},{5,1},{9,13},{13,9},{2,6},{6,2},{1... | collective-permute-start | bytes 983048 | tf_op jit(solution)/shard_map/ppermute | solution.py:601
  349.7 17.6 %collective-permute-start.53 = (bf16[320,384]{1,0:T(8,128)(2,1)S(1)}, bf16[320,384]{1,0:T(8,128)(2,1)S(1)}, u32[]{:S(2)}, u32[]{:S(2)}) collective-permute-start(bf16[320,384]{1,0:T(8,128)(2,1)S(1)} %get-tuple-element.233.refs_0_), channel_id=1, source_target_pairs={{0,4},{4,0},{8,12},{12,8},{1,5},{5,1},{9,13},{13,9},{2,6},{6,2},{1... | collective-permute-start | bytes 737288 | tf_op jit(solution)/shard_map/ppermute | solution.py:601
  371.7 66.7 %collective-permute-start.60 = (bf16[1280,512]{1,0:T(8,128)(2,1)}, bf16[1280,512]{1,0:T(8,128)(2,1)S(1)}, u32[]{:S(2)}, u32[]{:S(2)}) collective-permute-start(bf16[1280,512]{1,0:T(8,128)(2,1)} %shard_map.133.refs_1_), channel_id=1, source_target_pairs={{0,16},{16,0},{1,17},{17,1},{2,18},{18,2},{3,19},{19,3},{4,20},{20... | collective-permute-start | bytes 3932168 | tf_op jit(solution)/shard_map/ppermute | solution.py:591
  375.1 47.2 %collective-permute-start.59 = (bf16[1280,384]{1,0:T(8,128)(2,1)}, bf16[1280,384]{1,0:T(8,128)(2,1)S(1)}, u32[]{:S(2)}, u32[]{:S(2)}) collective-permute-start(bf16[1280,384]{1,0:T(8,128)(2,1)} %shard_map.132.refs_0_), channel_id=1, source_target_pairs={{0,16},{16,0},{1,17},{17,1},{2,18},{18,2},{3,19},{19,3},{4,20},{20... | collective-permute-start | bytes 2949128 | tf_op jit(solution)/shard_map/ppermute | solution.py:591
  376.7 14.0 %collective-permute-start.65 = (bf16[320,512]{1,0:T(8,128)(2,1)S(1)}, bf16[320,512]{1,0:T(8,128)(2,1)S(1)}, u32[]{:S(2)}, u32[]{:S(2)}) collective-permute-start(bf16[320,512]{1,0:T(8,128)(2,1)S(1)} %copy-done.69), channel_id=1, source_target_pairs={{1,0},{0,1},{19,2},{18,3},{3,16},{2,17},{17,18},{16,19},{5,4},{4,5... | collective-permute-start | bytes 983048 | tf_op jit(solution)/shard_map/ppermute | solution.py:414
  376.7 32.1 %collective-permute-start.66 = (bf16[320,512]{1,0:T(8,128)(2,1)S(1)}, bf16[320,512]{1,0:T(8,128)(2,1)S(1)}, u32[]{:S(2)}, u32[]{:S(2)}) collective-permute-start(bf16[320,512]{1,0:T(8,128)(2,1)S(1)} %copy-done.68), channel_id=1, source_target_pairs={{2,0},{3,1},{16,2},{17,3},{0,16},{1,17},{18,18},{19,19},{6,4},{7,5... | collective-permute-start | bytes 983048 | tf_op jit(solution)/shard_map/ppermute | solution.py:414
  379.8 28.9 %collective-permute-start.67 = (bf16[320,512]{1,0:T(8,128)(2,1)S(1)}, bf16[320,512]{1,0:T(8,128)(2,1)S(1)}, u32[]{:S(2)}, u32[]{:S(2)}) collective-permute-start(bf16[320,512]{1,0:T(8,128)(2,1)S(1)} %copy-done.67), channel_id=1, source_target_pairs={{3,0},{2,1},{17,2},{16,3},{1,16},{0,17},{19,18},{18,19},{7,4},{6,5... | collective-permute-start | bytes 983048 | tf_op jit(solution)/shard_map/ppermute | solution.py:414
  390.7 31.1 %collective-permute-start.52 = (bf16[320,384]{1,0:T(8,128)(2,1)S(1)}, bf16[320,384]{1,0:T(8,128)(2,1)S(1)}, u32[]{:S(2)}, u32[]{:S(2)}) collective-permute-start(bf16[320,384]{1,0:T(8,128)(2,1)S(1)} %multiply_convert_fusion.4.refs_0_), channel_id=1, source_target_pairs={{0,3},{1,2},{2,1},{3,0},{4,7},{5,6},{6,5},{7,4},{8,11},{9,10},{10,... | collective-permute-start | bytes 737288 | tf_op jit(solution)/shard_map/ppermute | solution.py:601
  408.8 53.5 %collective-permute-start.51 = (bf16[320,384]{1,0:T(8,128)(2,1)S(1)}, bf16[320,384]{1,0:T(8,128)(2,1)S(1)}, u32[]{:S(2)}, u32[]{:S(2)}) collective-permute-start(bf16[320,384]{1,0:T(8,128)(2,1)S(1)} %multiply_convert_fusion.4.refs_0_), channel_id=1, source_target_pairs={{0,2},{1,3},{2,0},{3,1},{4,6},{5,7},{6,4},{7,5},{8,10},{9,11},{10,... | collective-permute-start | bytes 737288 | tf_op jit(solution)/shard_map/ppermute | solution.py:601
  408.8 53.5 %collective-permute-start.50 = (bf16[320,384]{1,0:T(8,128)(2,1)S(1)}, bf16[320,384]{1,0:T(8,128)(2,1)S(1)}, u32[]{:S(2)}, u32[]{:S(2)}) collective-permute-start(bf16[320,384]{1,0:T(8,128)(2,1)S(1)} %multiply_convert_fusion.4.refs_0_), channel_id=1, source_target_pairs={{0,1},{1,0},{2,3},{3,2},{4,5},{5,4},{6,7},{7,6},{8,9},{9,8},{10,11... | collective-permute-start | bytes 737288 | tf_op jit(solution)/shard_map/ppermute | solution.py:601
  421.8 46.1 %collective-permute-start.70 = (bf16[320,512]{1,0:T(8,128)(2,1)S(1)}, bf16[320,512]{1,0:T(8,128)(2,1)S(1)}, u32[]{:S(2)}, u32[]{:S(2)}) collective-permute-start(bf16[320,512]{1,0:T(8,128)(2,1)S(1)} %multiply_convert_fusion.refs_0_), channel_id=1, source_target_pairs={{0,3},{1,2},{2,1},{3,0},{4,7},{5,6},{6,5},{7,4},{8,11},{9,10},{10,... | collective-permute-start | bytes 983048 | tf_op jit(solution)/shard_map/ppermute | solution.py:601
  422.3 45.6 %collective-permute-start.69 = (bf16[320,512]{1,0:T(8,128)(2,1)S(1)}, bf16[320,512]{1,0:T(8,128)(2,1)S(1)}, u32[]{:S(2)}, u32[]{:S(2)}) collective-permute-start(bf16[320,512]{1,0:T(8,128)(2,1)S(1)} %multiply_convert_fusion.refs_0_), channel_id=1, source_target_pairs={{0,2},{1,3},{2,0},{3,1},{4,6},{5,7},{6,4},{7,5},{8,10},{9,11},{10,... | collective-permute-start | bytes 983048 | tf_op jit(solution)/shard_map/ppermute | solution.py:601
  438.4 29.6 %collective-permute-start.68 = (bf16[320,512]{1,0:T(8,128)(2,1)S(1)}, bf16[320,512]{1,0:T(8,128)(2,1)S(1)}, u32[]{:S(2)}, u32[]{:S(2)}) collective-permute-start(bf16[320,512]{1,0:T(8,128)(2,1)S(1)} %multiply_convert_fusion.refs_0_), channel_id=1, source_target_pairs={{0,1},{1,0},{2,3},{3,2},{4,5},{5,4},{6,7},{7,6},{8,9},{9,8},{10,11... | collective-permute-start | bytes 983048 | tf_op jit(solution)/shard_map/ppermute | solution.py:601
  474.6 18.4 %collective-permute-start.74 = (bf16[160,512]{1,0:T(8,128)(2,1)}, bf16[160,512]{1,0:T(8,128)(2,1)S(1)}, u32[]{:S(2)}, u32[]{:S(2)}) collective-permute-start(bf16[160,512]{1,0:T(8,128)(2,1)} %get-tuple-element.261), channel_id=1, source_target_pairs={{0,8},{4,12},{8,0},{12,4},{1,9},{5,13},{9,1},{13,5},{2,10},{6,14},... | collective-permute-start | bytes 491528 | tf_op jit(solution)/shard_map/ppermute | solution.py:601
  475.7 17.3 %collective-permute-start.75 = (bf16[160,512]{1,0:T(8,128)(2,1)}, bf16[160,512]{1,0:T(8,128)(2,1)S(1)}, u32[]{:S(2)}, u32[]{:S(2)}) collective-permute-start(bf16[160,512]{1,0:T(8,128)(2,1)} %get-tuple-element.262), channel_id=1, source_target_pairs={{0,12},{4,8},{8,4},{12,0},{1,13},{5,9},{9,5},{13,1},{2,14},{6,10},... | collective-permute-start | bytes 491528 | tf_op jit(solution)/shard_map/ppermute | solution.py:601
  481.0 12.0 %collective-permute-start.61 = (bf16[160,384]{1,0:T(8,128)(2,1)S(1)}, bf16[160,384]{1,0:T(8,128)(2,1)S(1)}, u32[]{:S(2)}, u32[]{:S(2)}) collective-permute-start(bf16[160,384]{1,0:T(8,128)(2,1)S(1)} %copy-done.95), channel_id=1, source_target_pairs={{0,4},{4,0},{8,12},{12,8},{1,5},{5,1},{9,13},{13,9},{2,6},{6,2},{1... | collective-permute-start | bytes 368648 | tf_op jit(solution)/shard_map/ppermute | solution.py:601
  481.9 11.1 %collective-permute-start.62 = (bf16[160,384]{1,0:T(8,128)(2,1)S(1)}, bf16[160,384]{1,0:T(8,128)(2,1)S(1)}, u32[]{:S(2)}, u32[]{:S(2)}) collective-permute-start(bf16[160,384]{1,0:T(8,128)(2,1)S(1)} %copy-done.94), channel_id=1, source_target_pairs={{0,8},{4,12},{8,0},{12,4},{1,9},{5,13},{9,1},{13,5},{2,10},{6,14},... | collective-permute-start | bytes 368648 | tf_op jit(solution)/shard_map/ppermute | solution.py:601
  525.8 30.9 %collective-permute-start.76 = (bf16[160,784]{1,0:T(8,128)(2,1)}, bf16[160,784]{1,0:T(8,128)(2,1)S(1)}, u32[]{:S(2)}, u32[]{:S(2)}) collective-permute-start(bf16[160,784]{1,0:T(8,128)(2,1)} %get-tuple-element.274), channel_id=1, source_target_pairs={{0,1},{1,0},{2,3},{3,2},{4,5},{5,4},{6,7},{7,6},{8,9},{9,8},{10,11... | collective-permute-start | bytes 752648 | tf_op jit(solution)/shard_map/ppermute | solution.py:601
  526.8 29.9 %collective-permute-start.77 = (bf16[160,784]{1,0:T(8,128)(2,1)S(1)}, bf16[160,784]{1,0:T(8,128)(2,1)S(1)}, u32[]{:S(2)}, u32[]{:S(2)}) collective-permute-start(bf16[160,784]{1,0:T(8,128)(2,1)S(1)} %copy-done.83), channel_id=1, source_target_pairs={{0,2},{1,3},{2,0},{3,1},{4,6},{5,7},{6,4},{7,5},{8,10},{9,11},{10,... | collective-permute-start | bytes 752648 | tf_op jit(solution)/shard_map/ppermute | solution.py:601
  527.3 29.3 %collective-permute-start.78 = (bf16[160,784]{1,0:T(8,128)(2,1)S(1)}, bf16[160,784]{1,0:T(8,128)(2,1)S(1)}, u32[]{:S(2)}, u32[]{:S(2)}) collective-permute-start(bf16[160,784]{1,0:T(8,128)(2,1)S(1)} %copy-done.82), channel_id=1, source_target_pairs={{0,3},{1,2},{2,1},{3,0},{4,7},{5,6},{6,5},{7,4},{8,11},{9,10},{10,... | collective-permute-start | bytes 752648 | tf_op jit(solution)/shard_map/ppermute | solution.py:601
  (112 other events, 1497.9 us)

commit v3 on v2

--- a/solution.py
+++ b/solution.py
@@ -164,14 +164,13 @@
 
 
 def conv_back_body(m_ref, w_ref, *refs, side, n):
-    outs, padded, (planes, total) = refs[:n], refs[n], refs[n + 1 :]
+    outs, (planes, total) = refs[:n], refs[n:]
     t = pl.program_id(0)
     me = lax.axis_index("cout")
 
     @pl.when(t == 0)
     def _():
         fill_columns(planes, m_ref[...], side)
-        padded[...] = planes[1]
         total[...] = jnp.zeros_like(total)
 
     term = None
@@ -189,15 +188,15 @@
     width, pixels = m.shape
     wide = lanes_of(pixels + side + 1)
     depth = kernel.shape[1]
-    outs = pl.pallas_call(
+    return pl.pallas_call(
         functools.partial(conv_back_body, side=side, n=n),
-        out_shape=[like((depth // n, pixels))] * n + [like((width, wide))],
+        out_shape=[like((depth // n, pixels))] * n,
         grid=(3,),
         in_specs=[
             whole((width, pixels)),
             pl.BlockSpec((3, depth, width), lambda t: (t, 0, 0)),
         ],
-        out_specs=[whole((depth // n, pixels))] * n + [whole((width, wide))],
+        out_specs=[whole((depth // n, pixels))] * n,
         scratch_shapes=[
             pltpu.VMEM((3, width, wide), BF16),
             pltpu.VMEM((depth, wide), F32),
@@ -205,19 +204,19 @@
         compiler_params=params(),
         cost_estimate=cost(2 * TAPS * depth * width * wide, 2 * kernel.size + 4 * width * wide),
     )(m, kernel)
-    return outs[:n], outs[n]
 
 
 def conv_weight_body(xa_ref, xb_ref, ma_ref, mb_ref, o_ref, pa, pb, both, *, side):
     t = pl.program_id(0)
-    wide = pa.shape[2]
+    wide, pixels = pa.shape[2], ma_ref.shape[1]
 
     @pl.when(t == 0)
     def _():
         fill_columns(pa, xa_ref[...], side)
         fill_columns(pb, xb_ref[...], side)
-        both[:, :wide] = ma_ref[...]
-        both[:, wide:] = mb_ref[...]
+        both[...] = jnp.zeros_like(both)
+        both[:, :pixels] = ma_ref[...]
+        both[:, wide : wide + pixels] = mb_ref[...]
 
     dy, dx = t // 3 - 1, t % 3 - 1
     window = jnp.concatenate(
@@ -228,12 +227,13 @@
 
 def conv_weight(xa, xb, ma, mb, side):
     depth, pixels = xa.shape
-    width, wide = ma.shape
+    width = ma.shape[0]
+    wide = lanes_of(pixels + side + 1)
     return pl.pallas_call(
         functools.partial(conv_weight_body, side=side),
         out_shape=like((TAPS, depth, width), F32),
         grid=(TAPS,),
-        in_specs=[whole((depth, pixels))] * 2 + [whole((width, wide))] * 2,
+        in_specs=[whole((depth, pixels))] * 2 + [whole((width, pixels))] * 2,
         out_specs=pl.BlockSpec((1, depth, width), lambda t: (t, 0, 0)),
         scratch_shapes=[pltpu.VMEM((3, depth, wide), BF16)] * 2
         + [pltpu.VMEM((width, 2 * wide), BF16)],
@@ -324,11 +324,11 @@
 
 
 def half_weight_body(*refs, side):
-    mine, other, g_ref, o_ref, (moved, planes) = refs[0:2], refs[2:4], refs[4], refs[5], refs[6:]
+    mine, other, g_ref, o_ref, moved, planes = refs
     t = pl.program_id(0)
     count = g_ref.shape[0]
-    half = mine[0].shape[0] // count
-    pixels = sum(ref.shape[1] for ref in mine)
+    half = mine.shape[0] // count
+    pixels = mine.shape[1]
     wide = moved.shape[2] // count
     core = lax.axis_index("section")
 
@@ -337,13 +337,9 @@
         fill_moved(moved, g_ref[...], side // 2)
         for k in range(4):
             pick = chosen(k, wide, pixels, side)
-            for pair, place in ((mine, core), (other, 1 - core)):
+            for ref, place in ((mine, core), (other, 1 - core)):
                 for b in range(count):
-                    rows = slice(b * half, (b + 1) * half)
-                    plane = None
-                    for ref, (start, stop) in zip(pair, spans(pixels)):
-                        term = dot(ref[rows, :], pick[:, start:stop], NT)
-                        plane = term if plane is None else plane + term
+                    plane = dot(ref[b * half : (b + 1) * half, :], pick, NT)
                     planes[k, rows_at(place, half), b * wide : (b + 1) * wide] = plane.astype(BF16)
 
     ty, tx = t // 3, t % 3
@@ -354,13 +350,13 @@
 
 def half_weight(mine, other, cots, side):
     count, width, small = cots.shape
-    depth = 2 * mine[0].shape[0] // count
+    depth = 2 * mine.shape[0] // count
     wide = lanes_of(small + side // 2 + 1)
     return pl.pallas_call(
         functools.partial(half_weight_body, side=side),
         out_shape=like((TAPS, depth, width), F32),
         grid=(TAPS,),
-        in_specs=[whole(v.shape) for v in (*mine, *other, cots)],
+        in_specs=[whole(v.shape) for v in (mine, other, cots)],
         out_specs=pl.BlockSpec((1, depth, width), lambda t: (t, 0, 0)),
         scratch_shapes=[
             pltpu.VMEM((4, width, count * wide), BF16),
@@ -370,7 +366,7 @@
         cost_estimate=cost(
             2 * TAPS * depth * width * count * small * 2, 4 * TAPS * depth * width
         ),
-    )(*mine, *other, cots)
+    )(mine, other, cots)
 
 
 def expand(first_block, weight, n):
@@ -589,6 +585,11 @@
 
 def swap(value):
     return lax.ppermute(value, "section", [(0, 1), (1, 0)])
+
+
+def swap_blocks(value, n):
+    rows, width = value.shape
+    return swap(value.reshape(n, rows // n, width)).reshape(rows, width)
 
 
 def after(value, *earlier):
@@ -668,7 +669,7 @@
         expand_got.append(exchange(ready, "cout"))
 
     back_kept, back_sent = half_back(after(cot_block, ready), stride_kernel, SIDE)
-    feature_other = swap(after(feature_block, ready))
+    feature_other = swap_blocks(after(feature_block, ready), n)
     first_other = [swap(after(v, ready)) for v in first_block]
 
     joined_pre, joined_got = [], []
@@ -705,41 +706,42 @@
             mask_got = after(mask_got, parts)
         mine.append(join_pieces(mask_got, m))
         other.append(swap(mine[j]))
+        if j > 0:
+            act_got = spread(jnp.concatenate(act_piece, axis=1), "cin")
         ready = reduce_back(mine[j], other[j], reduce_weight, n)
         round_got.append([round_send(ready[r], r, n, True) for r in range(n)])
-    act_got = [spread(v, "cin") for v in after(act_piece, ready)]
-
     input_gradient, input_got = [], []
+    input_wide, input_other, back_got = [], [], []
     for j in range(2):
         slope = gate_slope(joined_pre[j])
-        got = after(round_got[0], ready) if j == 0 else after(round_got[1], act_mine)
-        input_gradient.append((add_up(got) * slope).astype(BF16))
+        input_gradient.append((add_up(round_got[j]) * slope).astype(BF16))
         input_got.append(spread(input_gradient[j], "cout"))
+        got = input_got[j]
         if j > 0:
-            break
-        reduce_gradient = reduce_weight_gradient(after(joined_two, input_gradient[0]), mine, other)
-        act_got = after(act_got, reduce_gradient)
-        act_mine = [join_pieces(v, m) for v in act_got]
-    act_other = [swap(v) for v in act_mine]
-    stride_gradient = half_weight(act_mine, act_other, cot_block, SIDE)
-
-    input_wide, back_got = [], []
-    for j in range(2):
-        got = after(input_got[j], stride_gradient, *input_wide)
+            stride_gradient = half_weight(act_mine, act_other, cot_block, SIDE)
+            got = after(got, stride_gradient)
         parts, block = expand_back(got, expand_weight, m, n)
         input_wide.append(block)
         back_got.append(exchange(parts, "cin"))
-    input_other = [swap(v) for v in after(input_wide, parts)]
+        input_other.append(swap(block))
+        if j > 0:
+            break
+        reduce_gradient = reduce_weight_gradient(after(joined_two, ready), mine, other)
+        act_mine = join_pieces(after(act_got, reduce_gradient), m)
+        act_other = swap(act_mine)
+        round_got[1] = after(round_got[1], act_mine)
     expand_gradient = outer_sum([*first_block, *first_other], [*input_wide, *input_other])
     masked_first = []
     for j in range(2):
         got = after(back_got[j], expand_gradient)
         masked_first.append((add_up(got) * gate_slope(hidden[j])).astype(BF16))
     masked_block = gather(jnp.concatenate(masked_first, axis=1)[:, :pixels], "cin")
-    inner_parts, padded = conv_back(masked_block, first_kernel, SIDE, n)
+    masked_other = swap_blocks(masked_block, m)
+    inner_parts = conv_back(masked_block, first_kernel, SIDE, n)
     inner_got = exchange(inner_parts, "cout")
-    padded_other = swap(padded)
-    first_gradient = conv_weight(feature_block, feature_other, padded, padded_other, SIDE)
+    first_gradient = conv_weight(
+        feature_block, feature_other, masked_block, masked_other, SIDE
+    )
     inner_gradient = add_up(after(inner_got, first_gradient))
     outward = jnp.concatenate(input_gradient, axis=1)[:, :pixels]
     return (

time: 564 us -> 567 us (level)
  waiting for transfers between devices: 132 us -> 170 us
  starting transfers between devices: 160 us -> 134 us
    ppermute x48 -> x45, waiting for transfers between devices: 99.9 us -> 133 us  [exchange(): lax.ppermute(parts[k], name, [(i, partner(i, k, n)) for i in range(n)])]
    ppermute x13 -> x12, starting transfers between devices: 37.7 us -> 24.8 us  [swap(): return lax.ppermute(value, 'section', [(0, 1), (1, 0)])]
    ppermute x48 -> x45, starting transfers between devices: 78.8 us -> 69.9 us  [exchange(): lax.ppermute(parts[k], name, [(i, partner(i, k, n)) for i in range(n)])]
    pallas_call x17 -> x16, Pallas kernels: 76.5 us -> 74.6 us  [one_step(): pl.pallas_call(body, out_shape=outs, in_specs=[pl.BlockSpec(memory_space=...]
    unnamed x192 -> x166, local copies, waits for them, and re-layouts: 12.6 us -> 12 us
  transfers between devices with their start and end apart: 80 -> 76, of which waited for: 25 -> 28; matrix products, arithmetic and copies ran while one was open for 2% -> 1% of each run, Pallas kernels for 20% -> 22%
where the time goes in v3:
time: 567 us; the launch traced here: 561 us
  Pallas kernels  175 us (31%)
  waiting for transfers between devices  170 us (30%)
  starting transfers between devices  134 us (24%)
  blocking collectives  60.8 us (11%)
  local copies, waits for them, and re-layouts  12.1 us (2%)
  other arithmetic  7.43 us (1%)
    ppermute x45, waiting for transfers between devices, exchange(): lax.ppermute(parts[k], name, [(i, partner(i, k, n)) for i in range(n)])  133 us
    pallas_call x16, Pallas kernels, one_step(): pl.pallas_call(body, out_shape=outs, in_specs=[pl.BlockSpec(memory_space=...  74.6 us
    ppermute x45, starting transfers between devices, exchange(): lax.ppermute(parts[k], name, [(i, partner(i, k, n)) for i in range(n)])  69.9 us
    all_gather x4, blocking collectives, gather(): return lax.all_gather(shard, name, axis=0, tiled=True)  60.8 us
    ppermute x16, starting transfers between devices, round_send(): return lax.ppermute(value, ('section', 'cout'), round_pairs(r, n, back))  35.3 us
    ppermute x16, waiting for transfers between devices, round_send(): return lax.ppermute(value, ('section', 'cout'), round_pairs(r, n, back))  31 us
    pallas_call x1, Pallas kernels, conv_weight(): pl.pallas_call(functools.partial(conv_weight_body, side=side), out_shape=...  25.6 us
    ppermute x12, starting transfers between devices, swap(): return lax.ppermute(value, 'section', [(0, 1), (1, 0)])  24.8 us
  transfers between devices with their start and end apart: 76, of which 28 were waited for; matrix products, arithmetic and copies ran while one was open for 1% of the time, Pallas kernels for 22%

profile of v3, /device:TPU:0, one launch (start us, length us, event | category | flops | bytes accessed | tf_op | source)
XLA Modules:
  0.0 561.0 jit_solution(14577770666111212098)
XLA Ops:
  0.6 26.5 %all-gather = bf16[1,640,784]{2,1,0:T(8,128)(2,1)} all-gather(bf16[1,160,784]{2,1,0:T(8,128)(2,1)} %bitcast.26), channel_id=2, replica_groups=mesh['section'=2,'cin'=4,'cout'=4] {'cout'}, dimensions={1}, use_global_device_ids=true | all-gather | bytes 1254400 | tf_op jit(solution)/shard_map/all_gather | solution.py:635
  27.1 14.0 %shard_map.118 = (bf16[160,384]{1,0:T(8,128)(2,1)}, bf16[160,384]{1,0:T(8,128)(2,1)}, bf16[160,384]{1,0:T(8,128)(2,1)}, bf16[160,384]{1,0:T(8,128)(2,1)}, bf16[1...) custom-call(bf16[640,784]{1,0:T(8,128)(2,1)} %bitcast.22, ...), custom_call_target="tpu_custom_call" | custom-call | flops 6606028800 | bytes 9379840 | tf_op jit(solution)/shard_map/pallas_call | solution.py:146
  47.7 2.2 collective-permute-start.5
  51.4 2.8 collective-permute-start.1
  55.2 10.9 %all_gather.13.x_ref.refs_0_ = bf16[640,384]{1,0:T(8,128)(2,1)} all-gather(bf16[160,384]{1,0:T(8,128)(2,1)S(1)} %multiply_convert_fusion.9), channel_id=1, replica_groups=mesh['section'=2,'cin'=4,'cout'=4] {'cin'}, dimensions={0}, use_global_device_ids=true | all-gather | bytes 614400 | tf_op jit(solution)/shard_map/all_gather | solution.py:635
  66.1 3.9 shard_map.119
  71.7 5.5 collective-permute-done.2
  77.4 10.7 %all_gather.14.x_ref.refs_1_ = bf16[640,512]{1,0:T(8,128)(2,1)} all-gather(bf16[160,512]{1,0:T(8,128)(2,1)S(1)} %multiply_convert_fusion.7), channel_id=1, replica_groups=mesh['section'=2,'cin'=4,'cout'=4] {'cin'}, dimensions={0}, use_global_device_ids=true | all-gather | bytes 819200 | tf_op jit(solution)/shard_map/all_gather | solution.py:635
  88.1 4.0 shard_map.120
  92.2 24.1 %shard_map.121 = (bf16[1280,896]{1,0:T(8,128)(2,1)}, bf16[1280,896]{1,0:T(8,128)(2,1)}) custom-call(bf16[2,640,196]{2,1,0:T(8,128)(2,1)} %copy-done.16, bf16[9,1280,640]{2,1,0:T(8,128)(2,1)} %w_ref.8), custom_call_target="tpu_custom_call" | custom-call | flops 11560550400 | bytes 14745600 | tf_op jit(solution)/shard_map/pallas_call | solution.py:307
  116.3 2.0 collective-permute-start.14
  118.3 2.4 collective-permute-start.15
  120.7 8.5 %collective-permute-done.13 = bf16[320,384]{1,0:T(8,128)(2,1)S(1)} collective-permute-done((bf16[320,384]{1,0:T(8,128)(2,1)S(1)}, bf16[320,384]{1,0:T(8,128)(2,1)S(1)}, u32[]{:S(2)}, u32[]{:S(2)}) %collective-permute-start.13) | collective-permute-done | bytes 245792 | tf_op jit(solution)/shard_map/ppermute | solution.py:602
  129.5 7.2 %collective-permute-done.14 = bf16[320,384]{1,0:T(8,128)(2,1)S(1)} collective-permute-done((bf16[320,384]{1,0:T(8,128)(2,1)S(1)}, bf16[320,384]{1,0:T(8,128)(2,1)S(1)}, u32[]{:S(2)}, u32[]{:S(2)}) %collective-permute-start.14) | collective-permute-done | bytes 245792 | tf_op jit(solution)/shard_map/ppermute | solution.py:602
  139.2 3.6 collective-permute-done.27
  143.8 24.5 %collective-permute-done.28 = bf16[320,512]{1,0:T(8,128)(2,1)S(1)} collective-permute-done((bf16[320,512]{1,0:T(8,128)(2,1)S(1)}, bf16[320,512]{1,0:T(8,128)(2,1)S(1)}, u32[]{:S(2)}, u32[]{:S(2)}) %collective-permute-start.28) | collective-permute-done | bytes 327712 | tf_op jit(solution)/shard_map/ppermute | solution.py:602
  170.3 2.0 collective-permute-start.19
  172.2 9.5 %collective-permute-start.34 = (bf16[4,160,784]{2,1,0:T(8,128)(2,1)S(1)}, bf16[4,160,784]{2,1,0:T(8,128)(2,1)}, u32[]{:S(2)}, u32[]{:S(2)}) collective-permute-start(bf16[4,160,784]{2,1,0:T(8,128)(2,1)S(1)} %bitcast.24), channel_id=1, source_target_pairs={{0,16},{16,0},{1,17},{17,1},{2,18},{18,2},{3,19},{19,3},{4,20},{20... | collective-permute-start | bytes 3010568 | tf_op jit(solution)/shard_map/ppermute | solution.py:587
  181.8 4.5 shard_map.122
  188.7 6.2 %shard_map.123 = (bf16[2,640,384]{2,1,0:T(8,128)(2,1)}, bf16[1280,384]{1,0:T(8,128)(2,1)}, bf16[1280,384]{1,0:T(8,128)(2,1)}) custom-call(bf16[320,384]{1,0:T(8,128)(2,1)} %copy-done.76, bf16[320,384]{1,0:T(8,128)(2,1)} %copy-done.77, bf16[320,384]{1,0:T(8,128)(2,1)} %copy-done.78, bf16[320,384]{1,0:T(8,128)(2,1)} %copy-done.79, bf16[640,1280]{1,0:T(8,128)(2,1)} %refs_2_.3), custom_call_target="tpu_custom_call" | custom-call | flops 1258291200 | bytes 5570560 | tf_op jit(solution)/shard_map/pallas_call | solution.py:79
  195.9 3.1 collective-permute-start.31
  199.0 5.4 collective-permute-start.32
  204.5 4.7 collective-permute-start.36
  209.2 7.3 %collective-permute-start.35 = (bf16[640,384]{1,0:T(8,128)(2,1)S(1)}, bf16[640,384]{1,0:T(8,128)(2,1)}, u32[]{:S(2)}, u32[]{:S(2)}) collective-permute-start(bf16[640,384]{1,0:T(8,128)(2,1)S(1)} %copy-done.29), channel_id=1, source_target_pairs={{0,16},{16,0},{1,17},{17,1},{2,18},{18,2},{3,19},{19,3},{4,20},{20... | collective-permute-start | bytes 1474568 | tf_op jit(solution)/shard_map/ppermute | solution.py:587
  216.5 7.8 %collective-permute-start.33 = (bf16[320,512]{1,0:T(8,128)(2,1)S(1)}, bf16[320,512]{1,0:T(8,128)(2,1)S(1)}, u32[]{:S(2)}, u32[]{:S(2)}) collective-permute-start(bf16[320,512]{1,0:T(8,128)(2,1)S(1)} %multiply_convert_fusion.2), channel_id=1, source_target_pairs={{0,3},{1,2},{2,17},{3,16},{16,1},{17,0},{18,19},{19,18},{4,7},{5,6... | collective-permute-start | bytes 983048 | tf_op jit(solution)/shard_map/ppermute | solution.py:410
  224.3 6.5 %collective-permute-done.33.refs_3_ = bf16[320,512]{1,0:T(8,128)(2,1)S(1)} collective-permute-done((bf16[320,512]{1,0:T(8,128)(2,1)S(1)}, bf16[320,512]{1,0:T(8,128)(2,1)S(1)}, u32[]{:S(2)}, u32[]{:S(2)}) %collective-permute-start.33) | collective-permute-done | bytes 327712 | tf_op jit(solution)/shard_map/ppermute | solution.py:410
  233.1 2.8 shard_map.124
  237.4 6.5 %shard_map.125 = (bf16[2,640,512]{2,1,0:T(8,128)(2,1)}, bf16[1280,512]{1,0:T(8,128)(2,1)}, bf16[1280,512]{1,0:T(8,128)(2,1)}) custom-call(bf16[320,512]{1,0:T(8,128)(2,1)} %copy-done.52, bf16[320,512]{1,0:T(8,128)(2,1)} %copy-done.54, bf16[320,512]{1,0:T(8,128)(2,1)} %copy-done.55, bf16[320,512]{1,0:T(8,128)(2,1)} %copy-done.65, bf16[640,1280]{1,0:T(8,128)(2,1)} %refs_2_.3), custom_call_target="tpu_custom_call" | custom-call | flops 1677721600 | bytes 6881280 | tf_op jit(solution)/shard_map/pallas_call | solution.py:79
  249.9 9.1 %collective-permute-done.12 = bf16[320,896]{1,0:T(8,128)(2,1)} collective-permute-done((bf16[320,896]{1,0:T(8,128)(2,1)}, bf16[320,896]{1,0:T(8,128)(2,1)}, u32[]{:S(2)}, u32[]{:S(2)}) %collective-permute-start.12) | collective-permute-done | bytes 573472 | tf_op jit(solution)/shard_map/ppermute | solution.py:602
  260.5 2.8 collective-permute-done.21
  263.3 3.1 collective-permute-done.22
  266.4 3.1 collective-permute-done.23
  274.4 3.3 shard_map.126
  278.3 6.1 %collective-permute-done.25.refs_2_ = bf16[320,384]{1,0:T(8,128)(2,1)S(1)} collective-permute-done((bf16[320,384]{1,0:T(8,128)(2,1)S(1)}, bf16[320,384]{1,0:T(8,128)(2,1)S(1)}, u32[]{:S(2)}, u32[]{:S(2)}) %collective-permute-start.25) | collective-permute-done | bytes 245792 | tf_op jit(solution)/shard_map/ppermute | solution.py:602
  285.1 2.5 shard_map.127.refs_0_.refs_2_
  292.2 4.8 shard_map.128
  299.5 6.4 %collective-permute-done.51 = bf16[320,512]{1,0:T(8,128)(2,1)S(1)} collective-permute-done((bf16[320,512]{1,0:T(8,128)(2,1)S(1)}, bf16[320,512]{1,0:T(8,128)(2,1)S(1)}, u32[]{:S(2)}, u32[]{:S(2)}) %collective-permute-start.51) | collective-permute-done | bytes 327712 | tf_op jit(solution)/shard_map/ppermute | solution.py:602
  309.9 7.1 %collective-permute-done.52.refs_1_ = bf16[320,512]{1,0:T(8,128)(2,1)S(1)} collective-permute-done((bf16[320,512]{1,0:T(8,128)(2,1)S(1)}, bf16[320,512]{1,0:T(8,128)(2,1)S(1)}, u32[]{:S(2)}, u32[]{:S(2)}) %collective-permute-start.52) | collective-permute-done | bytes 327712 | tf_op jit(solution)/shard_map/ppermute | solution.py:602
  317.0 5.8 %collective-permute-done.53.refs_2_ = bf16[320,512]{1,0:T(8,128)(2,1)S(1)} collective-permute-done((bf16[320,512]{1,0:T(8,128)(2,1)S(1)}, bf16[320,512]{1,0:T(8,128)(2,1)S(1)}, u32[]{:S(2)}, u32[]{:S(2)}) %collective-permute-start.53) | collective-permute-done | bytes 327712 | tf_op jit(solution)/shard_map/ppermute | solution.py:602
  324.3 2.5 shard_map.130.refs_0_.refs_3_
  331.4 5.0 shard_map.131
  336.4 8.6 %shard_map.132 = f32[640,1280]{1,0:T(8,128)} custom-call(bf16[2,640,384]{2,1,0:T(8,128)(2,1)} %get-tuple-element.213.refs_0_, bf16[2,640,512]{2,1,0:T(8,128)(2,1)} %get-tuple-element.214.refs_1_, bf16[1280,384]{1,0:T(8,128)(2,1)} %shard_map.127.refs_0_.refs_2_, bf16[1280,512]{1,0:T(8,128)(2,1)} %shard_map.130.refs_0_.refs_3_, bf16[1280,384]{1,0:T(8,128)(2,1)} %copy-done.49, ...), custom_call_target="tpu_custom_call" | custom-call | flops 2936012800 | bytes 10158080 | tf_op jit(solution)/shard_map/pallas_call | solution.py:79
  345.1 10.7 %collective-permute-done.61.refs_2_ = bf16[320,896]{1,0:T(8,128)(2,1)S(1)} collective-permute-done((bf16[320,896]{1,0:T(8,128)(2,1)S(1)}, bf16[320,896]{1,0:T(8,128)(2,1)S(1)}, u32[]{:S(2)}, u32[]{:S(2)}) %collective-permute-start.61) | collective-permute-done | bytes 573472 | tf_op jit(solution)/shard_map/ppermute | solution.py:602
  357.4 3.3 shard_map.133.refs_0_
  362.5 2.7 collective-permute-start.58
  365.2 3.7 collective-permute-start.59
  370.5 21.3 %collective-permute-done.58 = bf16[320,512]{1,0:T(8,128)(2,1)S(1)} collective-permute-done((bf16[320,512]{1,0:T(8,128)(2,1)S(1)}, bf16[320,512]{1,0:T(8,128)(2,1)S(1)}, u32[]{:S(2)}, u32[]{:S(2)}) %collective-permute-start.58) | collective-permute-done | bytes 327712 | tf_op jit(solution)/shard_map/ppermute | solution.py:410
  392.4 4.1 collective-permute-start.63
  399.2 7.0 %collective-permute-done.63.refs_1_ = bf16[320,512]{1,0:T(8,128)(2,1)S(1)} collective-permute-done((bf16[320,512]{1,0:T(8,128)(2,1)S(1)}, bf16[320,512]{1,0:T(8,128)(2,1)S(1)}, u32[]{:S(2)}, u32[]{:S(2)}) %collective-permute-start.63) | collective-permute-done | bytes 327712 | tf_op jit(solution)/shard_map/ppermute | solution.py:602
  406.2 1.9 collective-permute-start.41
  408.1 3.6 collective-permute-done.64.refs_2_
  411.7 11.6 %collective-permute-start.65 = (bf16[320,512]{1,0:T(8,128)(2,1)S(1)}, bf16[320,512]{1,0:T(8,128)(2,1)S(1)}, u32[]{:S(2)}, u32[]{:S(2)}) collective-permute-start(bf16[320,512]{1,0:T(8,128)(2,1)S(1)} %multiply_convert_fusion.refs_0_), channel_id=1, source_target_pairs={{0,3},{1,2},{2,1},{3,0},{4,7},{5,6},{6,5},{7,4},{8,11},{9,10},{10,... | collective-permute-start | bytes 983048 | tf_op jit(solution)/shard_map/ppermute | solution.py:602
  423.3 22.8 %shard_map.134 = f32[9,1280,640]{2,1,0:T(8,128)} custom-call(bf16[1280,896]{1,0:T(8,128)(2,1)} %shard_map.133.refs_0_, bf16[1280,896]{1,0:T(8,128)(2,1)} %copy-done.45, bf16[2,640,196]{2,1,0:T(8,128)(2,1)} %copy-done.16), custom_call_target="tpu_custom_call" | custom-call | flops 11560550400 | bytes 29491200 | tf_op jit(solution)/shard_map/pallas_call | solution.py:355
  446.8 4.3 shard_map.135
  453.1 2.7 collective-permute-start.44
  457.4 8.0 %collective-permute-done.43.refs_1_ = bf16[320,384]{1,0:T(8,128)(2,1)S(1)} collective-permute-done((bf16[320,384]{1,0:T(8,128)(2,1)S(1)}, bf16[320,384]{1,0:T(8,128)(2,1)S(1)}, u32[]{:S(2)}, u32[]{:S(2)}) %collective-permute-start.43) | collective-permute-done | bytes 245792 | tf_op jit(solution)/shard_map/ppermute | solution.py:602
  465.5 8.0 %collective-permute-done.44.refs_2_ = bf16[320,384]{1,0:T(8,128)(2,1)S(1)} collective-permute-done((bf16[320,384]{1,0:T(8,128)(2,1)S(1)}, bf16[320,384]{1,0:T(8,128)(2,1)S(1)}, u32[]{:S(2)}, u32[]{:S(2)}) %collective-permute-start.44) | collective-permute-done | bytes 245792 | tf_op jit(solution)/shard_map/ppermute | solution.py:602
  474.9 4.2 shard_map.129
  482.6 2.9 collective-permute-done.46
  489.1 8.3 %shard_map.136 = f32[640,1280]{1,0:T(8,128)} custom-call(bf16[640,384]{1,0:T(8,128)(2,1)} %all_gather.13.x_ref.refs_0_, bf16[640,512]{1,0:T(8,128)(2,1)} %all_gather.14.x_ref.refs_1_, bf16[640,384]{1,0:T(8,128)(2,1)} %collective-permute-done.35.refs_2_, bf16[640,512]{1,0:T(8,128)(2,1)} %copy-done.51, bf16[1280,384]{1,0:T(8,128)(2,1)} %get-tuple-element.202.refs_4_, ...), custom_call_target="tpu_custom_call" | custom-call | flops 2936012800 | bytes 10158080 | tf_op jit(solution)/shard_map/pallas_call | solution.py:79
  498.8 12.8 %all_gather.15.m_ref.ma_ref = bf16[640,784]{1,0:T(8,128)(2,1)S(1)} all-gather(bf16[160,784]{1,0:T(8,128)(2,1)S(1)} %pad_maximum_fusion.2), channel_id=1, replica_groups=mesh['section'=2,'cin'=4,'cout'=4] {'cin'}, dimensions={0}, use_global_device_ids=true | all-gather | bytes 1254400 | tf_op jit(solution)/shard_map/all_gather | solution.py:635
  512.8 13.8 %shard_map.137 = (bf16[160,784]{1,0:T(8,128)(2,1)}, bf16[160,784]{1,0:T(8,128)(2,1)}, bf16[160,784]{1,0:T(8,128)(2,1)}, bf16[160,784]{1,0:T(8,128)(2,1)}) custom-call(bf16[640,784]{1,0:T(8,128)(2,1)} %copy-done.11, bf16[9,640,640]{2,1,0:T(8,128)(2,1)} %w_ref.9), custom_call_target="tpu_custom_call" | custom-call | flops 6606028800 | bytes 9666560 | tf_op jit(solution)/shard_map/pallas_call | solution.py:191
  526.6 4.2 collective-permute-start.72
  534.2 25.6 %shard_map.138 = f32[9,640,640]{2,1,0:T(8,128)} custom-call(bf16[640,784]{1,0:T(8,128)(2,1)} %bitcast.23, bf16[640,784]{1,0:T(8,128)(2,1)} %bitcast.7.xb_ref, bf16[640,784]{1,0:T(8,128)(2,1)} %copy-done.11, bf16[640,784]{1,0:T(8,128)(2,1)} %bitcast.31), custom_call_target="tpu_custom_call" | custom-call | flops 13212057600 | bytes 14745600 | tf_op jit(solution)/shard_map/pallas_call | solution.py:232
  (299 shorter events, 82.5 us)
Async XLA Ops:
  44.6 32.6 %collective-permute-start.3 = (bf16[160,512]{1,0:T(8,128)(2,1)}, bf16[160,512]{1,0:T(8,128)(2,1)S(1)}, u32[]{:S(2)}, u32[]{:S(2)}) collective-permute-start(bf16[160,512]{1,0:T(8,128)(2,1)} %get-tuple-element.132), channel_id=1, source_target_pairs={{0,4},{4,0},{8,12},{12,8},{1,5},{5,1},{9,13},{13,9},{2,6},{6,2},{1... | collective-permute-start | bytes 491528 | tf_op jit(solution)/shard_map/ppermute | solution.py:602
  46.1 31.2 %collective-permute-start.4 = (bf16[160,512]{1,0:T(8,128)(2,1)}, bf16[160,512]{1,0:T(8,128)(2,1)S(1)}, u32[]{:S(2)}, u32[]{:S(2)}) collective-permute-start(bf16[160,512]{1,0:T(8,128)(2,1)} %get-tuple-element.133), channel_id=1, source_target_pairs={{0,8},{4,12},{8,0},{12,4},{1,9},{5,13},{9,1},{13,5},{2,10},{6,14},... | collective-permute-start | bytes 491528 | tf_op jit(solution)/shard_map/ppermute | solution.py:602
  47.7 29.5 %collective-permute-start.5 = (bf16[160,512]{1,0:T(8,128)(2,1)}, bf16[160,512]{1,0:T(8,128)(2,1)S(1)}, u32[]{:S(2)}, u32[]{:S(2)}) collective-permute-start(bf16[160,512]{1,0:T(8,128)(2,1)} %get-tuple-element.134), channel_id=1, source_target_pairs={{0,12},{4,8},{8,4},{12,0},{1,13},{5,9},{9,5},{13,1},{2,14},{6,10},... | collective-permute-start | bytes 491528 | tf_op jit(solution)/shard_map/ppermute | solution.py:602
  51.3 18.7 %collective-permute-start = (bf16[2,160,196]{2,1,0:T(8,128)(2,1)S(1)}, bf16[2,160,196]{2,1,0:T(8,128)(2,1)S(1)}, u32[]{:S(2)}, u32[]{:S(2)}) collective-permute-start(bf16[2,160,196]{2,1,0:T(8,128)(2,1)S(1)} %bitcast.28), channel_id=1, source_target_pairs={{0,1},{1,0},{2,3},{3,2},{4,5},{5,4},{6,7},{7,6},{8,9},{9,8},{10,11... | collective-permute-start | bytes 376328 | tf_op jit(solution)/shard_map/ppermute | solution.py:629
  51.4 20.2 %collective-permute-start.1 = (bf16[2,160,196]{2,1,0:T(8,128)(2,1)S(1)}, bf16[2,160,196]{2,1,0:T(8,128)(2,1)S(1)}, u32[]{:S(2)}, u32[]{:S(2)}) collective-permute-start(bf16[2,160,196]{2,1,0:T(8,128)(2,1)S(1)} %bitcast.29), channel_id=1, source_target_pairs={{0,2},{1,3},{2,0},{3,1},{4,6},{5,7},{6,4},{7,5},{8,10},{9,11},{10,... | collective-permute-start | bytes 376328 | tf_op jit(solution)/shard_map/ppermute | solution.py:629
  116.2 56.0 %collective-permute-start.9 = (bf16[1280,896]{1,0:T(8,128)(2,1)}, bf16[1280,896]{1,0:T(8,128)(2,1)S(1)}, u32[]{:S(2)}, u32[]{:S(2)}) collective-permute-start(bf16[1280,896]{1,0:T(8,128)(2,1)} %get-tuple-element.150), channel_id=1, source_target_pairs={{0,16},{16,0},{1,17},{17,1},{2,18},{18,2},{3,19},{19,3},{4,20},{20... | collective-permute-start | bytes 6881288 | tf_op jit(solution)/shard_map/ppermute | solution.py:587
  116.2 12.9 %collective-permute-start.13 = (bf16[320,384]{1,0:T(8,128)(2,1)S(1)}, bf16[320,384]{1,0:T(8,128)(2,1)S(1)}, u32[]{:S(2)}, u32[]{:S(2)}) collective-permute-start(bf16[320,384]{1,0:T(8,128)(2,1)S(1)} %copy-done.73), channel_id=1, source_target_pairs={{0,1},{1,0},{2,3},{3,2},{4,5},{5,4},{6,7},{7,6},{8,9},{9,8},{10,11... | collective-permute-start | bytes 737288 | tf_op jit(solution)/shard_map/ppermute | solution.py:602
  116.3 20.4 %collective-permute-start.14 = (bf16[320,384]{1,0:T(8,128)(2,1)S(1)}, bf16[320,384]{1,0:T(8,128)(2,1)S(1)}, u32[]{:S(2)}, u32[]{:S(2)}) collective-permute-start(bf16[320,384]{1,0:T(8,128)(2,1)S(1)} %copy-done.72), channel_id=1, source_target_pairs={{0,2},{1,3},{2,0},{3,1},{4,6},{5,7},{6,4},{7,5},{8,10},{9,11},{10,... | collective-permute-start | bytes 737288 | tf_op jit(solution)/shard_map/ppermute | solution.py:602
  118.3 19.9 %collective-permute-start.15 = (bf16[320,384]{1,0:T(8,128)(2,1)S(1)}, bf16[320,384]{1,0:T(8,128)(2,1)S(1)}, u32[]{:S(2)}, u32[]{:S(2)}) collective-permute-start(bf16[320,384]{1,0:T(8,128)(2,1)S(1)} %copy-done.71), channel_id=1, source_target_pairs={{0,3},{1,2},{2,1},{3,0},{4,7},{5,6},{6,5},{7,4},{8,11},{9,10},{10,... | collective-permute-start | bytes 737288 | tf_op jit(solution)/shard_map/ppermute | solution.py:602
  120.7 22.0 %collective-permute-start.27 = (bf16[320,512]{1,0:T(8,128)(2,1)S(1)}, bf16[320,512]{1,0:T(8,128)(2,1)S(1)}, u32[]{:S(2)}, u32[]{:S(2)}) collective-permute-start(bf16[320,512]{1,0:T(8,128)(2,1)S(1)} %copy-done.58), channel_id=1, source_target_pairs={{0,1},{1,0},{2,3},{3,2},{4,5},{5,4},{6,7},{7,6},{8,9},{9,8},{10,11... | collective-permute-start | bytes 983048 | tf_op jit(solution)/shard_map/ppermute | solution.py:602
  129.2 39.2 %collective-permute-start.28 = (bf16[320,512]{1,0:T(8,128)(2,1)S(1)}, bf16[320,512]{1,0:T(8,128)(2,1)S(1)}, u32[]{:S(2)}, u32[]{:S(2)}) collective-permute-start(bf16[320,512]{1,0:T(8,128)(2,1)S(1)} %copy-done.56), channel_id=1, source_target_pairs={{0,2},{1,3},{2,0},{3,1},{4,6},{5,7},{6,4},{7,5},{8,10},{9,11},{10,... | collective-permute-start | bytes 983048 | tf_op jit(solution)/shard_map/ppermute | solution.py:602
  136.8 33.5 %collective-permute-start.29 = (bf16[320,512]{1,0:T(8,128)(2,1)S(1)}, bf16[320,512]{1,0:T(8,128)(2,1)S(1)}, u32[]{:S(2)}, u32[]{:S(2)}) collective-permute-start(bf16[320,512]{1,0:T(8,128)(2,1)S(1)} %copy-done.53), channel_id=1, source_target_pairs={{0,3},{1,2},{2,1},{3,0},{4,7},{5,6},{6,5},{7,4},{8,11},{9,10},{10,... | collective-permute-start | bytes 983048 | tf_op jit(solution)/shard_map/ppermute | solution.py:602
  138.5 47.9 %collective-permute-start.16 = (bf16[320,384]{1,0:T(8,128)(2,1)S(1)}, bf16[320,384]{1,0:T(8,128)(2,1)S(1)}, u32[]{:S(2)}, u32[]{:S(2)}) collective-permute-start(bf16[320,384]{1,0:T(8,128)(2,1)S(1)} %multiply_convert_fusion.5), channel_id=1, source_target_pairs={{0,0},{1,1},{2,18},{3,19},{16,2},{17,3},{18,16},{19,17},{4,4},{5,5... | collective-permute-start | bytes 737288 | tf_op jit(solution)/shard_map/ppermute | solution.py:410
  142.8 43.6 %collective-permute-start.17 = (bf16[320,384]{1,0:T(8,128)(2,1)S(1)}, bf16[320,384]{1,0:T(8,128)(2,1)S(1)}, u32[]{:S(2)}, u32[]{:S(2)}) collective-permute-start(bf16[320,384]{1,0:T(8,128)(2,1)S(1)} %multiply_convert_fusion.5), channel_id=1, source_target_pairs={{0,1},{1,0},{2,19},{3,18},{16,3},{17,2},{18,17},{19,16},{4,5},{5,4... | collective-permute-start | bytes 737288 | tf_op jit(solution)/shard_map/ppermute | solution.py:410
  168.4 18.0 %collective-permute-start.18 = (bf16[320,384]{1,0:T(8,128)(2,1)S(1)}, bf16[320,384]{1,0:T(8,128)(2,1)S(1)}, u32[]{:S(2)}, u32[]{:S(2)}) collective-permute-start(bf16[320,384]{1,0:T(8,128)(2,1)S(1)} %multiply_convert_fusion.5), channel_id=1, source_target_pairs={{0,2},{1,3},{2,16},{3,17},{16,0},{17,1},{18,18},{19,19},{4,6},{5,7... | collective-permute-start | bytes 737288 | tf_op jit(solution)/shard_map/ppermute | solution.py:410
  170.3 17.7 %collective-permute-start.19 = (bf16[320,384]{1,0:T(8,128)(2,1)S(1)}, bf16[320,384]{1,0:T(8,128)(2,1)S(1)}, u32[]{:S(2)}, u32[]{:S(2)}) collective-permute-start(bf16[320,384]{1,0:T(8,128)(2,1)S(1)} %multiply_convert_fusion.5), channel_id=1, source_target_pairs={{0,3},{1,2},{2,17},{3,16},{16,1},{17,0},{18,19},{19,18},{4,7},{5,6... | collective-permute-start | bytes 737288 | tf_op jit(solution)/shard_map/ppermute | solution.py:410
  172.2 65.1 %collective-permute-start.34 = (bf16[4,160,784]{2,1,0:T(8,128)(2,1)S(1)}, bf16[4,160,784]{2,1,0:T(8,128)(2,1)}, u32[]{:S(2)}, u32[]{:S(2)}) collective-permute-start(bf16[4,160,784]{2,1,0:T(8,128)(2,1)S(1)} %bitcast.24), channel_id=1, source_target_pairs={{0,16},{16,0},{1,17},{17,1},{2,18},{18,2},{3,19},{19,3},{4,20},{20... | collective-permute-start | bytes 3010568 | tf_op jit(solution)/shard_map/ppermute | solution.py:587
  194.9 37.2 %collective-permute-start.20 = (bf16[1280,384]{1,0:T(8,128)(2,1)}, bf16[1280,384]{1,0:T(8,128)(2,1)S(1)}, u32[]{:S(2)}, u32[]{:S(2)}) collective-permute-start(bf16[1280,384]{1,0:T(8,128)(2,1)} %get-tuple-element.164), channel_id=1, source_target_pairs={{0,16},{16,0},{1,17},{17,1},{2,18},{18,2},{3,19},{19,3},{4,20},{20... | collective-permute-start | bytes 2949128 | tf_op jit(solution)/shard_map/ppermute | solution.py:587
  195.9 13.2 %collective-permute-start.31 = (bf16[320,512]{1,0:T(8,128)(2,1)S(1)}, bf16[320,512]{1,0:T(8,128)(2,1)S(1)}, u32[]{:S(2)}, u32[]{:S(2)}) collective-permute-start(bf16[320,512]{1,0:T(8,128)(2,1)S(1)} %multiply_convert_fusion.2), channel_id=1, source_target_pairs={{0,1},{1,0},{2,19},{3,18},{16,3},{17,2},{18,17},{19,16},{4,5},{5,4... | collective-permute-start | bytes 983048 | tf_op jit(solution)/shard_map/ppermute | solution.py:410
  199.0 17.5 %collective-permute-start.32 = (bf16[320,512]{1,0:T(8,128)(2,1)S(1)}, bf16[320,512]{1,0:T(8,128)(2,1)S(1)}, u32[]{:S(2)}, u32[]{:S(2)}) collective-permute-start(bf16[320,512]{1,0:T(8,128)(2,1)S(1)} %multiply_convert_fusion.2), channel_id=1, source_target_pairs={{0,2},{1,3},{2,16},{3,17},{16,0},{17,1},{18,18},{19,19},{4,6},{5,7... | collective-permute-start | bytes 983048 | tf_op jit(solution)/shard_map/ppermute | solution.py:410
  204.5 32.9 %collective-permute-start.36 = (bf16[640,512]{1,0:T(8,128)(2,1)S(1)}, bf16[640,512]{1,0:T(8,128)(2,1)S(1)}, u32[]{:S(2)}, u32[]{:S(2)}) collective-permute-start(bf16[640,512]{1,0:T(8,128)(2,1)S(1)} %copy-done.15), channel_id=1, source_target_pairs={{0,16},{16,0},{1,17},{17,1},{2,18},{18,2},{3,19},{19,3},{4,20},{20... | collective-permute-start | bytes 1966088 | tf_op jit(solution)/shard_map/ppermute | solution.py:587
  209.2 26.7 %collective-permute-start.35 = (bf16[640,384]{1,0:T(8,128)(2,1)S(1)}, bf16[640,384]{1,0:T(8,128)(2,1)}, u32[]{:S(2)}, u32[]{:S(2)}) collective-permute-start(bf16[640,384]{1,0:T(8,128)(2,1)S(1)} %copy-done.29), channel_id=1, source_target_pairs={{0,16},{16,0},{1,17},{17,1},{2,18},{18,2},{3,19},{19,3},{4,20},{20... | collective-permute-start | bytes 1474568 | tf_op jit(solution)/shard_map/ppermute | solution.py:587
  216.5 14.3 %collective-permute-start.33 = (bf16[320,512]{1,0:T(8,128)(2,1)S(1)}, bf16[320,512]{1,0:T(8,128)(2,1)S(1)}, u32[]{:S(2)}, u32[]{:S(2)}) collective-permute-start(bf16[320,512]{1,0:T(8,128)(2,1)S(1)} %multiply_convert_fusion.2), channel_id=1, source_target_pairs={{0,3},{1,2},{2,17},{3,16},{16,1},{17,0},{18,19},{19,18},{4,7},{5,6... | collective-permute-start | bytes 983048 | tf_op jit(solution)/shard_map/ppermute | solution.py:410
  230.8 15.5 %collective-permute-start.10 = (bf16[320,896]{1,0:T(8,128)(2,1)}, bf16[320,896]{1,0:T(8,128)(2,1)S(1)}, u32[]{:S(2)}, u32[]{:S(2)}) collective-permute-start(bf16[320,896]{1,0:T(8,128)(2,1)} %get-tuple-element.152), channel_id=1, source_target_pairs={{0,4},{4,0},{8,12},{12,8},{1,5},{5,1},{9,13},{13,9},{2,6},{6,2},{1... | collective-permute-start | bytes 1720328 | tf_op jit(solution)/shard_map/ppermute | solution.py:602
  232.1 16.3 %collective-permute-start.11 = (bf16[320,896]{1,0:T(8,128)(2,1)}, bf16[320,896]{1,0:T(8,128)(2,1)}, u32[]{:S(2)}, u32[]{:S(2)}) collective-permute-start(bf16[320,896]{1,0:T(8,128)(2,1)} %get-tuple-element.153), channel_id=1, source_target_pairs={{0,8},{4,12},{8,0},{12,4},{1,9},{5,13},{9,1},{13,5},{2,10},{6,14},... | collective-permute-start | bytes 1720328 | tf_op jit(solution)/shard_map/ppermute | solution.py:602
  235.9 23.1 %collective-permute-start.12 = (bf16[320,896]{1,0:T(8,128)(2,1)}, bf16[320,896]{1,0:T(8,128)(2,1)}, u32[]{:S(2)}, u32[]{:S(2)}) collective-permute-start(bf16[320,896]{1,0:T(8,128)(2,1)} %get-tuple-element.154), channel_id=1, source_target_pairs={{0,12},{4,8},{8,4},{12,0},{1,13},{5,9},{9,5},{13,1},{2,14},{6,10},... | collective-permute-start | bytes 1720328 | tf_op jit(solution)/shard_map/ppermute | solution.py:602
  243.9 29.4 %collective-permute-start.37 = (bf16[1280,512]{1,0:T(8,128)(2,1)}, bf16[1280,512]{1,0:T(8,128)(2,1)S(1)}, u32[]{:S(2)}, u32[]{:S(2)}) collective-permute-start(bf16[1280,512]{1,0:T(8,128)(2,1)} %get-tuple-element.185), channel_id=1, source_target_pairs={{0,16},{16,0},{1,17},{17,1},{2,18},{18,2},{3,19},{19,3},{4,20},{20... | collective-permute-start | bytes 3932168 | tf_op jit(solution)/shard_map/ppermute | solution.py:587
  245.4 17.8 %collective-permute-start.21 = (bf16[320,384]{1,0:T(8,128)(2,1)}, bf16[320,384]{1,0:T(8,128)(2,1)S(1)}, u32[]{:S(2)}, u32[]{:S(2)}) collective-permute-start(bf16[320,384]{1,0:T(8,128)(2,1)} %get-tuple-element.166), channel_id=1, source_target_pairs={{0,4},{4,0},{8,12},{12,8},{1,5},{5,1},{9,13},{13,9},{2,6},{6,2},{1... | collective-permute-start | bytes 737288 | tf_op jit(solution)/shard_map/ppermute | solution.py:602
  246.3 20.1 %collective-permute-start.22 = (bf16[320,384]{1,0:T(8,128)(2,1)S(1)}, bf16[320,384]{1,0:T(8,128)(2,1)S(1)}, u32[]{:S(2)}, u32[]{:S(2)}) collective-permute-start(bf16[320,384]{1,0:T(8,128)(2,1)S(1)} %copy-done.75), channel_id=1, source_target_pairs={{0,8},{4,12},{8,0},{12,4},{1,9},{5,13},{9,1},{13,5},{2,10},{6,14},... | collective-permute-start | bytes 737288 | tf_op jit(solution)/shard_map/ppermute | solution.py:602
  248.4 21.1 %collective-permute-start.23 = (bf16[320,384]{1,0:T(8,128)(2,1)S(1)}, bf16[320,384]{1,0:T(8,128)(2,1)S(1)}, u32[]{:S(2)}, u32[]{:S(2)}) collective-permute-start(bf16[320,384]{1,0:T(8,128)(2,1)S(1)} %copy-done.74), channel_id=1, source_target_pairs={{0,12},{4,8},{8,4},{12,0},{1,13},{5,9},{9,5},{13,1},{2,14},{6,10},... | collective-permute-start | bytes 737288 | tf_op jit(solution)/shard_map/ppermute | solution.py:602
  270.5 13.8 %collective-permute-start.25 = (bf16[320,384]{1,0:T(8,128)(2,1)S(1)}, bf16[320,384]{1,0:T(8,128)(2,1)S(1)}, u32[]{:S(2)}, u32[]{:S(2)}) collective-permute-start(bf16[320,384]{1,0:T(8,128)(2,1)S(1)} %get-tuple-element.190.refs_0_), channel_id=1, source_target_pairs={{0,8},{4,12},{8,0},{12,4},{1,9},{5,13},{9,1},{13,5},{2,10},{6,14},... | collective-permute-start | bytes 737288 | tf_op jit(solution)/shard_map/ppermute | solution.py:602
  271.9 12.4 %collective-permute-start.26 = (bf16[320,384]{1,0:T(8,128)(2,1)S(1)}, bf16[320,384]{1,0:T(8,128)(2,1)S(1)}, u32[]{:S(2)}, u32[]{:S(2)}) collective-permute-start(bf16[320,384]{1,0:T(8,128)(2,1)S(1)} %get-tuple-element.190.refs_0_), channel_id=1, source_target_pairs={{0,12},{4,8},{8,4},{12,0},{1,13},{5,9},{9,5},{13,1},{2,14},{6,10},... | collective-permute-start | bytes 737288 | tf_op jit(solution)/shard_map/ppermute | solution.py:602
  287.7 10.8 %collective-permute-start.49 = (bf16[320,512]{1,0:T(8,128)(2,1)}, bf16[320,512]{1,0:T(8,128)(2,1)S(1)}, u32[]{:S(2)}, u32[]{:S(2)}) collective-permute-start(bf16[320,512]{1,0:T(8,128)(2,1)} %get-tuple-element.187), channel_id=1, source_target_pairs={{0,4},{4,0},{8,12},{12,8},{1,5},{5,1},{9,13},{13,9},{2,6},{6,2},{1... | collective-permute-start | bytes 983048 | tf_op jit(solution)/shard_map/ppermute | solution.py:602
  289.2 10.3 %collective-permute-start.50 = (bf16[320,512]{1,0:T(8,128)(2,1)S(1)}, bf16[320,512]{1,0:T(8,128)(2,1)S(1)}, u32[]{:S(2)}, u32[]{:S(2)}) collective-permute-start(bf16[320,512]{1,0:T(8,128)(2,1)S(1)} %copy-done.62), channel_id=1, source_target_pairs={{0,8},{4,12},{8,0},{12,4},{1,9},{5,13},{9,1},{13,5},{2,10},{6,14},... | collective-permute-start | bytes 983048 | tf_op jit(solution)/shard_map/ppermute | solution.py:602
  289.7 16.2 %collective-permute-start.51 = (bf16[320,512]{1,0:T(8,128)(2,1)S(1)}, bf16[320,512]{1,0:T(8,128)(2,1)S(1)}, u32[]{:S(2)}, u32[]{:S(2)}) collective-permute-start(bf16[320,512]{1,0:T(8,128)(2,1)S(1)} %copy-done.60), channel_id=1, source_target_pairs={{0,12},{4,8},{8,4},{12,0},{1,13},{5,9},{9,5},{13,1},{2,14},{6,10},... | collective-permute-start | bytes 983048 | tf_op jit(solution)/shard_map/ppermute | solution.py:602
  306.4 10.7 %collective-permute-start.52 = (bf16[320,512]{1,0:T(8,128)(2,1)S(1)}, bf16[320,512]{1,0:T(8,128)(2,1)S(1)}, u32[]{:S(2)}, u32[]{:S(2)}) collective-permute-start(bf16[320,512]{1,0:T(8,128)(2,1)S(1)} %get-tuple-element.249.refs_0_), channel_id=1, source_target_pairs={{0,4},{4,0},{8,12},{12,8},{1,5},{5,1},{9,13},{13,9},{2,6},{6,2},{1... | collective-permute-start | bytes 983048 | tf_op jit(solution)/shard_map/ppermute | solution.py:602
  307.0 15.8 %collective-permute-start.53 = (bf16[320,512]{1,0:T(8,128)(2,1)S(1)}, bf16[320,512]{1,0:T(8,128)(2,1)S(1)}, u32[]{:S(2)}, u32[]{:S(2)}) collective-permute-start(bf16[320,512]{1,0:T(8,128)(2,1)S(1)} %get-tuple-element.249.refs_0_), channel_id=1, source_target_pairs={{0,8},{4,12},{8,0},{12,4},{1,9},{5,13},{9,1},{13,5},{2,10},{6,14},... | collective-permute-start | bytes 983048 | tf_op jit(solution)/shard_map/ppermute | solution.py:602
  308.4 14.4 %collective-permute-start.54 = (bf16[320,512]{1,0:T(8,128)(2,1)S(1)}, bf16[320,512]{1,0:T(8,128)(2,1)S(1)}, u32[]{:S(2)}, u32[]{:S(2)}) collective-permute-start(bf16[320,512]{1,0:T(8,128)(2,1)S(1)} %get-tuple-element.249.refs_0_), channel_id=1, source_target_pairs={{0,12},{4,8},{8,4},{12,0},{1,13},{5,9},{9,5},{13,1},{2,14},{6,10},... | collective-permute-start | bytes 983048 | tf_op jit(solution)/shard_map/ppermute | solution.py:602
  326.8 18.2 %collective-permute-start.60 = (bf16[320,896]{1,0:T(8,128)(2,1)S(1)}, bf16[320,896]{1,0:T(8,128)(2,1)S(1)}, u32[]{:S(2)}, u32[]{:S(2)}) collective-permute-start(bf16[320,896]{1,0:T(8,128)(2,1)S(1)} %pad_maximum_fusion.1.refs_0_), channel_id=1, source_target_pairs={{0,4},{4,0},{8,12},{12,8},{1,5},{5,1},{9,13},{13,9},{2,6},{6,2},{1... | collective-permute-start | bytes 1720328 | tf_op jit(solution)/shard_map/ppermute | solution.py:602
  328.4 27.4 %collective-permute-start.61 = (bf16[320,896]{1,0:T(8,128)(2,1)S(1)}, bf16[320,896]{1,0:T(8,128)(2,1)S(1)}, u32[]{:S(2)}, u32[]{:S(2)}) collective-permute-start(bf16[320,896]{1,0:T(8,128)(2,1)S(1)} %pad_maximum_fusion.1.refs_0_), channel_id=1, source_target_pairs={{0,8},{4,12},{8,0},{12,4},{1,9},{5,13},{9,1},{13,5},{2,10},{6,14},... | collective-permute-start | bytes 1720328 | tf_op jit(solution)/shard_map/ppermute | solution.py:602
  328.9 26.8 %collective-permute-start.62 = (bf16[320,896]{1,0:T(8,128)(2,1)S(1)}, bf16[320,896]{1,0:T(8,128)(2,1)S(1)}, u32[]{:S(2)}, u32[]{:S(2)}) collective-permute-start(bf16[320,896]{1,0:T(8,128)(2,1)S(1)} %pad_maximum_fusion.1.refs_0_), channel_id=1, source_target_pairs={{0,12},{4,8},{8,4},{12,0},{1,13},{5,9},{9,5},{13,1},{2,14},{6,10},... | collective-permute-start | bytes 1720328 | tf_op jit(solution)/shard_map/ppermute | solution.py:602
  360.7 51.0 %collective-permute-start.66 = (bf16[1280,896]{1,0:T(8,128)(2,1)}, bf16[1280,896]{1,0:T(8,128)(2,1)S(1)}, u32[]{:S(2)}, u32[]{:S(2)}) collective-permute-start(bf16[1280,896]{1,0:T(8,128)(2,1)} %shard_map.133.refs_0_), channel_id=1, source_target_pairs={{0,16},{16,0},{1,17},{17,1},{2,18},{18,2},{3,19},{19,3},{4,20},{20... | collective-permute-start | bytes 6881288 | tf_op jit(solution)/shard_map/ppermute | solution.py:587
  362.5 29.4 %collective-permute-start.58 = (bf16[320,512]{1,0:T(8,128)(2,1)S(1)}, bf16[320,512]{1,0:T(8,128)(2,1)S(1)}, u32[]{:S(2)}, u32[]{:S(2)}) collective-permute-start(bf16[320,512]{1,0:T(8,128)(2,1)S(1)} %copy-done.59), channel_id=1, source_target_pairs={{2,0},{3,1},{16,2},{17,3},{0,16},{1,17},{18,18},{19,19},{6,4},{7,5... | collective-permute-start | bytes 983048 | tf_op jit(solution)/shard_map/ppermute | solution.py:410
  365.2 26.7 %collective-permute-start.59 = (bf16[320,512]{1,0:T(8,128)(2,1)S(1)}, bf16[320,512]{1,0:T(8,128)(2,1)S(1)}, u32[]{:S(2)}, u32[]{:S(2)}) collective-permute-start(bf16[320,512]{1,0:T(8,128)(2,1)S(1)} %copy-done.57), channel_id=1, source_target_pairs={{3,0},{2,1},{17,2},{16,3},{1,16},{0,17},{19,18},{18,19},{7,4},{6,5... | collective-permute-start | bytes 983048 | tf_op jit(solution)/shard_map/ppermute | solution.py:410
  392.4 13.7 %collective-permute-start.63 = (bf16[320,512]{1,0:T(8,128)(2,1)S(1)}, bf16[320,512]{1,0:T(8,128)(2,1)S(1)}, u32[]{:S(2)}, u32[]{:S(2)}) collective-permute-start(bf16[320,512]{1,0:T(8,128)(2,1)S(1)} %multiply_convert_fusion.refs_0_), channel_id=1, source_target_pairs={{0,1},{1,0},{2,3},{3,2},{4,5},{5,4},{6,7},{7,6},{8,9},{9,8},{10,11... | collective-permute-start | bytes 983048 | tf_op jit(solution)/shard_map/ppermute | solution.py:602
  396.6 15.1 %collective-permute-start.64 = (bf16[320,512]{1,0:T(8,128)(2,1)S(1)}, bf16[320,512]{1,0:T(8,128)(2,1)S(1)}, u32[]{:S(2)}, u32[]{:S(2)}) collective-permute-start(bf16[320,512]{1,0:T(8,128)(2,1)S(1)} %multiply_convert_fusion.refs_0_), channel_id=1, source_target_pairs={{0,2},{1,3},{2,0},{3,1},{4,6},{5,7},{6,4},{7,5},{8,10},{9,11},{10,... | collective-permute-start | bytes 983048 | tf_op jit(solution)/shard_map/ppermute | solution.py:602
  396.6 55.9 %collective-permute-start.39 = (bf16[320,384]{1,0:T(8,128)(2,1)}, bf16[320,384]{1,0:T(8,128)(2,1)S(1)}, u32[]{:S(2)}, u32[]{:S(2)}) collective-permute-start(bf16[320,384]{1,0:T(8,128)(2,1)} %get-tuple-element.194), channel_id=1, source_target_pairs={{0,0},{1,1},{18,2},{19,3},{2,16},{3,17},{16,18},{17,19},{4,4},{5,5... | collective-permute-start | bytes 737288 | tf_op jit(solution)/shard_map/ppermute | solution.py:410
  398.2 54.3 %collective-permute-start.40 = (bf16[320,384]{1,0:T(8,128)(2,1)S(1)}, bf16[320,384]{1,0:T(8,128)(2,1)S(1)}, u32[]{:S(2)}, u32[]{:S(2)}) collective-permute-start(bf16[320,384]{1,0:T(8,128)(2,1)S(1)} %copy-done.70), channel_id=1, source_target_pairs={{1,0},{0,1},{19,2},{18,3},{3,16},{2,17},{17,18},{16,19},{5,4},{4,5... | collective-permute-start | bytes 737288 | tf_op jit(solution)/shard_map/ppermute | solution.py:410
  406.2 46.3 %collective-permute-start.41 = (bf16[320,384]{1,0:T(8,128)(2,1)S(1)}, bf16[320,384]{1,0:T(8,128)(2,1)S(1)}, u32[]{:S(2)}, u32[]{:S(2)}) collective-permute-start(bf16[320,384]{1,0:T(8,128)(2,1)S(1)} %copy-done.69), channel_id=1, source_target_pairs={{2,0},{3,1},{16,2},{17,3},{0,16},{1,17},{18,18},{19,19},{6,4},{7,5... | collective-permute-start | bytes 737288 | tf_op jit(solution)/shard_map/ppermute | solution.py:410
  411.7 40.8 %collective-permute-start.42 = (bf16[320,384]{1,0:T(8,128)(2,1)S(1)}, bf16[320,384]{1,0:T(8,128)(2,1)S(1)}, u32[]{:S(2)}, u32[]{:S(2)}) collective-permute-start(bf16[320,384]{1,0:T(8,128)(2,1)S(1)} %copy-done.68), channel_id=1, source_target_pairs={{3,0},{2,1},{17,2},{16,3},{1,16},{0,17},{19,18},{18,19},{7,4},{6,5... | collective-permute-start | bytes 737288 | tf_op jit(solution)/shard_map/ppermute | solution.py:410
  411.7 34.4 %collective-permute-start.65 = (bf16[320,512]{1,0:T(8,128)(2,1)S(1)}, bf16[320,512]{1,0:T(8,128)(2,1)S(1)}, u32[]{:S(2)}, u32[]{:S(2)}) collective-permute-start(bf16[320,512]{1,0:T(8,128)(2,1)S(1)} %multiply_convert_fusion.refs_0_), channel_id=1, source_target_pairs={{0,3},{1,2},{2,1},{3,0},{4,7},{5,6},{6,5},{7,4},{8,11},{9,10},{10,... | collective-permute-start | bytes 983048 | tf_op jit(solution)/shard_map/ppermute | solution.py:602
  451.1 36.5 %collective-permute-start.68 = (bf16[1280,512]{1,0:T(8,128)(2,1)}, bf16[1280,512]{1,0:T(8,128)(2,1)S(1)}, u32[]{:S(2)}, u32[]{:S(2)}) collective-permute-start(bf16[1280,512]{1,0:T(8,128)(2,1)} %get-tuple-element.227.refs_5_), channel_id=1, source_target_pairs={{0,16},{16,0},{1,17},{17,1},{2,18},{18,2},{3,19},{19,3},{4,20},{20... | collective-permute-start | bytes 3932168 | tf_op jit(solution)/shard_map/ppermute | solution.py:587
  453.0 12.5 %collective-permute-start.43 = (bf16[320,384]{1,0:T(8,128)(2,1)S(1)}, bf16[320,384]{1,0:T(8,128)(2,1)S(1)}, u32[]{:S(2)}, u32[]{:S(2)}) collective-permute-start(bf16[320,384]{1,0:T(8,128)(2,1)S(1)} %multiply_convert_fusion.4.refs_0_), channel_id=1, source_target_pairs={{0,1},{1,0},{2,3},{3,2},{4,5},{5,4},{6,7},{7,6},{8,9},{9,8},{10,11... | collective-permute-start | bytes 737288 | tf_op jit(solution)/shard_map/ppermute | solution.py:602
  453.1 20.4 %collective-permute-start.44 = (bf16[320,384]{1,0:T(8,128)(2,1)S(1)}, bf16[320,384]{1,0:T(8,128)(2,1)S(1)}, u32[]{:S(2)}, u32[]{:S(2)}) collective-permute-start(bf16[320,384]{1,0:T(8,128)(2,1)S(1)} %multiply_convert_fusion.4.refs_0_), channel_id=1, source_target_pairs={{0,2},{1,3},{2,0},{3,1},{4,6},{5,7},{6,4},{7,5},{8,10},{9,11},{10,... | collective-permute-start | bytes 737288 | tf_op jit(solution)/shard_map/ppermute | solution.py:602
  455.8 17.7 %collective-permute-start.45 = (bf16[320,384]{1,0:T(8,128)(2,1)S(1)}, bf16[320,384]{1,0:T(8,128)(2,1)S(1)}, u32[]{:S(2)}, u32[]{:S(2)}) collective-permute-start(bf16[320,384]{1,0:T(8,128)(2,1)S(1)} %multiply_convert_fusion.4.refs_0_), channel_id=1, source_target_pairs={{0,3},{1,2},{2,1},{3,0},{4,7},{5,6},{6,5},{7,4},{8,11},{9,10},{10,... | collective-permute-start | bytes 737288 | tf_op jit(solution)/shard_map/ppermute | solution.py:602
  479.6 17.8 %collective-permute-start.47 = (bf16[160,384]{1,0:T(8,128)(2,1)}, bf16[160,384]{1,0:T(8,128)(2,1)S(1)}, u32[]{:S(2)}, u32[]{:S(2)}) collective-permute-start(bf16[160,384]{1,0:T(8,128)(2,1)} %get-tuple-element.200), channel_id=1, source_target_pairs={{0,8},{4,12},{8,0},{12,4},{1,9},{5,13},{9,1},{13,5},{2,10},{6,14},... | collective-permute-start | bytes 368648 | tf_op jit(solution)/shard_map/ppermute | solution.py:602
  481.1 16.3 %collective-permute-start.48 = (bf16[160,384]{1,0:T(8,128)(2,1)}, bf16[160,384]{1,0:T(8,128)(2,1)S(1)}, u32[]{:S(2)}, u32[]{:S(2)}) collective-permute-start(bf16[160,384]{1,0:T(8,128)(2,1)} %get-tuple-element.201), channel_id=1, source_target_pairs={{0,12},{4,8},{8,4},{12,0},{1,13},{5,9},{9,5},{13,1},{2,14},{6,10},... | collective-permute-start | bytes 368648 | tf_op jit(solution)/shard_map/ppermute | solution.py:602
  485.5 12.0 %collective-permute-start.69 = (bf16[160,512]{1,0:T(8,128)(2,1)S(1)}, bf16[160,512]{1,0:T(8,128)(2,1)S(1)}, u32[]{:S(2)}, u32[]{:S(2)}) collective-permute-start(bf16[160,512]{1,0:T(8,128)(2,1)S(1)} %copy-done.82), channel_id=1, source_target_pairs={{0,4},{4,0},{8,12},{12,8},{1,5},{5,1},{9,13},{13,9},{2,6},{6,2},{1... | collective-permute-start | bytes 491528 | tf_op jit(solution)/shard_map/ppermute | solution.py:602
  485.8 11.7 %collective-permute-start.70 = (bf16[160,512]{1,0:T(8,128)(2,1)S(1)}, bf16[160,512]{1,0:T(8,128)(2,1)S(1)}, u32[]{:S(2)}, u32[]{:S(2)}) collective-permute-start(bf16[160,512]{1,0:T(8,128)(2,1)S(1)} %copy-done.81), channel_id=1, source_target_pairs={{0,8},{4,12},{8,0},{12,4},{1,9},{5,13},{9,1},{13,5},{2,10},{6,14},... | collective-permute-start | bytes 491528 | tf_op jit(solution)/shard_map/ppermute | solution.py:602
  487.6 9.9 %collective-permute-start.71 = (bf16[160,512]{1,0:T(8,128)(2,1)S(1)}, bf16[160,512]{1,0:T(8,128)(2,1)S(1)}, u32[]{:S(2)}, u32[]{:S(2)}) collective-permute-start(bf16[160,512]{1,0:T(8,128)(2,1)S(1)} %copy-done.80), channel_id=1, source_target_pairs={{0,12},{4,8},{8,4},{12,0},{1,13},{5,9},{9,5},{13,1},{2,14},{6,10},... | collective-permute-start | bytes 491528 | tf_op jit(solution)/shard_map/ppermute | solution.py:602
  511.6 21.6 %collective-permute-start.75 = (bf16[4,160,784]{2,1,0:T(8,128)(2,1)S(1)}, bf16[4,160,784]{2,1,0:T(8,128)(2,1)S(1)}, u32[]{:S(2)}, u32[]{:S(2)}) collective-permute-start(bf16[4,160,784]{2,1,0:T(8,128)(2,1)S(1)} %bitcast.25), channel_id=1, source_target_pairs={{0,16},{16,0},{1,17},{17,1},{2,18},{18,2},{3,19},{19,3},{4,20},{20... | collective-permute-start | bytes 3010568 | tf_op jit(solution)/shard_map/ppermute | solution.py:587
  526.6 33.2 %collective-permute-start.72 = (bf16[160,784]{1,0:T(8,128)(2,1)}, bf16[160,784]{1,0:T(8,128)(2,1)S(1)}, u32[]{:S(2)}, u32[]{:S(2)}) collective-permute-start(bf16[160,784]{1,0:T(8,128)(2,1)} %get-tuple-element.241), channel_id=1, source_target_pairs={{0,1},{1,0},{2,3},{3,2},{4,5},{5,4},{6,7},{7,6},{8,9},{9,8},{10,11... | collective-permute-start | bytes 752648 | tf_op jit(solution)/shard_map/ppermute | solution.py:602
  530.8 29.0 %collective-permute-start.73 = (bf16[160,784]{1,0:T(8,128)(2,1)}, bf16[160,784]{1,0:T(8,128)(2,1)S(1)}, u32[]{:S(2)}, u32[]{:S(2)}) collective-permute-start(bf16[160,784]{1,0:T(8,128)(2,1)} %get-tuple-element.242), channel_id=1, source_target_pairs={{0,2},{1,3},{2,0},{3,1},{4,6},{5,7},{6,4},{7,5},{8,10},{9,11},{10,... | collective-permute-start | bytes 752648 | tf_op jit(solution)/shard_map/ppermute | solution.py:602
  531.5 28.3 %collective-permute-start.74 = (bf16[160,784]{1,0:T(8,128)(2,1)}, bf16[160,784]{1,0:T(8,128)(2,1)S(1)}, u32[]{:S(2)}, u32[]{:S(2)}) collective-permute-start(bf16[160,784]{1,0:T(8,128)(2,1)} %get-tuple-element.243), channel_id=1, source_target_pairs={{0,3},{1,2},{2,1},{3,0},{4,7},{5,6},{6,5},{7,4},{8,11},{9,10},{10,... | collective-permute-start | bytes 752648 | tf_op jit(solution)/shard_map/ppermute | solution.py:602
  (95 other events, 1366.0 us)

commit v4 on v3

--- a/solution.py
+++ b/solution.py
@@ -9,6 +9,7 @@
 
 SIDE = 28
 TAPS = 9
+CORES, CIN, COUT = "section", "cin", "cout"
 F32 = jnp.float32
 BF16 = jnp.bfloat16
 NN = (((1,), (0,)), ((), ()))
@@ -35,7 +36,7 @@
 
 def params():
     return pltpu.CompilerParams(
-        dimension_semantics=("arbitrary",), vmem_limit_bytes=56 * 1024 * 1024
+        vmem_limit_bytes=56 * 1024 * 1024
     )
 
 
@@ -91,10 +92,6 @@
     return jax.ShapeDtypeStruct(shape, dtype)
 
 
-def held_type(size):
-    return BF16 if size % 16 == 0 else F32
-
-
 def rows_at(index, size):
     return pl.ds(pl.multiple_of(index * size, 8), size)
 
@@ -120,7 +117,7 @@
 def conv_forward_body(x_ref, w_ref, *rest, side, n):
     outs, (planes, windows, total) = rest[:-3], rest[-3:]
     t = pl.program_id(0)
-    me = lax.axis_index("cin")
+    me = lax.axis_index(CIN)
 
     @pl.when(t == 0)
     def _():
@@ -166,7 +163,7 @@
 def conv_back_body(m_ref, w_ref, *refs, side, n):
     outs, (planes, total) = refs[:n], refs[n:]
     t = pl.program_id(0)
-    me = lax.axis_index("cout")
+    me = lax.axis_index(COUT)
 
     @pl.when(t == 0)
     def _():
@@ -242,13 +239,14 @@
     )(xa, xb, ma, mb)
 
 
-def fill_moved(moved, cots, half):
-    count, rows, pixels = cots.shape
+def fill_moved(moved, images, half):
+    count = len(images)
+    rows, pixels = images[0].shape
     wide = moved.shape[2] // count
     column = lax.broadcasted_iota(jnp.int32, (rows, wide), 1) % half
     for b in range(count):
         moved[0, :, b * wide : (b + 1) * wide] = jnp.zeros((rows, wide), moved.dtype)
-        moved[0, :, b * wide : b * wide + pixels] = cots[b]
+        moved[0, :, b * wide : b * wide + pixels] = images[b]
         image = moved[0, :, b * wide : (b + 1) * wide]
         inner = jnp.where(column == 0, jnp.zeros_like(image), image)
         moved[1, :, b * wide : (b + 1) * wide] = pltpu.roll(inner, wide - 1, 1)
@@ -269,14 +267,13 @@
 def half_back_body(g_ref, w_ref, kept, sent, moved, total, placed, *, side):
     t = pl.program_id(0)
     count = g_ref.shape[0]
-    rows, pixels = placed.shape
-    half = rows // 2
+    pixels = placed.shape[1]
     wide = moved.shape[2] // count
-    core = lax.axis_index("section")
+    core = lax.axis_index(CORES)
 
     @pl.when(t == 0)
     def _():
-        fill_moved(moved, g_ref[...], side // 2)
+        fill_moved(moved, [g_ref[core], g_ref[1 - core]], side // 2)
         total[...] = jnp.zeros_like(total)
 
     ty, tx = t // 3, t % 3
@@ -294,8 +291,7 @@
                     NN,
                 )
                 placed[...] = term if k == 0 else placed[...] + term
-            kept[b * half : (b + 1) * half, :] = placed[rows_at(core, half), :].astype(BF16)
-            sent[b * half : (b + 1) * half, :] = placed[rows_at(1 - core, half), :].astype(BF16)
+            (kept, sent)[b][...] = placed[...].astype(BF16)
 
 
 def half_back(cots, kernel, side):
@@ -303,7 +299,7 @@
     depth = kernel.shape[1]
     wide = lanes_of(small + side // 2 + 1)
     pixels = lanes_of(side * side + side + 1)
-    out = (count * depth // 2, pixels)
+    out = (depth, pixels)
     return pl.pallas_call(
         functools.partial(half_back_body, side=side),
         out_shape=[like(out)] * 2,
@@ -327,20 +323,18 @@
     mine, other, g_ref, o_ref, moved, planes = refs
     t = pl.program_id(0)
     count = g_ref.shape[0]
-    half = mine.shape[0] // count
     pixels = mine.shape[1]
     wide = moved.shape[2] // count
-    core = lax.axis_index("section")
+    core = lax.axis_index(CORES)
 
     @pl.when(t == 0)
     def _():
-        fill_moved(moved, g_ref[...], side // 2)
+        fill_moved(moved, [g_ref[core], g_ref[1 - core]], side // 2)
         for k in range(4):
             pick = chosen(k, wide, pixels, side)
-            for ref, place in ((mine, core), (other, 1 - core)):
-                for b in range(count):
-                    plane = dot(ref[b * half : (b + 1) * half, :], pick, NT)
-                    planes[k, rows_at(place, half), b * wide : (b + 1) * wide] = plane.astype(BF16)
+            for b, ref in enumerate((mine, other)):
+                plane = dot(ref[...], pick, NT)
+                planes[k, :, b * wide : (b + 1) * wide] = plane.astype(BF16)
 
     ty, tx = t // 3, t % 3
     plane = jnp.where(ty == 1, 0, 2) + jnp.where(tx == 1, 0, 1)
@@ -350,7 +344,7 @@
 
 def half_weight(mine, other, cots, side):
     count, width, small = cots.shape
-    depth = 2 * mine.shape[0] // count
+    depth = mine.shape[0]
     wide = lanes_of(small + side // 2 + 1)
     return pl.pallas_call(
         functools.partial(half_weight_body, side=side),
@@ -376,7 +370,7 @@
     def body(x_ref, w_ref, *rest):
         outs, total = rest[:n], rest[n]
         total[...] = dot(w_ref[...], x_ref[...], TN)
-        write_chunks(outs, total, lax.axis_index("cout"), n)
+        write_chunks(outs, total, lax.axis_index(COUT), n)
 
     return one_step(
         body,
@@ -387,153 +381,102 @@
     )
 
 
-def round_target(r, core, z, n):
-    return z // (n // 2), z ^ r ^ (core * (n // 2))
-
-
-def round_block(r, core, z, n):
-    place = z ^ r
-    return lax.rem(place, n // 2), core ^ (place // (n // 2))
-
-
-def round_pairs(r, n, back):
-    pairs = []
-    for core in range(2):
-        for z in range(n):
-            to_core, to_z = round_target(r, core, z, n)
-            pair = (core * n + z, to_core * n + to_z)
-            pairs.append(pair[::-1] if back else pair)
-    return pairs
-
-
-def round_send(value, r, n, back=False):
-    return lax.ppermute(value, ("section", "cout"), round_pairs(r, n, back))
-
-
-def reduce_forward(parts, weight, n):
+def reduce_forward(parts, mine, other, n, m):
     size, pixels = parts[0].shape
-    depth, width = weight.shape
-    half = width // 2
+    depth, width = mine.shape
 
     def body(*refs):
-        ins, w_ref = refs[:n], refs[n]
-        joined, kept, sent, total = refs[n + 1 :]
-        core, z = lax.axis_index("section"), lax.axis_index("cout")
-        for r in range(n):
-            block, image = round_block(r, core, z, n)
-            joined[image, rows_at(block, size), :] = ins[r][...]
-        for image in range(2):
-            total[...] = dot(w_ref[...], joined[image], TN)
-            span = slice(image * half, (image + 1) * half)
-            kept[span, :] = total[rows_at(core, half), :].astype(BF16)
-            sent[span, :] = total[rows_at(1 - core, half), :].astype(BF16)
-
-    return one_step(
+        ins, a_ref, b_ref = refs[:n], refs[n], refs[n + 1]
+        joined, lent, outs, total = refs[n + 2], refs[n + 3], refs[n + 4 : -1], refs[-1]
+        core, z = lax.axis_index(CORES), lax.axis_index(COUT)
+        for k in range(n):
+            joined[rows_at(source(z, k, n), size), :] = ins[k][...]
+        lent[...] = joined[rows_at(1 - core, depth), :]
+        total[...] = dot(a_ref[...], joined[rows_at(core, depth), :], TN) + dot(
+            b_ref[...], lent[...], TN
+        )
+        write_chunks(outs, total, lax.axis_index(CIN), m)
+
+    outs = one_step(
         body,
-        [*parts, weight],
-        [like((2, depth, pixels)), like((2 * half, pixels)), like((2 * half, pixels))],
+        [*parts, mine, other],
+        [like((2 * depth, pixels)), like((depth, pixels))] + [like((width // m, pixels))] * m,
         [pltpu.VMEM((width, pixels), F32)],
         4 * depth * width * pixels,
     )
+    return outs[0], outs[1], outs[2:]
 
 
 def add_halves(kept, got, n):
     rows, pixels = kept.shape
-    size = rows // 2 // n
 
     def body(a_ref, b_ref, *rest):
         outs, total = rest[:n], rest[n]
-        me = lax.axis_index("cin")
         total[...] = a_ref[...].astype(F32) + b_ref[...].astype(F32)
-        for k in range(n):
-            for image in range(2):
-                start = image * (rows // 2) + partner(me, k, n) * size
-                value = total[pl.ds(pl.multiple_of(start, 8), size), :]
-                outs[k][image * size : (image + 1) * size, :] = value.astype(BF16)
+        write_chunks(outs, total, lax.axis_index(CIN), n)
 
     return one_step(
         body,
         [kept, got],
-        [like((2 * size, pixels))] * n,
+        [like((rows // n, pixels))] * n,
         [pltpu.VMEM((rows, pixels), F32)],
         rows * pixels,
     )
 
 
 def join_pieces(parts, n):
-    double, pixels = parts[0].shape
-    size = double // 2
+    size, pixels = parts[0].shape
 
     def body(*refs):
-        ins, out, held = refs[:n], refs[n], refs[n + 1]
-        me = lax.axis_index("cin")
+        ins, out = refs[:n], refs[n]
+        me = lax.axis_index(CIN)
         for k in range(n):
-            for image in range(2):
-                start = image * n * size + source(me, k, n) * size
-                value = ins[k][image * size : (image + 1) * size, :]
-                held[pl.ds(pl.multiple_of(start, 8), size), :] = value.astype(held.dtype)
-        out[...] = held[...].astype(BF16)
+            out[rows_at(source(me, k, n), size), :] = ins[k][...]
+
+    return one_step(body, parts, [like((n * size, pixels))], [], size * pixels)[0]
+
+
+def reduce_back(parts, mine, other, m, n):
+    size, pixels = parts[0].shape
+    depth, width = mine.shape
+
+    def body(*refs):
+        ins, a_ref, b_ref = refs[:m], refs[m], refs[m + 1]
+        masked, outs, total = refs[m + 2], refs[m + 3 : -1], refs[-1]
+        core, c = lax.axis_index(CORES), lax.axis_index(CIN)
+        for k in range(m):
+            masked[rows_at(source(c, k, m), size), :] = ins[k][...]
+        total[rows_at(core, depth), :] = dot(a_ref[...], masked[...], NN)
+        total[rows_at(1 - core, depth), :] = dot(b_ref[...], masked[...], NN)
+        write_chunks(outs, total, lax.axis_index(COUT), n)
+
+    outs = one_step(
+        body,
+        [*parts, mine, other],
+        [like((width, pixels))] + [like((2 * depth // n, pixels))] * n,
+        [pltpu.VMEM((2 * depth, pixels), F32)],
+        4 * depth * width * pixels,
+    )
+    return outs[0], outs[1:]
+
+
+def reduce_weight_gradient(joined, lent, masked, masked_other):
+    depth, width = lent[0].shape[0], masked[0].shape[0]
+    count = len(joined)
+
+    def body(*refs):
+        out, core = refs[4 * count], lax.axis_index(CORES)
+        for j in range(count):
+            own, theirs, a, b = refs[j : 4 * count : count]
+            term = dot(own[rows_at(core, depth), :], a[...], NT) + dot(theirs[...], b[...], NT)
+            out[...] = term if j == 0 else out[...] + term
 
     return one_step(
         body,
-        parts,
-        [like((n * double, pixels))],
-        [pltpu.VMEM((n * double, pixels), held_type(size))],
-        double * pixels,
-    )[0]
-
-
-def place_halves(masked, mine, other, core):
-    half = mine.shape[0] // 2
-    for image in range(2):
-        rows = slice(image * half, (image + 1) * half)
-        masked[image, rows_at(core, half), :] = mine[rows, :]
-        masked[image, rows_at(1 - core, half), :] = other[rows, :]
-
-
-def reduce_back(mine, other, weight, n):
-    depth, width = weight.shape
-    pixels = mine.shape[1]
-    size = depth // (n // 2)
-
-    def body(*refs):
-        a, b, w_ref = refs[:3]
-        outs, masked = refs[3 : 3 + n], refs[3 + n]
-        core, z = lax.axis_index("section"), lax.axis_index("cout")
-        place_halves(masked, a, b, core)
-        for r in range(n):
-            block, image = round_block(r, core, z, n)
-            outs[r][...] = dot(w_ref[rows_at(block, size), :], masked[image], NN).astype(BF16)
-
-    return one_step(
-        body,
-        [mine, other, weight],
-        [like((size, pixels))] * n,
-        [pltpu.VMEM((2, width, pixels), BF16)],
-        4 * depth * width * pixels,
-    )
-
-
-def reduce_weight_gradient(joined, mine, other):
-    _, depth, _ = joined[0].shape
-    width = mine[0].shape[0]
-    pixels = sum(v.shape[1] for v in mine)
-
-    def body(*refs):
-        js, a, b, out = refs[0:2], refs[2:4], refs[4:6], refs[6]
-        core = lax.axis_index("section")
-        for j in range(2):
-            masked = refs[7 + j]
-            place_halves(masked, a[j], b[j], core)
-            term = dot(js[j][0], masked[0], NT) + dot(js[j][1], masked[1], NT)
-            out[...] = term if j == 0 else out[...] + term
-
-    return one_step(
-        body,
-        [*joined, *mine, *other],
+        [*joined, *lent, *masked, *masked_other],
         [like((depth, width), F32)],
-        [pltpu.VMEM((2, width, v.shape[1]), BF16) for v in mine],
-        4 * depth * width * pixels,
+        [],
+        4 * width * sum(v.size for v in lent),
     )[0]
 
 
@@ -544,11 +487,11 @@
     def body(*refs):
         ins, w_ref, outs = refs[:n], refs[n], refs[n + 1 : n + 1 + m]
         held, total = refs[n + 1 + m :]
-        z = lax.axis_index("cout")
+        z = lax.axis_index(COUT)
         for k in range(n):
             held[rows_at(source(z, k, n), size), :] = ins[k][...]
         total[...] = dot(w_ref[...], held[...], NN)
-        write_chunks(outs, total, lax.axis_index("cin"), m)
+        write_chunks(outs, total, lax.axis_index(CIN), m)
 
     outs = one_step(
         body,
@@ -584,7 +527,7 @@
 
 
 def swap(value):
-    return lax.ppermute(value, "section", [(0, 1), (1, 0)])
+    return lax.ppermute(value, CORES, [(0, 1), (1, 0)])
 
 
 def swap_blocks(value, n):
@@ -644,19 +587,19 @@
     stride_kernel,
     output_grad,
 ):
-    m, n = axis_size("cin"), axis_size("cout")
+    m, n = axis_size(CIN), axis_size(COUT)
     pixels = SIDE * SIDE
     wide = lanes_of(pixels + SIDE + 1)
     cuts = spans(wide)
     skip = jnp.pad(turn(block_input)[0], ((0, 0), (0, wide - pixels)))
     cots = turn(output_grad)
 
-    feature_block = gather(turn(inner_features)[0], "cout")
+    feature_block = gather(turn(inner_features)[0], COUT)
     first_parts = conv_forward(feature_block, first_kernel, SIDE, m)
-    cot_block = collect(after(cots, first_parts), "cout", 1)
+    cot_block = collect(after(cots, first_parts), COUT, 1)
     first_got = []
     for j in range(2):
-        first_got.append(exchange(first_parts[j], "cin"))
+        first_got.append(exchange(first_parts[j], CIN))
 
     hidden, first_block, expand_got = [], [], []
     ready = None
@@ -664,13 +607,14 @@
         got = first_got[j] if j == 0 else after(first_got[j], ready)
         hidden.append(add_up(got))
         act = smooth_gate(hidden[j]).astype(BF16)
-        first_block.append(gather(act, "cin"))
+        first_block.append(gather(act, CIN))
         ready = expand(first_block[j], expand_weight, n)
-        expand_got.append(exchange(ready, "cout"))
+        expand_got.append(exchange(ready, COUT))
 
     back_kept, back_sent = half_back(after(cot_block, ready), stride_kernel, SIDE)
     feature_other = swap_blocks(after(feature_block, ready), n)
     first_other = [swap(after(v, ready)) for v in first_block]
+    reduce_other = swap(after(reduce_weight, ready))
 
     joined_pre, joined_got = [], []
     for j in range(2):
@@ -678,55 +622,58 @@
         got = after(expand_got[j], back_kept)
         joined_pre.append(skip[:, start:stop].astype(F32) + add_up(got))
         joined = smooth_gate(joined_pre[j]).astype(BF16)
-        joined_got.append([round_send(joined, r, n) for r in range(n)])
+        joined_got.append(spread(joined, COUT))
     back_other = swap(back_sent)
     back_parts = add_halves(back_kept, back_other, m)
-    back_got = exchange(back_parts, "cin")
-
-    joined_two, hidden_got = [], []
+    back_got = exchange(back_parts, CIN)
+
+    joined_own, joined_lent, hidden_got = [], [], []
     for j in range(2):
         got = after(joined_got[j], back_parts)
         if j > 0:
             got = after(got, parts, feature_other, first_other)
-        two, kept, sent = reduce_forward(got, reduce_weight, n)
-        joined_two.append(two)
-        other_sent = swap(sent)
-        parts = add_halves(kept, other_sent, m)
-        hidden_got.append(exchange(parts, "cin"))
+        own, lent, parts = reduce_forward(got, reduce_weight, reduce_other, n, m)
+        joined_own.append(own)
+        hidden_got.append(exchange(parts, CIN))
+        joined_lent.append(lent)
     back_piece = add_up(back_got)
-    act_piece, mine, other, round_got = [], [], [], []
+    act_piece, masked, masked_other, round_got = [], [], [], []
     for j in range(2):
         start, stop = cuts[j]
         got = hidden_got[j] if j == 0 else after(hidden_got[j], ready)
         piece = add_up(got)
         act_piece.append(smooth_gate(piece).astype(BF16))
-        masked = (back_piece[:, start:stop] * gate_slope(piece)).astype(BF16)
-        mask_got = spread(masked, "cin")
+        mask = (back_piece[:, start:stop] * gate_slope(piece)).astype(BF16)
+        mask_got = spread(mask, CIN)
         if j == 0:
             mask_got = after(mask_got, parts)
-        mine.append(join_pieces(mask_got, m))
-        other.append(swap(mine[j]))
-        if j > 0:
-            act_got = spread(jnp.concatenate(act_piece, axis=1), "cin")
-        ready = reduce_back(mine[j], other[j], reduce_weight, n)
-        round_got.append([round_send(ready[r], r, n, True) for r in range(n)])
+        else:
+            act_got = spread(jnp.concatenate(act_piece, axis=1), CIN)
+        block, ready = reduce_back(mask_got, reduce_weight, reduce_other, m, n)
+        masked.append(block)
+        round_got.append(exchange(ready, COUT))
+        masked_other.append(swap(block))
+        joined_lent[j] = swap(after(joined_lent[j], block))
+
     input_gradient, input_got = [], []
     input_wide, input_other, back_got = [], [], []
     for j in range(2):
         slope = gate_slope(joined_pre[j])
         input_gradient.append((add_up(round_got[j]) * slope).astype(BF16))
-        input_got.append(spread(input_gradient[j], "cout"))
+        input_got.append(spread(input_gradient[j], COUT))
         got = input_got[j]
         if j > 0:
             stride_gradient = half_weight(act_mine, act_other, cot_block, SIDE)
             got = after(got, stride_gradient)
         parts, block = expand_back(got, expand_weight, m, n)
         input_wide.append(block)
-        back_got.append(exchange(parts, "cin"))
+        back_got.append(exchange(parts, CIN))
         input_other.append(swap(block))
         if j > 0:
             break
-        reduce_gradient = reduce_weight_gradient(after(joined_two, ready), mine, other)
+        reduce_gradient = reduce_weight_gradient(
+            after(joined_own, ready), joined_lent, masked, masked_other
+        )
         act_mine = join_pieces(after(act_got, reduce_gradient), m)
         act_other = swap(act_mine)
         round_got[1] = after(round_got[1], act_mine)
@@ -735,10 +682,10 @@
     for j in range(2):
         got = after(back_got[j], expand_gradient)
         masked_first.append((add_up(got) * gate_slope(hidden[j])).astype(BF16))
-    masked_block = gather(jnp.concatenate(masked_first, axis=1)[:, :pixels], "cin")
+    masked_block = gather(jnp.concatenate(masked_first, axis=1)[:, :pixels], CIN)
     masked_other = swap_blocks(masked_block, m)
     inner_parts = conv_back(masked_block, first_kernel, SIDE, n)
-    inner_got = exchange(inner_parts, "cout")
+    inner_got = exchange(inner_parts, COUT)
     first_gradient = conv_weight(
         feature_block, feature_other, masked_block, masked_other, SIDE
     )
@@ -759,21 +706,21 @@
         both_blocks,
         mesh=mesh,
         in_specs=(
-            P("section", None, ("cin", "cout")),
-            P("section", None, ("cin", "cout")),
-            P(None, "cin", "cout"),
-            P("cout", "cin"),
-            P(("cin", "section"), "cout"),
-            P(None, "cout", ("section", "cin")),
-            P(None, None, ("section", "cin", "cout")),
+            P(CORES, None, (CIN, COUT)),
+            P(CORES, None, (CIN, COUT)),
+            P(None, CIN, COUT),
+            P(COUT, CIN),
+            P((CIN, CORES), COUT),
+            P(None, COUT, (CORES, CIN)),
+            P(None, None, (CORES, CIN, COUT)),
         ),
         out_specs=(
-            P("section", None, ("cin", "cout")),
-            P("section", None, ("cin", "cout")),
-            P(None, "cin", "cout"),
-            P("cout", "cin"),
-            P(("cin", "section"), "cout"),
-            P(None, "cout", ("section", "cin")),
+            P(CORES, None, (CIN, COUT)),
+            P(CORES, None, (CIN, COUT)),
+            P(None, CIN, COUT),
+            P(COUT, CIN),
+            P((CIN, CORES), COUT),
+            P(None, COUT, (CORES, CIN)),
         ),
         check_vma=False,
     )

time: 567 us -> 552 us (0.974)
  Pallas kernels: 175 us -> 163 us
  starting transfers between devices: 134 us -> 126 us
    ppermute x28 -> x13, starting transfers between devices: 60 us -> 2.24 us  [swap(): return lax.ppermute(value, CORES, [(0, 1), (1, 0)])]
    ppermute x45 -> x57, starting transfers between devices: 69.9 us -> 119 us  [exchange(): lax.ppermute(parts[k], name, [(i, partner(i, k, n)) for i in range(n)])]
    ppermute x45 -> x57, waiting for transfers between devices: 133 us -> 165 us  [exchange(): lax.ppermute(parts[k], name, [(i, partner(i, k, n)) for i in range(n)])]
    ppermute x28 -> x13, waiting for transfers between devices: 31.1 us -> 4.48 us  [swap(): return lax.ppermute(value, CORES, [(0, 1), (1, 0)])]
    pallas_call x16 -> x12, Pallas kernels: 74.6 us -> 63.9 us  [one_step(): pl.pallas_call(body, out_shape=outs, in_specs=[pl.BlockSpec(memory_space=...]
    unnamed x166 -> x172, local copies, waits for them, and re-layouts: 12 us -> 12.4 us
  transfers between devices with their start and end apart: 76 -> 73, of which waited for: 28 -> 23; matrix products, arithmetic and copies ran while one was open for 1% -> 1% of each run, Pallas kernels for 22% -> 21%
where the time goes in v4:
time: 552 us; the launch traced here: 547 us
  waiting for transfers between devices  175 us (32%)
  Pallas kernels  163 us (30%)
  starting transfers between devices  126 us (23%)
  blocking collectives  60.7 us (11%)
  local copies, waits for them, and re-layouts  12.5 us (2%)
  other arithmetic  6.96 us (1%)
    ppermute x57, waiting for transfers between devices, exchange(): lax.ppermute(parts[k], name, [(i, partner(i, k, n)) for i in range(n)])  165 us
    ppermute x57, starting transfers between devices, exchange(): lax.ppermute(parts[k], name, [(i, partner(i, k, n)) for i in range(n)])  119 us
    pallas_call x12, Pallas kernels, one_step(): pl.pallas_call(body, out_shape=outs, in_specs=[pl.BlockSpec(memory_space=...  63.9 us
    all_gather x4, blocking collectives, gather(): return lax.all_gather(shard, name, axis=0, tiled=True)  60.7 us
    pallas_call x1, Pallas kernels, conv_weight(): pl.pallas_call(functools.partial(conv_weight_body, side=side), out_shape=...  25.6 us
    pallas_call x1, Pallas kernels, half_weight(): pl.pallas_call(functools.partial(half_weight_body, side=side), out_shape=...  23 us
    pallas_call x1, Pallas kernels, half_back(): pl.pallas_call(functools.partial(half_back_body, side=side), out_shape=[l...  22.8 us
    pallas_call x1, Pallas kernels, conv_back(): pl.pallas_call(functools.partial(conv_back_body, side=side, n=n), out_sha...  14 us
  transfers between devices with their start and end apart: 73, of which 23 were waited for; matrix products, arithmetic and copies ran while one was open for 1% of the time, Pallas kernels for 21%

profile of v4, /device:TPU:0, one launch (start us, length us, event | category | flops | bytes accessed | tf_op | source)
XLA Modules:
  0.0 546.8 jit_solution(7110875359977111015)
XLA Ops:
  0.6 26.4 %all-gather = bf16[1,640,784]{2,1,0:T(8,128)(2,1)} all-gather(bf16[1,160,784]{2,1,0:T(8,128)(2,1)} %bitcast.26), channel_id=2, replica_groups=mesh['section'=2,'cin'=4,'cout'=4] {'cout'}, dimensions={1}, use_global_device_ids=true | all-gather | bytes 1254400 | tf_op jit(solution)/shard_map/all_gather | solution.py:578
  27.1 14.0 %shard_map.118 = (bf16[160,384]{1,0:T(8,128)(2,1)}, bf16[160,384]{1,0:T(8,128)(2,1)}, bf16[160,384]{1,0:T(8,128)(2,1)}, bf16[160,384]{1,0:T(8,128)(2,1)}, bf16[1...) custom-call(bf16[640,784]{1,0:T(8,128)(2,1)} %bitcast.22, ...), custom_call_target="tpu_custom_call" | custom-call | flops 6606028800 | bytes 9379840 | tf_op jit(solution)/shard_map/pallas_call | solution.py:143
  47.7 2.2 collective-permute-start.5
  51.4 2.7 collective-permute-start.1
  55.1 10.9 %all_gather.13.x_ref.refs_0_ = bf16[640,384]{1,0:T(8,128)(2,1)} all-gather(bf16[160,384]{1,0:T(8,128)(2,1)S(1)} %multiply_convert_fusion.9), channel_id=1, replica_groups=mesh['section'=2,'cin'=4,'cout'=4] {'cin'}, dimensions={0}, use_global_device_ids=true | all-gather | bytes 614400 | tf_op jit(solution)/shard_map/all_gather | solution.py:578
  66.1 3.9 shard_map.119
  70.0 1.7 collective-permute-start.2
  71.7 5.4 collective-permute-done.2
  77.4 10.6 %all_gather.14.x_ref.refs_1_ = bf16[640,512]{1,0:T(8,128)(2,1)} all-gather(bf16[160,512]{1,0:T(8,128)(2,1)S(1)} %multiply_convert_fusion.7), channel_id=1, replica_groups=mesh['section'=2,'cin'=4,'cout'=4] {'cin'}, dimensions={0}, use_global_device_ids=true | all-gather | bytes 819200 | tf_op jit(solution)/shard_map/all_gather | solution.py:578
  88.1 4.0 shard_map.120
  92.2 22.8 %shard_map.121 = (bf16[1280,896]{1,0:T(8,128)(2,1)}, bf16[1280,896]{1,0:T(8,128)(2,1)}) custom-call(bf16[2,640,196]{2,1,0:T(8,128)(2,1)} %copy-done.16, bf16[9,1280,640]{2,1,0:T(8,128)(2,1)} %w_ref.8), custom_call_target="tpu_custom_call" | custom-call | flops 11560550400 | bytes 14745600 | tf_op jit(solution)/shard_map/pallas_call | solution.py:303
  115.6 2.1 collective-permute-start.14
  117.7 2.3 collective-permute-start.15
  120.0 7.7 %collective-permute-done.13 = bf16[320,384]{1,0:T(8,128)(2,1)S(1)} collective-permute-done((bf16[320,384]{1,0:T(8,128)(2,1)S(1)}, bf16[320,384]{1,0:T(8,128)(2,1)S(1)}, u32[]{:S(2)}, u32[]{:S(2)}) %collective-permute-start.13) | collective-permute-done | bytes 245792 | tf_op jit(solution)/shard_map/ppermute | solution.py:545
  127.7 8.3 %collective-permute-done.14 = bf16[320,384]{1,0:T(8,128)(2,1)S(1)} collective-permute-done((bf16[320,384]{1,0:T(8,128)(2,1)S(1)}, bf16[320,384]{1,0:T(8,128)(2,1)S(1)}, u32[]{:S(2)}, u32[]{:S(2)}) %collective-permute-start.14) | collective-permute-done | bytes 245792 | tf_op jit(solution)/shard_map/ppermute | solution.py:545
  136.1 1.6 collective-permute-start.28
  137.9 5.0 collective-permute-done.26
  142.9 13.0 %collective-permute-start.16 = (bf16[320,384]{1,0:T(8,128)(2,1)S(1)}, bf16[320,384]{1,0:T(8,128)(2,1)S(1)}, u32[]{:S(2)}, u32[]{:S(2)}) collective-permute-start(bf16[320,384]{1,0:T(8,128)(2,1)S(1)} %multiply_convert_fusion.5.refs_0_), channel_id=1, source_target_pairs={{0,1},{1,0},{2,3},{3,2},{4,5},{5,4},{6,7},{7,6},{8,9},{9,8},{10,11... | collective-permute-start | bytes 737288 | tf_op jit(solution)/shard_map/ppermute | solution.py:545
  155.9 6.5 %collective-permute-done.27 = bf16[320,512]{1,0:T(8,128)(2,1)S(1)} collective-permute-done((bf16[320,512]{1,0:T(8,128)(2,1)S(1)}, bf16[320,512]{1,0:T(8,128)(2,1)S(1)}, u32[]{:S(2)}, u32[]{:S(2)}) %collective-permute-start.27) | collective-permute-done | bytes 327712 | tf_op jit(solution)/shard_map/ppermute | solution.py:545
  162.4 1.6 collective-permute-start.18
  165.1 17.2 %collective-permute-start.29 = (bf16[320,512]{1,0:T(8,128)(2,1)}, bf16[320,512]{1,0:T(8,128)(2,1)}, u32[]{:S(2)}, u32[]{:S(2)}) collective-permute-start(bf16[320,512]{1,0:T(8,128)(2,1)} %multiply_convert_fusion.2.refs_0_), channel_id=1, source_target_pairs={{0,1},{1,0},{2,3},{3,2},{4,5},{5,4},{6,7},{7,6},{8,9},{9,8},{10,11... | collective-permute-start | bytes 983048 | tf_op jit(solution)/shard_map/ppermute | solution.py:545
  182.3 4.5 shard_map.122
  190.4 5.8 %shard_map.123 = (bf16[1280,384]{1,0:T(8,128)(2,1)}, bf16[640,384]{1,0:T(8,128)(2,1)}, bf16[320,384]{1,0:T(8,128)(2,1)}, bf16[320,384]{1,0:T(8,128)(2,1)}, bf16[...) custom-call(bf16[320,384]{1,0:T(8,128)(2,1)} %copy-done.43, bf16[320,384]{1,0:T(8,128)(2,1)} %copy-done.77, ...), custom_call_target="tpu_custom_call" | custom-call | flops 1258291200 | bytes 6717440 | tf_op jit(solution)/shard_map/pallas_call | solution.py:80
  197.6 19.8 %collective-permute-done.20 = bf16[320,384]{1,0:T(8,128)(2,1)S(1)} collective-permute-done((bf16[320,384]{1,0:T(8,128)(2,1)}, bf16[320,384]{1,0:T(8,128)(2,1)S(1)}, u32[]{:S(2)}, u32[]{:S(2)}) %collective-permute-start.20) | collective-permute-done | bytes 245792 | tf_op jit(solution)/shard_map/ppermute | solution.py:545
  218.7 5.1 collective-permute-done.21
  224.3 2.4 collective-permute-start.30
  228.4 7.0 %collective-permute-done.22 = bf16[320,384]{1,0:T(8,128)(2,1)S(1)} collective-permute-done((bf16[320,384]{1,0:T(8,128)(2,1)}, bf16[320,384]{1,0:T(8,128)(2,1)S(1)}, u32[]{:S(2)}, u32[]{:S(2)}) %collective-permute-start.22) | collective-permute-done | bytes 245792 | tf_op jit(solution)/shard_map/ppermute | solution.py:545
  237.4 12.6 %collective-permute-done.30.refs_2_ = bf16[320,512]{1,0:T(8,128)(2,1)S(1)} collective-permute-done((bf16[320,512]{1,0:T(8,128)(2,1)}, bf16[320,512]{1,0:T(8,128)(2,1)S(1)}, u32[]{:S(2)}, u32[]{:S(2)}) %collective-permute-start.30) | collective-permute-done | bytes 327712 | tf_op jit(solution)/shard_map/ppermute | solution.py:545
  255.0 5.9 %shard_map.124 = (bf16[1280,512]{1,0:T(8,128)(2,1)}, bf16[640,512]{1,0:T(8,128)(2,1)}, bf16[320,512]{1,0:T(8,128)(2,1)}, bf16[320,512]{1,0:T(8,128)(2,1)}, bf16[...) custom-call(bf16[320,512]{1,0:T(8,128)(2,1)} %multiply_convert_fusion.2.refs_0_, ...), custom_call_target="tpu_custom_call" | custom-call | flops 1677721600 | bytes 7864320 | tf_op jit(solution)/shard_map/pallas_call | solution.py:80
  266.3 5.5 %shard_map.125 = (bf16[1280,384]{1,0:T(8,128)(2,1)}, bf16[320,384]{1,0:T(8,128)(2,1)}, bf16[320,384]{1,0:T(8,128)(2,1)}, bf16[320,384]{1,0:T(8,128)(2,1)}, bf16[320,384]{1,0:T(8,128)(2,1)}) custom-call(bf16[320,384]{1,0:T(8,128)(2,1)} %copy-done.44, bf16[320,384]{1,0:T(8,128)(2,1)} %copy-done.78, bf16[320,384]{1,0:T(8,128)(2,1)} %copy-done.81, ...), custom_call_target="tpu_custom_call" | custom-call | flops 1258291200 | bytes 6225920 | tf_op jit(solution)/shard_map/pallas_call | solution.py:80
  271.8 7.4 %collective-permute-done.45 = bf16[320,512]{1,0:T(8,128)(2,1)S(1)} collective-permute-done((bf16[320,512]{1,0:T(8,128)(2,1)}, bf16[320,512]{1,0:T(8,128)(2,1)S(1)}, u32[]{:S(2)}, u32[]{:S(2)}) %collective-permute-start.45) | collective-permute-done | bytes 327712 | tf_op jit(solution)/shard_map/ppermute | solution.py:545
  279.7 2.0 collective-permute-start.48
  283.2 3.8 collective-permute-done.47.refs_1_
  287.0 5.1 collective-permute-done.48.refs_2_
  293.5 5.8 %shard_map.127 = (bf16[1280,512]{1,0:T(8,128)(2,1)}, bf16[320,512]{1,0:T(8,128)(2,1)}, bf16[320,512]{1,0:T(8,128)(2,1)}, bf16[320,512]{1,0:T(8,128)(2,1)}, bf16[320,512]{1,0:T(8,128)(2,1)}) custom-call(bf16[320,512]{1,0:T(8,128)(2,1)} %copy-done.39, bf16[320,512]{1,0:T(8,128)(2,1)} %copy-done.66, bf16[320,512]{1,0:T(8,128)(2,1)} %copy-done.68, ...), custom_call_target="tpu_custom_call" | custom-call | flops 1677721600 | bytes 7208960 | tf_op jit(solution)/shard_map/pallas_call | solution.py:80
  301.2 4.5 collective-permute-done.56.refs_2_
  309.9 8.6 %shard_map.128 = f32[640,1280]{1,0:T(8,128)} custom-call(bf16[1280,384]{1,0:T(8,128)(2,1)} %get-tuple-element.213.refs_0_, bf16[1280,512]{1,0:T(8,128)(2,1)} %get-tuple-element.214.refs_1_, bf16[640,384]{1,0:T(8,128)(2,1)} %copy-done.36, bf16[640,512]{1,0:T(8,128)(2,1)} %copy-done.14, bf16[1280,384]{1,0:T(8,128)(2,1)} %get-tuple-element.216.refs_4_, ...), custom_call_target="tpu_custom_call" | custom-call | flops 2936012800 | bytes 11304960 | tf_op jit(solution)/shard_map/pallas_call | solution.py:80
  318.5 14.4 %collective-permute-done.54.refs_2_ = bf16[320,896]{1,0:T(8,128)(2,1)S(1)} collective-permute-done((bf16[320,896]{1,0:T(8,128)(2,1)S(1)}, bf16[320,896]{1,0:T(8,128)(2,1)S(1)}, u32[]{:S(2)}, u32[]{:S(2)}) %collective-permute-start.54) | collective-permute-done | bytes 573472 | tf_op jit(solution)/shard_map/ppermute | solution.py:545
  334.5 3.1 shard_map.129.refs_0_
  337.8 9.4 %collective-permute-start.50 = (bf16[320,512]{1,0:T(8,128)(2,1)S(1)}, bf16[320,512]{1,0:T(8,128)(2,1)S(1)}, u32[]{:S(2)}, u32[]{:S(2)}) collective-permute-start(bf16[320,512]{1,0:T(8,128)(2,1)S(1)} %copy-done.59), channel_id=1, source_target_pairs={{0,1},{1,0},{2,3},{3,2},{4,5},{5,4},{6,7},{7,6},{8,9},{9,8},{10,11... | collective-permute-start | bytes 983048 | tf_op jit(solution)/shard_map/ppermute | solution.py:545
  347.9 1.7 collective-permute-start.52
  349.6 12.2 %collective-permute-done.50 = bf16[320,512]{1,0:T(8,128)(2,1)S(1)} collective-permute-done((bf16[320,512]{1,0:T(8,128)(2,1)S(1)}, bf16[320,512]{1,0:T(8,128)(2,1)S(1)}, u32[]{:S(2)}, u32[]{:S(2)}) %collective-permute-start.50) | collective-permute-done | bytes 327712 | tf_op jit(solution)/shard_map/ppermute | solution.py:545
  361.8 10.9 %collective-permute-done.51 = bf16[320,512]{1,0:T(8,128)(2,1)S(1)} collective-permute-done((bf16[320,512]{1,0:T(8,128)(2,1)S(1)}, bf16[320,512]{1,0:T(8,128)(2,1)S(1)}, u32[]{:S(2)}, u32[]{:S(2)}) %collective-permute-start.51) | collective-permute-done | bytes 327712 | tf_op jit(solution)/shard_map/ppermute | solution.py:545
  373.3 6.8 %collective-permute-start.60 = (bf16[320,512]{1,0:T(8,128)(2,1)S(1)}, bf16[320,512]{1,0:T(8,128)(2,1)S(1)}, u32[]{:S(2)}, u32[]{:S(2)}) collective-permute-start(bf16[320,512]{1,0:T(8,128)(2,1)S(1)} %multiply_convert_fusion.refs_0_), channel_id=1, source_target_pairs={{0,1},{1,0},{2,3},{3,2},{4,5},{5,4},{6,7},{7,6},{8,9},{9,8},{10,11... | collective-permute-start | bytes 983048 | tf_op jit(solution)/shard_map/ppermute | solution.py:545
  380.2 2.6 collective-permute-start.36
  382.8 1.7 collective-permute-start.37
  384.5 9.4 %collective-permute-done.60.refs_1_ = bf16[320,512]{1,0:T(8,128)(2,1)S(1)} collective-permute-done((bf16[320,512]{1,0:T(8,128)(2,1)S(1)}, bf16[320,512]{1,0:T(8,128)(2,1)S(1)}, u32[]{:S(2)}, u32[]{:S(2)}) %collective-permute-start.60) | collective-permute-done | bytes 327712 | tf_op jit(solution)/shard_map/ppermute | solution.py:545
  394.2 2.0 collective-permute-start.62
  396.2 23.0 %shard_map.130 = f32[9,1280,640]{2,1,0:T(8,128)} custom-call(bf16[1280,896]{1,0:T(8,128)(2,1)} %shard_map.129.refs_0_, bf16[1280,896]{1,0:T(8,128)(2,1)} %collective-permute-done.63.refs_1_, bf16[2,640,196]{2,1,0:T(8,128)(2,1)} %copy-done.16), custom_call_target="tpu_custom_call" | custom-call | flops 11560550400 | bytes 29491200 | tf_op jit(solution)/shard_map/pallas_call | solution.py:349
  419.2 6.9 %collective-permute-done.61.refs_2_ = bf16[320,512]{1,0:T(8,128)(2,1)S(1)} collective-permute-done((bf16[320,512]{1,0:T(8,128)(2,1)S(1)}, bf16[320,512]{1,0:T(8,128)(2,1)S(1)}, u32[]{:S(2)}, u32[]{:S(2)}) %collective-permute-start.61) | collective-permute-done | bytes 327712 | tf_op jit(solution)/shard_map/ppermute | solution.py:545
  427.6 4.3 shard_map.131
  432.3 6.2 %collective-permute-start.38 = (bf16[320,384]{1,0:T(8,128)(2,1)S(1)}, bf16[320,384]{1,0:T(8,128)(2,1)S(1)}, u32[]{:S(2)}, u32[]{:S(2)}) collective-permute-start(bf16[320,384]{1,0:T(8,128)(2,1)S(1)} %multiply_convert_fusion.4.refs_0_), channel_id=1, source_target_pairs={{0,1},{1,0},{2,3},{3,2},{4,5},{5,4},{6,7},{7,6},{8,9},{9,8},{10,11... | collective-permute-start | bytes 737288 | tf_op jit(solution)/shard_map/ppermute | solution.py:545
  439.0 1.9 collective-permute-start.40
  440.9 8.7 %collective-permute-done.38.refs_1_ = bf16[320,384]{1,0:T(8,128)(2,1)S(1)} collective-permute-done((bf16[320,384]{1,0:T(8,128)(2,1)S(1)}, bf16[320,384]{1,0:T(8,128)(2,1)S(1)}, u32[]{:S(2)}, u32[]{:S(2)}) %collective-permute-start.38) | collective-permute-done | bytes 245792 | tf_op jit(solution)/shard_map/ppermute | solution.py:545
  449.7 9.1 %collective-permute-done.39.refs_2_ = bf16[320,384]{1,0:T(8,128)(2,1)S(1)} collective-permute-done((bf16[320,384]{1,0:T(8,128)(2,1)S(1)}, bf16[320,384]{1,0:T(8,128)(2,1)S(1)}, u32[]{:S(2)}, u32[]{:S(2)}) %collective-permute-start.39) | collective-permute-done | bytes 245792 | tf_op jit(solution)/shard_map/ppermute | solution.py:545
  460.2 4.2 shard_map.126
  467.9 2.9 collective-permute-done.41
  471.1 1.9 collective-permute-start.67
  474.5 8.3 %shard_map.132 = f32[640,1280]{1,0:T(8,128)} custom-call(bf16[640,384]{1,0:T(8,128)(2,1)} %all_gather.13.x_ref.refs_0_, bf16[640,512]{1,0:T(8,128)(2,1)} %all_gather.14.x_ref.refs_1_, bf16[640,384]{1,0:T(8,128)(2,1)} %copy-done.56, bf16[640,512]{1,0:T(8,128)(2,1)} %copy-done.55, bf16[1280,384]{1,0:T(8,128)(2,1)} %get-tuple-element.202.refs_4_, ...), custom_call_target="tpu_custom_call" | custom-call | flops 2936012800 | bytes 10158080 | tf_op jit(solution)/shard_map/pallas_call | solution.py:80
  484.2 12.7 %all_gather.15.m_ref.ma_ref = bf16[640,784]{1,0:T(8,128)(2,1)S(1)} all-gather(bf16[160,784]{1,0:T(8,128)(2,1)S(1)} %pad_maximum_fusion.2), channel_id=1, replica_groups=mesh['section'=2,'cin'=4,'cout'=4] {'cin'}, dimensions={0}, use_global_device_ids=true | all-gather | bytes 1254400 | tf_op jit(solution)/shard_map/all_gather | solution.py:578
  498.1 14.0 %shard_map.133 = (bf16[160,784]{1,0:T(8,128)(2,1)}, bf16[160,784]{1,0:T(8,128)(2,1)}, bf16[160,784]{1,0:T(8,128)(2,1)}, bf16[160,784]{1,0:T(8,128)(2,1)}) custom-call(bf16[640,784]{1,0:T(8,128)(2,1)} %copy-done.10, bf16[9,640,640]{2,1,0:T(8,128)(2,1)} %w_ref.9), custom_call_target="tpu_custom_call" | custom-call | flops 6606028800 | bytes 9666560 | tf_op jit(solution)/shard_map/pallas_call | solution.py:188
  512.2 4.4 collective-permute-start.69
  517.0 1.9 collective-permute-start.71
  520.0 25.6 %shard_map.134 = f32[9,640,640]{2,1,0:T(8,128)} custom-call(bf16[640,784]{1,0:T(8,128)(2,1)} %bitcast.23, bf16[640,784]{1,0:T(8,128)(2,1)} %bitcast.31, bf16[640,784]{1,0:T(8,128)(2,1)} %copy-done.10, bf16[640,784]{1,0:T(8,128)(2,1)} %bitcast.32), custom_call_target="tpu_custom_call" | custom-call | flops 13212057600 | bytes 14745600 | tf_op jit(solution)/shard_map/pallas_call | solution.py:229
  (295 shorter events, 59.0 us)
Async XLA Ops:
  42.6 8.8 %collective-permute-start.7 = (bf16[160,384]{1,0:T(8,128)(2,1)}, bf16[160,384]{1,0:T(8,128)(2,1)S(1)}, u32[]{:S(2)}, u32[]{:S(2)}) collective-permute-start(bf16[160,384]{1,0:T(8,128)(2,1)} %get-tuple-element.132), channel_id=1, source_target_pairs={{0,8},{4,12},{8,0},{12,4},{1,9},{5,13},{9,1},{13,5},{2,10},{6,14},... | collective-permute-start | bytes 368648 | tf_op jit(solution)/shard_map/ppermute | solution.py:545
  44.5 32.7 %collective-permute-start.3 = (bf16[160,512]{1,0:T(8,128)(2,1)}, bf16[160,512]{1,0:T(8,128)(2,1)S(1)}, u32[]{:S(2)}, u32[]{:S(2)}) collective-permute-start(bf16[160,512]{1,0:T(8,128)(2,1)} %get-tuple-element.135), channel_id=1, source_target_pairs={{0,4},{4,0},{8,12},{12,8},{1,5},{5,1},{9,13},{13,9},{2,6},{6,2},{1... | collective-permute-start | bytes 491528 | tf_op jit(solution)/shard_map/ppermute | solution.py:545
  46.1 31.2 %collective-permute-start.4 = (bf16[160,512]{1,0:T(8,128)(2,1)}, bf16[160,512]{1,0:T(8,128)(2,1)S(1)}, u32[]{:S(2)}, u32[]{:S(2)}) collective-permute-start(bf16[160,512]{1,0:T(8,128)(2,1)} %get-tuple-element.136), channel_id=1, source_target_pairs={{0,8},{4,12},{8,0},{12,4},{1,9},{5,13},{9,1},{13,5},{2,10},{6,14},... | collective-permute-start | bytes 491528 | tf_op jit(solution)/shard_map/ppermute | solution.py:545
  47.7 29.6 %collective-permute-start.5 = (bf16[160,512]{1,0:T(8,128)(2,1)}, bf16[160,512]{1,0:T(8,128)(2,1)S(1)}, u32[]{:S(2)}, u32[]{:S(2)}) collective-permute-start(bf16[160,512]{1,0:T(8,128)(2,1)} %get-tuple-element.137), channel_id=1, source_target_pairs={{0,12},{4,8},{8,4},{12,0},{1,13},{5,9},{9,5},{13,1},{2,14},{6,10},... | collective-permute-start | bytes 491528 | tf_op jit(solution)/shard_map/ppermute | solution.py:545
  51.3 18.7 %collective-permute-start = (bf16[2,160,196]{2,1,0:T(8,128)(2,1)S(1)}, bf16[2,160,196]{2,1,0:T(8,128)(2,1)S(1)}, u32[]{:S(2)}, u32[]{:S(2)}) collective-permute-start(bf16[2,160,196]{2,1,0:T(8,128)(2,1)S(1)} %bitcast.28), channel_id=1, source_target_pairs={{0,1},{1,0},{2,3},{3,2},{4,5},{5,4},{6,7},{7,6},{8,9},{9,8},{10,11... | collective-permute-start | bytes 376328 | tf_op jit(solution)/shard_map/ppermute | solution.py:572
  51.4 20.3 %collective-permute-start.1 = (bf16[2,160,196]{2,1,0:T(8,128)(2,1)S(1)}, bf16[2,160,196]{2,1,0:T(8,128)(2,1)S(1)}, u32[]{:S(2)}, u32[]{:S(2)}) collective-permute-start(bf16[2,160,196]{2,1,0:T(8,128)(2,1)S(1)} %bitcast.29), channel_id=1, source_target_pairs={{0,2},{1,3},{2,0},{3,1},{4,6},{5,7},{6,4},{7,5},{8,10},{9,11},{10,... | collective-permute-start | bytes 376328 | tf_op jit(solution)/shard_map/ppermute | solution.py:572
  115.0 50.0 %collective-permute-start.9 = (bf16[1280,896]{1,0:T(8,128)(2,1)}, bf16[1280,896]{1,0:T(8,128)(2,1)S(1)}, u32[]{:S(2)}, u32[]{:S(2)}) collective-permute-start(bf16[1280,896]{1,0:T(8,128)(2,1)} %get-tuple-element.153), channel_id=1, source_target_pairs={{0,16},{16,0},{1,17},{17,1},{2,18},{18,2},{3,19},{19,3},{4,20},{20... | collective-permute-start | bytes 6881288 | tf_op jit(solution)/shard_map/ppermute | solution.py:530
  115.1 75.3 %collective-permute-start.19 = (bf16[640,1280]{1,0:T(8,128)(2,1)}, bf16[640,1280]{1,0:T(8,128)(2,1)}, u32[]{:S(2)}, u32[]{:S(2)}) collective-permute-start(bf16[640,1280]{1,0:T(8,128)(2,1)} %refs_4_.10), channel_id=1, source_target_pairs={{0,16},{16,0},{1,17},{17,1},{2,18},{18,2},{3,19},{19,3},{4,20},{20... | collective-permute-start | bytes 4915208 | tf_op jit(solution)/shard_map/ppermute | solution.py:530
  115.6 12.1 %collective-permute-start.13 = (bf16[320,384]{1,0:T(8,128)(2,1)S(1)}, bf16[320,384]{1,0:T(8,128)(2,1)S(1)}, u32[]{:S(2)}, u32[]{:S(2)}) collective-permute-start(bf16[320,384]{1,0:T(8,128)(2,1)S(1)} %copy-done.76), channel_id=1, source_target_pairs={{0,1},{1,0},{2,3},{3,2},{4,5},{5,4},{6,7},{7,6},{8,9},{9,8},{10,11... | collective-permute-start | bytes 737288 | tf_op jit(solution)/shard_map/ppermute | solution.py:545
  115.6 20.4 %collective-permute-start.14 = (bf16[320,384]{1,0:T(8,128)(2,1)S(1)}, bf16[320,384]{1,0:T(8,128)(2,1)S(1)}, u32[]{:S(2)}, u32[]{:S(2)}) collective-permute-start(bf16[320,384]{1,0:T(8,128)(2,1)S(1)} %copy-done.75), channel_id=1, source_target_pairs={{0,2},{1,3},{2,0},{3,1},{4,6},{5,7},{6,4},{7,5},{8,10},{9,11},{10,... | collective-permute-start | bytes 737288 | tf_op jit(solution)/shard_map/ppermute | solution.py:545
  117.7 18.3 %collective-permute-start.15 = (bf16[320,384]{1,0:T(8,128)(2,1)S(1)}, bf16[320,384]{1,0:T(8,128)(2,1)S(1)}, u32[]{:S(2)}, u32[]{:S(2)}) collective-permute-start(bf16[320,384]{1,0:T(8,128)(2,1)S(1)} %copy-done.74), channel_id=1, source_target_pairs={{0,3},{1,2},{2,1},{3,0},{4,7},{5,6},{6,5},{7,4},{8,11},{9,10},{10,... | collective-permute-start | bytes 737288 | tf_op jit(solution)/shard_map/ppermute | solution.py:545
  127.7 15.2 %collective-permute-start.26 = (bf16[320,512]{1,0:T(8,128)(2,1)S(1)}, bf16[320,512]{1,0:T(8,128)(2,1)S(1)}, u32[]{:S(2)}, u32[]{:S(2)}) collective-permute-start(bf16[320,512]{1,0:T(8,128)(2,1)S(1)} %copy-done.63), channel_id=1, source_target_pairs={{0,1},{1,0},{2,3},{3,2},{4,5},{5,4},{6,7},{7,6},{8,9},{9,8},{10,11... | collective-permute-start | bytes 983048 | tf_op jit(solution)/shard_map/ppermute | solution.py:545
  136.0 26.3 %collective-permute-start.27 = (bf16[320,512]{1,0:T(8,128)(2,1)S(1)}, bf16[320,512]{1,0:T(8,128)(2,1)S(1)}, u32[]{:S(2)}, u32[]{:S(2)}) collective-permute-start(bf16[320,512]{1,0:T(8,128)(2,1)S(1)} %copy-done.62), channel_id=1, source_target_pairs={{0,2},{1,3},{2,0},{3,1},{4,6},{5,7},{6,4},{7,5},{8,10},{9,11},{10,... | collective-permute-start | bytes 983048 | tf_op jit(solution)/shard_map/ppermute | solution.py:545
  136.1 26.3 %collective-permute-start.28 = (bf16[320,512]{1,0:T(8,128)(2,1)S(1)}, bf16[320,512]{1,0:T(8,128)(2,1)S(1)}, u32[]{:S(2)}, u32[]{:S(2)}) collective-permute-start(bf16[320,512]{1,0:T(8,128)(2,1)S(1)} %copy-done.60), channel_id=1, source_target_pairs={{0,3},{1,2},{2,1},{3,0},{4,7},{5,6},{6,5},{7,4},{8,11},{9,10},{10,... | collective-permute-start | bytes 983048 | tf_op jit(solution)/shard_map/ppermute | solution.py:545
  142.9 43.9 %collective-permute-start.16 = (bf16[320,384]{1,0:T(8,128)(2,1)S(1)}, bf16[320,384]{1,0:T(8,128)(2,1)S(1)}, u32[]{:S(2)}, u32[]{:S(2)}) collective-permute-start(bf16[320,384]{1,0:T(8,128)(2,1)S(1)} %multiply_convert_fusion.5.refs_0_), channel_id=1, source_target_pairs={{0,1},{1,0},{2,3},{3,2},{4,5},{5,4},{6,7},{7,6},{8,9},{9,8},{10,11... | collective-permute-start | bytes 737288 | tf_op jit(solution)/shard_map/ppermute | solution.py:545
  162.4 25.8 %collective-permute-start.17 = (bf16[320,384]{1,0:T(8,128)(2,1)S(1)}, bf16[320,384]{1,0:T(8,128)(2,1)S(1)}, u32[]{:S(2)}, u32[]{:S(2)}) collective-permute-start(bf16[320,384]{1,0:T(8,128)(2,1)S(1)} %multiply_convert_fusion.5.refs_0_), channel_id=1, source_target_pairs={{0,2},{1,3},{2,0},{3,1},{4,6},{5,7},{6,4},{7,5},{8,10},{9,11},{10,... | collective-permute-start | bytes 737288 | tf_op jit(solution)/shard_map/ppermute | solution.py:545
  162.4 26.5 %collective-permute-start.18 = (bf16[320,384]{1,0:T(8,128)(2,1)S(1)}, bf16[320,384]{1,0:T(8,128)(2,1)S(1)}, u32[]{:S(2)}, u32[]{:S(2)}) collective-permute-start(bf16[320,384]{1,0:T(8,128)(2,1)S(1)} %multiply_convert_fusion.5.refs_0_), channel_id=1, source_target_pairs={{0,3},{1,2},{2,1},{3,0},{4,7},{5,6},{6,5},{7,4},{8,11},{9,10},{10,... | collective-permute-start | bytes 737288 | tf_op jit(solution)/shard_map/ppermute | solution.py:545
  165.1 32.5 %collective-permute-start.29 = (bf16[320,512]{1,0:T(8,128)(2,1)}, bf16[320,512]{1,0:T(8,128)(2,1)}, u32[]{:S(2)}, u32[]{:S(2)}) collective-permute-start(bf16[320,512]{1,0:T(8,128)(2,1)} %multiply_convert_fusion.2.refs_0_), channel_id=1, source_target_pairs={{0,1},{1,0},{2,3},{3,2},{4,5},{5,4},{6,7},{7,6},{8,9},{9,8},{10,11... | collective-permute-start | bytes 983048 | tf_op jit(solution)/shard_map/ppermute | solution.py:545
  186.8 36.9 %collective-permute-start.10 = (bf16[320,896]{1,0:T(8,128)(2,1)}, bf16[320,896]{1,0:T(8,128)(2,1)S(1)}, u32[]{:S(2)}, u32[]{:S(2)}) collective-permute-start(bf16[320,896]{1,0:T(8,128)(2,1)} %get-tuple-element.155), channel_id=1, source_target_pairs={{0,4},{4,0},{8,12},{12,8},{1,5},{5,1},{9,13},{13,9},{2,6},{6,2},{1... | collective-permute-start | bytes 1720328 | tf_op jit(solution)/shard_map/ppermute | solution.py:545
  188.2 36.1 %collective-permute-start.11 = (bf16[320,896]{1,0:T(8,128)(2,1)}, bf16[320,896]{1,0:T(8,128)(2,1)S(1)}, u32[]{:S(2)}, u32[]{:S(2)}) collective-permute-start(bf16[320,896]{1,0:T(8,128)(2,1)} %get-tuple-element.156), channel_id=1, source_target_pairs={{0,8},{4,12},{8,0},{12,4},{1,9},{5,13},{9,1},{13,5},{2,10},{6,14},... | collective-permute-start | bytes 1720328 | tf_op jit(solution)/shard_map/ppermute | solution.py:545
  188.9 37.8 %collective-permute-start.12 = (bf16[320,896]{1,0:T(8,128)(2,1)}, bf16[320,896]{1,0:T(8,128)(2,1)S(1)}, u32[]{:S(2)}, u32[]{:S(2)}) collective-permute-start(bf16[320,896]{1,0:T(8,128)(2,1)} %get-tuple-element.157), channel_id=1, source_target_pairs={{0,12},{4,8},{8,4},{12,0},{1,13},{5,9},{9,5},{13,1},{2,14},{6,10},... | collective-permute-start | bytes 1720328 | tf_op jit(solution)/shard_map/ppermute | solution.py:545
  196.2 21.1 %collective-permute-start.20 = (bf16[320,384]{1,0:T(8,128)(2,1)}, bf16[320,384]{1,0:T(8,128)(2,1)S(1)}, u32[]{:S(2)}, u32[]{:S(2)}) collective-permute-start(bf16[320,384]{1,0:T(8,128)(2,1)} %get-tuple-element.168), channel_id=1, source_target_pairs={{0,4},{4,0},{8,12},{12,8},{1,5},{5,1},{9,13},{13,9},{2,6},{6,2},{1... | collective-permute-start | bytes 737288 | tf_op jit(solution)/shard_map/ppermute | solution.py:545
  197.6 53.8 %collective-permute-start.32 = (bf16[4,160,784]{2,1,0:T(8,128)(2,1)S(1)}, bf16[4,160,784]{2,1,0:T(8,128)(2,1)S(1)}, u32[]{:S(2)}, u32[]{:S(2)}) collective-permute-start(bf16[4,160,784]{2,1,0:T(8,128)(2,1)S(1)} %bitcast.24), channel_id=1, source_target_pairs={{0,16},{16,0},{1,17},{17,1},{2,18},{18,2},{3,19},{19,3},{4,20},{20... | collective-permute-start | bytes 3010568 | tf_op jit(solution)/shard_map/ppermute | solution.py:530
  223.7 27.6 %collective-permute-start.34 = (bf16[640,512]{1,0:T(8,128)(2,1)S(1)}, bf16[640,512]{1,0:T(8,128)(2,1)S(1)}, u32[]{:S(2)}, u32[]{:S(2)}) collective-permute-start(bf16[640,512]{1,0:T(8,128)(2,1)S(1)} %copy-done.15), channel_id=1, source_target_pairs={{0,16},{16,0},{1,17},{17,1},{2,18},{18,2},{3,19},{19,3},{4,20},{20... | collective-permute-start | bytes 1966088 | tf_op jit(solution)/shard_map/ppermute | solution.py:530
  223.8 27.6 %collective-permute-start.33 = (bf16[640,384]{1,0:T(8,128)(2,1)}, bf16[640,384]{1,0:T(8,128)(2,1)S(1)}, u32[]{:S(2)}, u32[]{:S(2)}) collective-permute-start(bf16[640,384]{1,0:T(8,128)(2,1)} %all_gather.13.x_ref.refs_0_), channel_id=1, source_target_pairs={{0,16},{16,0},{1,17},{17,1},{2,18},{18,2},{3,19},{19,3},{4,20},{20... | collective-permute-start | bytes 1474568 | tf_op jit(solution)/shard_map/ppermute | solution.py:530
  224.3 25.7 %collective-permute-start.30 = (bf16[320,512]{1,0:T(8,128)(2,1)}, bf16[320,512]{1,0:T(8,128)(2,1)S(1)}, u32[]{:S(2)}, u32[]{:S(2)}) collective-permute-start(bf16[320,512]{1,0:T(8,128)(2,1)} %multiply_convert_fusion.2.refs_0_), channel_id=1, source_target_pairs={{0,2},{1,3},{2,0},{3,1},{4,6},{5,7},{6,4},{7,5},{8,10},{9,11},{10,... | collective-permute-start | bytes 983048 | tf_op jit(solution)/shard_map/ppermute | solution.py:545
  226.7 8.8 %collective-permute-start.22 = (bf16[320,384]{1,0:T(8,128)(2,1)}, bf16[320,384]{1,0:T(8,128)(2,1)S(1)}, u32[]{:S(2)}, u32[]{:S(2)}) collective-permute-start(bf16[320,384]{1,0:T(8,128)(2,1)} %get-tuple-element.170), channel_id=1, source_target_pairs={{0,12},{4,8},{8,4},{12,0},{1,13},{5,9},{9,5},{13,1},{2,14},{6,10},... | collective-permute-start | bytes 737288 | tf_op jit(solution)/shard_map/ppermute | solution.py:545
  235.5 15.9 %collective-permute-start.31 = (bf16[320,512]{1,0:T(8,128)(2,1)}, bf16[320,512]{1,0:T(8,128)(2,1)S(1)}, u32[]{:S(2)}, u32[]{:S(2)}) collective-permute-start(bf16[320,512]{1,0:T(8,128)(2,1)} %multiply_convert_fusion.2.refs_0_), channel_id=1, source_target_pairs={{0,3},{1,2},{2,1},{3,0},{4,7},{5,6},{6,5},{7,4},{8,11},{9,10},{10,... | collective-permute-start | bytes 983048 | tf_op jit(solution)/shard_map/ppermute | solution.py:545
  250.0 12.9 %collective-permute-start.23 = (bf16[320,384]{1,0:T(8,128)(2,1)S(1)}, bf16[320,384]{1,0:T(8,128)(2,1)S(1)}, u32[]{:S(2)}, u32[]{:S(2)}) collective-permute-start(bf16[320,384]{1,0:T(8,128)(2,1)S(1)} %get-tuple-element.190.refs_0_), channel_id=1, source_target_pairs={{0,4},{4,0},{8,12},{12,8},{1,5},{5,1},{9,13},{13,9},{2,6},{6,2},{1... | collective-permute-start | bytes 737288 | tf_op jit(solution)/shard_map/ppermute | solution.py:545
  252.8 12.7 %collective-permute-start.24 = (bf16[320,384]{1,0:T(8,128)(2,1)S(1)}, bf16[320,384]{1,0:T(8,128)(2,1)S(1)}, u32[]{:S(2)}, u32[]{:S(2)}) collective-permute-start(bf16[320,384]{1,0:T(8,128)(2,1)S(1)} %get-tuple-element.190.refs_0_), channel_id=1, source_target_pairs={{0,8},{4,12},{8,0},{12,4},{1,9},{5,13},{9,1},{13,5},{2,10},{6,14},... | collective-permute-start | bytes 737288 | tf_op jit(solution)/shard_map/ppermute | solution.py:545
  253.5 12.0 %collective-permute-start.25 = (bf16[320,384]{1,0:T(8,128)(2,1)S(1)}, bf16[320,384]{1,0:T(8,128)(2,1)S(1)}, u32[]{:S(2)}, u32[]{:S(2)}) collective-permute-start(bf16[320,384]{1,0:T(8,128)(2,1)S(1)} %get-tuple-element.190.refs_0_), channel_id=1, source_target_pairs={{0,12},{4,8},{8,4},{12,0},{1,13},{5,9},{9,5},{13,1},{2,14},{6,10},... | collective-permute-start | bytes 737288 | tf_op jit(solution)/shard_map/ppermute | solution.py:545
  260.9 10.9 %collective-permute-start.44 = (bf16[320,512]{1,0:T(8,128)(2,1)}, bf16[320,512]{1,0:T(8,128)(2,1)S(1)}, u32[]{:S(2)}, u32[]{:S(2)}) collective-permute-start(bf16[320,512]{1,0:T(8,128)(2,1)} %get-tuple-element.187), channel_id=1, source_target_pairs={{0,4},{4,0},{8,12},{12,8},{1,5},{5,1},{9,13},{13,9},{2,6},{6,2},{1... | collective-permute-start | bytes 983048 | tf_op jit(solution)/shard_map/ppermute | solution.py:545
  262.2 17.0 %collective-permute-start.45 = (bf16[320,512]{1,0:T(8,128)(2,1)}, bf16[320,512]{1,0:T(8,128)(2,1)S(1)}, u32[]{:S(2)}, u32[]{:S(2)}) collective-permute-start(bf16[320,512]{1,0:T(8,128)(2,1)} %get-tuple-element.188), channel_id=1, source_target_pairs={{0,8},{4,12},{8,0},{12,4},{1,9},{5,13},{9,1},{13,5},{2,10},{6,14},... | collective-permute-start | bytes 983048 | tf_op jit(solution)/shard_map/ppermute | solution.py:545
  262.9 16.3 %collective-permute-start.46 = (bf16[320,512]{1,0:T(8,128)(2,1)}, bf16[320,512]{1,0:T(8,128)(2,1)S(1)}, u32[]{:S(2)}, u32[]{:S(2)}) collective-permute-start(bf16[320,512]{1,0:T(8,128)(2,1)} %get-tuple-element.189), channel_id=1, source_target_pairs={{0,12},{4,8},{8,4},{12,0},{1,13},{5,9},{9,5},{13,1},{2,14},{6,10},... | collective-permute-start | bytes 983048 | tf_op jit(solution)/shard_map/ppermute | solution.py:545
  279.7 12.3 %collective-permute-start.48 = (bf16[320,512]{1,0:T(8,128)(2,1)S(1)}, bf16[320,512]{1,0:T(8,128)(2,1)S(1)}, u32[]{:S(2)}, u32[]{:S(2)}) collective-permute-start(bf16[320,512]{1,0:T(8,128)(2,1)S(1)} %get-tuple-element.255.refs_0_), channel_id=1, source_target_pairs={{0,8},{4,12},{8,0},{12,4},{1,9},{5,13},{9,1},{13,5},{2,10},{6,14},... | collective-permute-start | bytes 983048 | tf_op jit(solution)/shard_map/ppermute | solution.py:545
  281.7 10.3 %collective-permute-start.49 = (bf16[320,512]{1,0:T(8,128)(2,1)S(1)}, bf16[320,512]{1,0:T(8,128)(2,1)S(1)}, u32[]{:S(2)}, u32[]{:S(2)}) collective-permute-start(bf16[320,512]{1,0:T(8,128)(2,1)S(1)} %get-tuple-element.255.refs_0_), channel_id=1, source_target_pairs={{0,12},{4,8},{8,4},{12,0},{1,13},{5,9},{9,5},{13,1},{2,14},{6,10},... | collective-permute-start | bytes 983048 | tf_op jit(solution)/shard_map/ppermute | solution.py:545
  299.3 9.5 %collective-permute-start.59 = (bf16[1280,512]{1,0:T(8,128)(2,1)}, bf16[1280,512]{1,0:T(8,128)(2,1)S(1)}, u32[]{:S(2)}, u32[]{:S(2)}) collective-permute-start(bf16[1280,512]{1,0:T(8,128)(2,1)} %get-tuple-element.219.refs_5_), channel_id=1, source_target_pairs={{0,16},{16,0},{1,17},{17,1},{2,18},{18,2},{3,19},{19,3},{4,20},{20... | collective-permute-start | bytes 3932168 | tf_op jit(solution)/shard_map/ppermute | solution.py:530
  299.3 8.5 %collective-permute-start.58 = (bf16[1280,384]{1,0:T(8,128)(2,1)S(1)}, bf16[1280,384]{1,0:T(8,128)(2,1)S(1)}, u32[]{:S(2)}, u32[]{:S(2)}) collective-permute-start(bf16[1280,384]{1,0:T(8,128)(2,1)S(1)} %copy-done.12), channel_id=1, source_target_pairs={{0,16},{16,0},{1,17},{17,1},{2,18},{18,2},{3,19},{19,3},{4,20},{20... | collective-permute-start | bytes 2949128 | tf_op jit(solution)/shard_map/ppermute | solution.py:530
  300.4 18.1 %collective-permute-start.53 = (bf16[320,896]{1,0:T(8,128)(2,1)S(1)}, bf16[320,896]{1,0:T(8,128)(2,1)S(1)}, u32[]{:S(2)}, u32[]{:S(2)}) collective-permute-start(bf16[320,896]{1,0:T(8,128)(2,1)S(1)} %pad_maximum_fusion.1.refs_0_), channel_id=1, source_target_pairs={{0,4},{4,0},{8,12},{12,8},{1,5},{5,1},{9,13},{13,9},{2,6},{6,2},{1... | collective-permute-start | bytes 1720328 | tf_op jit(solution)/shard_map/ppermute | solution.py:545
  305.6 27.3 %collective-permute-start.54 = (bf16[320,896]{1,0:T(8,128)(2,1)S(1)}, bf16[320,896]{1,0:T(8,128)(2,1)S(1)}, u32[]{:S(2)}, u32[]{:S(2)}) collective-permute-start(bf16[320,896]{1,0:T(8,128)(2,1)S(1)} %pad_maximum_fusion.1.refs_0_), channel_id=1, source_target_pairs={{0,8},{4,12},{8,0},{12,4},{1,9},{5,13},{9,1},{13,5},{2,10},{6,14},... | collective-permute-start | bytes 1720328 | tf_op jit(solution)/shard_map/ppermute | solution.py:545
  306.4 26.5 %collective-permute-start.55 = (bf16[320,896]{1,0:T(8,128)(2,1)S(1)}, bf16[320,896]{1,0:T(8,128)(2,1)S(1)}, u32[]{:S(2)}, u32[]{:S(2)}) collective-permute-start(bf16[320,896]{1,0:T(8,128)(2,1)S(1)} %pad_maximum_fusion.1.refs_0_), channel_id=1, source_target_pairs={{0,12},{4,8},{8,4},{12,0},{1,13},{5,9},{9,5},{13,1},{2,14},{6,10},... | collective-permute-start | bytes 1720328 | tf_op jit(solution)/shard_map/ppermute | solution.py:545
  337.7 56.5 %collective-permute-start.63 = (bf16[1280,896]{1,0:T(8,128)(2,1)}, bf16[1280,896]{1,0:T(8,128)(2,1)}, u32[]{:S(2)}, u32[]{:S(2)}) collective-permute-start(bf16[1280,896]{1,0:T(8,128)(2,1)} %shard_map.129.refs_0_), channel_id=1, source_target_pairs={{0,16},{16,0},{1,17},{17,1},{2,18},{18,2},{3,19},{19,3},{4,20},{20... | collective-permute-start | bytes 6881288 | tf_op jit(solution)/shard_map/ppermute | solution.py:530
  337.8 24.0 %collective-permute-start.50 = (bf16[320,512]{1,0:T(8,128)(2,1)S(1)}, bf16[320,512]{1,0:T(8,128)(2,1)S(1)}, u32[]{:S(2)}, u32[]{:S(2)}) collective-permute-start(bf16[320,512]{1,0:T(8,128)(2,1)S(1)} %copy-done.59), channel_id=1, source_target_pairs={{0,1},{1,0},{2,3},{3,2},{4,5},{5,4},{6,7},{7,6},{8,9},{9,8},{10,11... | collective-permute-start | bytes 983048 | tf_op jit(solution)/shard_map/ppermute | solution.py:545
  347.1 25.6 %collective-permute-start.51 = (bf16[320,512]{1,0:T(8,128)(2,1)S(1)}, bf16[320,512]{1,0:T(8,128)(2,1)S(1)}, u32[]{:S(2)}, u32[]{:S(2)}) collective-permute-start(bf16[320,512]{1,0:T(8,128)(2,1)S(1)} %copy-done.58), channel_id=1, source_target_pairs={{0,2},{1,3},{2,0},{3,1},{4,6},{5,7},{6,4},{7,5},{8,10},{9,11},{10,... | collective-permute-start | bytes 983048 | tf_op jit(solution)/shard_map/ppermute | solution.py:545
  347.9 24.8 %collective-permute-start.52 = (bf16[320,512]{1,0:T(8,128)(2,1)S(1)}, bf16[320,512]{1,0:T(8,128)(2,1)S(1)}, u32[]{:S(2)}, u32[]{:S(2)}) collective-permute-start(bf16[320,512]{1,0:T(8,128)(2,1)S(1)} %copy-done.57), channel_id=1, source_target_pairs={{0,3},{1,2},{2,1},{3,0},{4,7},{5,6},{6,5},{7,4},{8,11},{9,10},{10,... | collective-permute-start | bytes 983048 | tf_op jit(solution)/shard_map/ppermute | solution.py:545
  373.3 20.7 %collective-permute-start.60 = (bf16[320,512]{1,0:T(8,128)(2,1)S(1)}, bf16[320,512]{1,0:T(8,128)(2,1)S(1)}, u32[]{:S(2)}, u32[]{:S(2)}) collective-permute-start(bf16[320,512]{1,0:T(8,128)(2,1)S(1)} %multiply_convert_fusion.refs_0_), channel_id=1, source_target_pairs={{0,1},{1,0},{2,3},{3,2},{4,5},{5,4},{6,7},{7,6},{8,9},{9,8},{10,11... | collective-permute-start | bytes 983048 | tf_op jit(solution)/shard_map/ppermute | solution.py:545
  380.1 51.7 %collective-permute-start.35 = (bf16[320,384]{1,0:T(8,128)(2,1)S(1)}, bf16[320,384]{1,0:T(8,128)(2,1)S(1)}, u32[]{:S(2)}, u32[]{:S(2)}) collective-permute-start(bf16[320,384]{1,0:T(8,128)(2,1)S(1)} %copy-done.73), channel_id=1, source_target_pairs={{0,1},{1,0},{2,3},{3,2},{4,5},{5,4},{6,7},{7,6},{8,9},{9,8},{10,11... | collective-permute-start | bytes 737288 | tf_op jit(solution)/shard_map/ppermute | solution.py:545
  380.2 51.6 %collective-permute-start.36 = (bf16[320,384]{1,0:T(8,128)(2,1)S(1)}, bf16[320,384]{1,0:T(8,128)(2,1)S(1)}, u32[]{:S(2)}, u32[]{:S(2)}) collective-permute-start(bf16[320,384]{1,0:T(8,128)(2,1)S(1)} %copy-done.72), channel_id=1, source_target_pairs={{0,2},{1,3},{2,0},{3,1},{4,6},{5,7},{6,4},{7,5},{8,10},{9,11},{10,... | collective-permute-start | bytes 737288 | tf_op jit(solution)/shard_map/ppermute | solution.py:545
  382.8 49.0 %collective-permute-start.37 = (bf16[320,384]{1,0:T(8,128)(2,1)S(1)}, bf16[320,384]{1,0:T(8,128)(2,1)S(1)}, u32[]{:S(2)}, u32[]{:S(2)}) collective-permute-start(bf16[320,384]{1,0:T(8,128)(2,1)S(1)} %copy-done.71), channel_id=1, source_target_pairs={{0,3},{1,2},{2,1},{3,0},{4,7},{5,6},{6,5},{7,4},{8,11},{9,10},{10,... | collective-permute-start | bytes 737288 | tf_op jit(solution)/shard_map/ppermute | solution.py:545
  393.9 32.2 %collective-permute-start.61 = (bf16[320,512]{1,0:T(8,128)(2,1)S(1)}, bf16[320,512]{1,0:T(8,128)(2,1)S(1)}, u32[]{:S(2)}, u32[]{:S(2)}) collective-permute-start(bf16[320,512]{1,0:T(8,128)(2,1)S(1)} %multiply_convert_fusion.refs_0_), channel_id=1, source_target_pairs={{0,2},{1,3},{2,0},{3,1},{4,6},{5,7},{6,4},{7,5},{8,10},{9,11},{10,... | collective-permute-start | bytes 983048 | tf_op jit(solution)/shard_map/ppermute | solution.py:545
  394.2 31.9 %collective-permute-start.62 = (bf16[320,512]{1,0:T(8,128)(2,1)S(1)}, bf16[320,512]{1,0:T(8,128)(2,1)S(1)}, u32[]{:S(2)}, u32[]{:S(2)}) collective-permute-start(bf16[320,512]{1,0:T(8,128)(2,1)S(1)} %multiply_convert_fusion.refs_0_), channel_id=1, source_target_pairs={{0,3},{1,2},{2,1},{3,0},{4,7},{5,6},{6,5},{7,4},{8,11},{9,10},{10,... | collective-permute-start | bytes 983048 | tf_op jit(solution)/shard_map/ppermute | solution.py:545
  431.8 41.1 %collective-permute-start.65 = (bf16[1280,512]{1,0:T(8,128)(2,1)}, bf16[1280,512]{1,0:T(8,128)(2,1)S(1)}, u32[]{:S(2)}, u32[]{:S(2)}) collective-permute-start(bf16[1280,512]{1,0:T(8,128)(2,1)} %get-tuple-element.233.refs_5_), channel_id=1, source_target_pairs={{0,16},{16,0},{1,17},{17,1},{2,18},{18,2},{3,19},{19,3},{4,20},{20... | collective-permute-start | bytes 3932168 | tf_op jit(solution)/shard_map/ppermute | solution.py:530
  432.3 17.3 %collective-permute-start.38 = (bf16[320,384]{1,0:T(8,128)(2,1)S(1)}, bf16[320,384]{1,0:T(8,128)(2,1)S(1)}, u32[]{:S(2)}, u32[]{:S(2)}) collective-permute-start(bf16[320,384]{1,0:T(8,128)(2,1)S(1)} %multiply_convert_fusion.4.refs_0_), channel_id=1, source_target_pairs={{0,1},{1,0},{2,3},{3,2},{4,5},{5,4},{6,7},{7,6},{8,9},{9,8},{10,11... | collective-permute-start | bytes 737288 | tf_op jit(solution)/shard_map/ppermute | solution.py:545
  438.5 20.3 %collective-permute-start.39 = (bf16[320,384]{1,0:T(8,128)(2,1)S(1)}, bf16[320,384]{1,0:T(8,128)(2,1)S(1)}, u32[]{:S(2)}, u32[]{:S(2)}) collective-permute-start(bf16[320,384]{1,0:T(8,128)(2,1)S(1)} %multiply_convert_fusion.4.refs_0_), channel_id=1, source_target_pairs={{0,2},{1,3},{2,0},{3,1},{4,6},{5,7},{6,4},{7,5},{8,10},{9,11},{10,... | collective-permute-start | bytes 737288 | tf_op jit(solution)/shard_map/ppermute | solution.py:545
  439.0 19.8 %collective-permute-start.40 = (bf16[320,384]{1,0:T(8,128)(2,1)S(1)}, bf16[320,384]{1,0:T(8,128)(2,1)S(1)}, u32[]{:S(2)}, u32[]{:S(2)}) collective-permute-start(bf16[320,384]{1,0:T(8,128)(2,1)S(1)} %multiply_convert_fusion.4.refs_0_), channel_id=1, source_target_pairs={{0,3},{1,2},{2,1},{3,0},{4,7},{5,6},{6,5},{7,4},{8,11},{9,10},{10,... | collective-permute-start | bytes 737288 | tf_op jit(solution)/shard_map/ppermute | solution.py:545
  464.9 17.9 %collective-permute-start.42 = (bf16[160,384]{1,0:T(8,128)(2,1)}, bf16[160,384]{1,0:T(8,128)(2,1)S(1)}, u32[]{:S(2)}, u32[]{:S(2)}) collective-permute-start(bf16[160,384]{1,0:T(8,128)(2,1)} %get-tuple-element.200), channel_id=1, source_target_pairs={{0,8},{4,12},{8,0},{12,4},{1,9},{5,13},{9,1},{13,5},{2,10},{6,14},... | collective-permute-start | bytes 368648 | tf_op jit(solution)/shard_map/ppermute | solution.py:545
  466.5 16.4 %collective-permute-start.43 = (bf16[160,384]{1,0:T(8,128)(2,1)}, bf16[160,384]{1,0:T(8,128)(2,1)S(1)}, u32[]{:S(2)}, u32[]{:S(2)}) collective-permute-start(bf16[160,384]{1,0:T(8,128)(2,1)} %get-tuple-element.201), channel_id=1, source_target_pairs={{0,12},{4,8},{8,4},{12,0},{1,13},{5,9},{9,5},{13,1},{2,14},{6,10},... | collective-permute-start | bytes 368648 | tf_op jit(solution)/shard_map/ppermute | solution.py:545
  470.8 12.0 %collective-permute-start.66 = (bf16[160,512]{1,0:T(8,128)(2,1)S(1)}, bf16[160,512]{1,0:T(8,128)(2,1)S(1)}, u32[]{:S(2)}, u32[]{:S(2)}) collective-permute-start(bf16[160,512]{1,0:T(8,128)(2,1)S(1)} %copy-done.85), channel_id=1, source_target_pairs={{0,4},{4,0},{8,12},{12,8},{1,5},{5,1},{9,13},{13,9},{2,6},{6,2},{1... | collective-permute-start | bytes 491528 | tf_op jit(solution)/shard_map/ppermute | solution.py:545
  471.1 11.8 %collective-permute-start.67 = (bf16[160,512]{1,0:T(8,128)(2,1)S(1)}, bf16[160,512]{1,0:T(8,128)(2,1)S(1)}, u32[]{:S(2)}, u32[]{:S(2)}) collective-permute-start(bf16[160,512]{1,0:T(8,128)(2,1)S(1)} %copy-done.84), channel_id=1, source_target_pairs={{0,8},{4,12},{8,0},{12,4},{1,9},{5,13},{9,1},{13,5},{2,10},{6,14},... | collective-permute-start | bytes 491528 | tf_op jit(solution)/shard_map/ppermute | solution.py:545
  473.0 9.9 %collective-permute-start.68 = (bf16[160,512]{1,0:T(8,128)(2,1)S(1)}, bf16[160,512]{1,0:T(8,128)(2,1)S(1)}, u32[]{:S(2)}, u32[]{:S(2)}) collective-permute-start(bf16[160,512]{1,0:T(8,128)(2,1)S(1)} %copy-done.83), channel_id=1, source_target_pairs={{0,12},{4,8},{8,4},{12,0},{1,13},{5,9},{9,5},{13,1},{2,14},{6,10},... | collective-permute-start | bytes 491528 | tf_op jit(solution)/shard_map/ppermute | solution.py:545
  496.9 22.0 %collective-permute-start.72 = (bf16[4,160,784]{2,1,0:T(8,128)(2,1)S(1)}, bf16[4,160,784]{2,1,0:T(8,128)(2,1)S(1)}, u32[]{:S(2)}, u32[]{:S(2)}) collective-permute-start(bf16[4,160,784]{2,1,0:T(8,128)(2,1)S(1)} %bitcast.25), channel_id=1, source_target_pairs={{0,16},{16,0},{1,17},{17,1},{2,18},{18,2},{3,19},{19,3},{4,20},{20... | collective-permute-start | bytes 3010568 | tf_op jit(solution)/shard_map/ppermute | solution.py:530
  512.2 33.4 %collective-permute-start.69 = (bf16[160,784]{1,0:T(8,128)(2,1)}, bf16[160,784]{1,0:T(8,128)(2,1)S(1)}, u32[]{:S(2)}, u32[]{:S(2)}) collective-permute-start(bf16[160,784]{1,0:T(8,128)(2,1)} %get-tuple-element.247), channel_id=1, source_target_pairs={{0,1},{1,0},{2,3},{3,2},{4,5},{5,4},{6,7},{7,6},{8,9},{9,8},{10,11... | collective-permute-start | bytes 752648 | tf_op jit(solution)/shard_map/ppermute | solution.py:545
  516.5 29.1 %collective-permute-start.70 = (bf16[160,784]{1,0:T(8,128)(2,1)}, bf16[160,784]{1,0:T(8,128)(2,1)S(1)}, u32[]{:S(2)}, u32[]{:S(2)}) collective-permute-start(bf16[160,784]{1,0:T(8,128)(2,1)} %get-tuple-element.248), channel_id=1, source_target_pairs={{0,2},{1,3},{2,0},{3,1},{4,6},{5,7},{6,4},{7,5},{8,10},{9,11},{10,... | collective-permute-start | bytes 752648 | tf_op jit(solution)/shard_map/ppermute | solution.py:545
  517.0 28.6 %collective-permute-start.71 = (bf16[160,784]{1,0:T(8,128)(2,1)}, bf16[160,784]{1,0:T(8,128)(2,1)S(1)}, u32[]{:S(2)}, u32[]{:S(2)}) collective-permute-start(bf16[160,784]{1,0:T(8,128)(2,1)} %get-tuple-element.249), channel_id=1, source_target_pairs={{0,3},{1,2},{2,1},{3,0},{4,7},{5,6},{6,5},{7,4},{8,11},{9,10},{10,... | collective-permute-start | bytes 752648 | tf_op jit(solution)/shard_map/ppermute | solution.py:545
  (95 other events, 1440.7 us)
